TPU v7x, 32 devices: a whole 2x2x4 slice. The times are simulated.
32 devices in a mesh: fsdp: 8 (over y, x, core), tp: 4 (over z).
Axes of the slice: x: 2, y: 2, z: 4, core: 2. Of those that a mesh axis runs over, the one named last changes fastest.
Arguments:
- tokens: bfloat16 [8192, 2048], P(('fsdp', 'tp')), may hold values from -6 to 6
- norm1_gain: float32 [2048], replicated, may hold values from 0.25 to 1.75
- norm1_shift: float32 [2048], replicated, may hold values from -1 to 1
- w_query: bfloat16 [2048, 2048], P('fsdp', 'tp'), may hold values from -0.125 to 0.125
- b_query: float32 [2048], P('tp'), may hold values from -1 to 1
- w_key: bfloat16 [2048, 2048], P('fsdp', 'tp'), may hold values from -0.125 to 0.125
- w_value: bfloat16 [2048, 2048], P('fsdp', 'tp'), may hold values from -0.125 to 0.125
- b_value: float32 [2048], P('tp'), may hold values from -1 to 1
- w_out: bfloat16 [2048, 2048], P('fsdp', 'tp'), may hold values from -0.5 to 0.5
- b_out: float32 [2048], replicated, may hold values from -1 to 1
- norm2_gain: float32 [2048], replicated, may hold values from 0.25 to 1.75
- norm2_shift: float32 [2048], replicated, may hold values from -1 to 1
- w_up: bfloat16 [2048, 8192], P('fsdp', 'tp'), may hold values from -0.125 to 0.125
- b_up: float32 [8192], P('tp'), may hold values from -1 to 1
- w_down: bfloat16 [2048, 8192], P('fsdp', 'tp'), may hold values from -0.09375 to 0.09375
- b_down: float32 [2048], replicated, may hold values from -1 to 1
- teacher: bfloat16 [8192, 2048], P(('fsdp', 'tp')), may hold values from -6 to 6
- valid_mask: int32 [8192], P(('fsdp', 'tp')), may hold values from 0 to 1, as said below
- parents: int32 [8, 8], P('fsdp'), may hold values from -1 to 6, as said below
- summary: int32 [8, 8, 12], P('fsdp'), may hold values from 0 to 127, as said below
Outputs:
- output_states: bfloat16 [8192, 2048], P(('fsdp', 'tp'))
- mean_loss: float32 [], replicated
- grad_tokens: float32 [8192, 2048], P(('fsdp', 'tp'))
- grad_norm1_gain: float32 [2048], replicated
- grad_norm1_shift: float32 [2048], replicated
- grad_w_query: float32 [2048, 2048], P('fsdp', 'tp')
- grad_b_query: float32 [2048], P('tp')
- grad_w_key: float32 [2048, 2048], P('fsdp', 'tp')
- grad_w_value: float32 [2048, 2048], P('fsdp', 'tp')
- grad_b_value: float32 [2048], P('tp')
- grad_w_out: float32 [2048, 2048], P('fsdp', 'tp')
- grad_b_out: float32 [2048], replicated
- grad_norm2_gain: float32 [2048], replicated
- grad_norm2_shift: float32 [2048], replicated
- grad_w_up: float32 [2048, 8192], P('fsdp', 'tp')
- grad_b_up: float32 [8192], P('tp')
- grad_w_down: float32 [2048, 8192], P('fsdp', 'tp')
- grad_b_down: float32 [2048], replicated
Inputs may be any that keep to these rules, and one draw needn't show every extreme that they name: valid_mask is 1 at the first token of every tree. parents[f, 0] is -1 and 0 <= parents[f, s] < s for every later segment s; the last segment of every tree has the segment before it as parent. `summary`: the 12 offsets of one segment are distinct.
All inputs are finite; a program needn't handle non-finite values.
Results may differ from a plain program's by a relative error of at most 0.019.
Values may be sent and summed in bfloat16 or wider, within the bound.
No kernel may reach another device: no remote copies, remote signals or barrier semaphores. Data moves between devices by JAX's collectives and lax.ppermute only.
A program may use at most 192 MiB of HBM per device.

v0:
```python
import jax
import jax.numpy as jnp
from jax import lax
from jax.sharding import PartitionSpec as P

HD = 64


EPSILON = 1e-05
MASKED_SCORE = -1e30


def layer_norm(vectors, norm_gain, norm_shift):
    centre = jnp.mean(vectors, axis=-1, keepdims=True)
    centred = vectors - centre
    spread = jnp.mean(centred * centred, axis=-1, keepdims=True)
    return centred * lax.rsqrt(spread + EPSILON) * norm_gain + norm_shift


def ancestors(parent_row):
    segments = parent_row.shape[0]
    columns = jnp.arange(segments, dtype=jnp.int32)

    def follow(sweep, state_pair):
        ancestry, current = state_pair
        matches = current[:, None] == columns[None, :]
        ancestry = jnp.maximum(ancestry, matches.astype(jnp.float32))
        following = jnp.sum(jnp.where(matches, parent_row[None, :], 0), axis=1)
        current = jnp.where(current >= 0, following, -1)
        return (ancestry, current)

    start_table = jnp.zeros((segments, segments), jnp.float32)
    ancestry, finished = lax.fori_loop(0, segments, follow, (start_table, parent_row))
    return ancestry


def tree_tables(parent_row, summary_rows, length):
    segments = parent_row.shape[0]
    seg_length = length // segments
    ancestry = ancestors(parent_row)
    offsets = jnp.arange(seg_length, dtype=jnp.int32)
    marked = jnp.max(
        (summary_rows[:, :, None] == offsets[None, None, :]).astype(jnp.float32), axis=1
    ).reshape(length)
    key_segment = jnp.arange(length, dtype=jnp.int32) // seg_length
    key_onehot = (key_segment[:, None] == jnp.arange(segments, dtype=jnp.int32)[None, :]).astype(
        jnp.float32
    )
    return (ancestry, marked, key_segment, key_onehot, seg_length)


def block_mask(tables, start_row, block_rows):
    ancestry, marked, key_segment, key_onehot, seg_length = tables
    query_position = start_row + jnp.arange(block_rows, dtype=jnp.int32)
    query_segment = query_position // seg_length
    query_onehot = (
        query_segment[:, None] == jnp.arange(ancestry.shape[0], dtype=jnp.int32)[None, :]
    ).astype(jnp.float32)
    reached = jnp.dot(jnp.dot(query_onehot, ancestry, precision=None), key_onehot.T, precision=None)
    key_position = jnp.arange(marked.shape[0], dtype=jnp.int32)
    same_segment = (query_segment[:, None] == key_segment[None, :]) & (
        key_position[None, :] <= query_position[:, None]
    )
    return same_segment | (reached > 0.5) & (marked[None, :] > 0.5)


def contract(left_side, right_side, left_dim, right_dim):
    return lax.dot_general(
        left_side,
        right_side,
        (((left_dim,), (right_dim,)), ((), ())),
        preferred_element_type=jnp.float32,
    )


def attend_forward(queries, key_states, value_states, tables):
    length = queries.shape[0]
    head_count = queries.shape[1] // HD
    block_rows = min(512, length)
    query_heads = queries.reshape(length, head_count, HD)
    key_heads = key_states.reshape(length, head_count, HD)
    value_heads = value_states.reshape(length, head_count, HD)

    def one_block(start_row):
        query_block = lax.dynamic_slice_in_dim(query_heads, start_row, block_rows, 0)
        scores = jnp.einsum(
            "qhd,khd->hqk", query_block, key_heads, preferred_element_type=jnp.float32
        )
        allowed = block_mask(tables, start_row, block_rows)
        scores = jnp.where(allowed[None], scores, MASKED_SCORE)
        highest = jnp.max(scores, axis=-1, keepdims=True)
        exp_scores = jnp.exp(scores - highest)
        totals = jnp.sum(exp_scores, axis=-1, keepdims=True)
        shares = (exp_scores / totals).astype(jnp.bfloat16)
        attended = jnp.einsum(
            "hqk,khd->qhd", shares, value_heads, preferred_element_type=jnp.float32
        )
        return (attended.astype(jnp.bfloat16), (highest + jnp.log(totals))[..., 0])

    starts = jnp.arange(length // block_rows, dtype=jnp.int32) * block_rows
    attended, log_totals = lax.map(one_block, starts)
    return (attended.reshape(length, head_count * HD), log_totals)


def attend_backward(queries, key_states, value_states, grad_attended, log_totals, tables):
    length = queries.shape[0]
    head_count = queries.shape[1] // HD
    block_rows = min(512, length)
    query_heads = queries.reshape(length, head_count, HD)
    key_heads = key_states.reshape(length, head_count, HD)
    value_heads = value_states.reshape(length, head_count, HD)
    grad_heads = grad_attended.reshape(length, head_count, HD)

    def one_block(summed, members):
        start_row, log_block = members
        key_sum, value_sum = summed
        query_block = lax.dynamic_slice_in_dim(query_heads, start_row, block_rows, 0)
        grad_block = lax.dynamic_slice_in_dim(grad_heads, start_row, block_rows, 0)
        scores = jnp.einsum(
            "qhd,khd->hqk", query_block, key_heads, preferred_element_type=jnp.float32
        )
        allowed = block_mask(tables, start_row, block_rows)
        probs = jnp.where(allowed[None], jnp.exp(scores - log_block[..., None]), 0.0)
        grad_probs = jnp.einsum(
            "qhd,khd->hqk", grad_block, value_heads, preferred_element_type=jnp.float32
        )
        inner_sum = jnp.sum(probs * grad_probs, axis=-1, keepdims=True)
        grad_scores = (probs * (grad_probs - inner_sum)).astype(jnp.bfloat16)
        grad_query = jnp.einsum(
            "hqk,khd->qhd", grad_scores, key_heads, preferred_element_type=jnp.float32
        ).astype(jnp.bfloat16)
        key_sum = key_sum + jnp.einsum(
            "hqk,qhd->khd", grad_scores, query_block, preferred_element_type=jnp.float32
        )
        value_sum = value_sum + jnp.einsum(
            "hqk,qhd->khd",
            probs.astype(jnp.bfloat16),
            grad_block,
            preferred_element_type=jnp.float32,
        )
        return ((key_sum, value_sum), grad_query)

    starts = jnp.arange(length // block_rows, dtype=jnp.int32) * block_rows
    zero_heads = jnp.zeros((length, head_count, HD), jnp.float32)
    (key_sum, value_sum), grad_queries = lax.scan(
        one_block, (zero_heads, zero_heads), (starts, log_totals)
    )
    width = head_count * HD
    return (
        grad_queries.reshape(length, width),
        key_sum.reshape(length, width).astype(jnp.bfloat16),
        value_sum.reshape(length, width).astype(jnp.bfloat16),
    )


def body(
    tokens,
    norm1_gain,
    norm1_shift,
    w_query,
    b_query,
    w_key,
    w_value,
    b_value,
    w_out,
    b_out,
    norm2_gain,
    norm2_shift,
    w_up,
    b_up,
    w_down,
    b_down,
    teacher,
    valid_mask,
    parents,
    summary,
):

    def attention_weights():
        return (
            lax.all_gather(w_query, "fsdp", axis=0, tiled=True),
            lax.all_gather(w_key, "fsdp", axis=0, tiled=True),
            lax.all_gather(w_value, "fsdp", axis=0, tiled=True),
            lax.all_gather(w_out, "fsdp", axis=0, tiled=True),
        )

    def feed_weights():
        return (
            lax.all_gather(w_up, "fsdp", axis=0, tiled=True),
            lax.all_gather(w_down, "fsdp", axis=0, tiled=True),
        )

    inputs = tokens.astype(jnp.float32)
    normed = layer_norm(inputs, norm1_gain, norm1_shift).astype(jnp.bfloat16)
    normed_all = lax.all_gather(normed, "tp", axis=0, tiled=True)
    full_query, full_key, full_value, full_out = attention_weights()
    queries = (
        (jnp.dot(normed_all, full_query, preferred_element_type=jnp.float32) + b_query) * 0.125
    ).astype(jnp.bfloat16)
    key_states = jnp.dot(normed_all, full_key, preferred_element_type=jnp.float32).astype(
        jnp.bfloat16
    )
    value_states = (
        jnp.dot(normed_all, full_value, preferred_element_type=jnp.float32) + b_value
    ).astype(jnp.bfloat16)
    tables = tree_tables(parents[0], summary[0], normed_all.shape[0])
    attended, log_totals = attend_forward(queries, key_states, value_states, tables)
    branch = lax.psum_scatter(
        contract(attended, full_out, 1, 1), "tp", scatter_dimension=0, tiled=True
    )
    hidden = inputs + branch + b_out
    normed_mid = layer_norm(hidden, norm2_gain, norm2_shift).astype(jnp.bfloat16)
    normed_mid_all = lax.all_gather(normed_mid, "tp", axis=0, tiled=True)
    full_up, full_down = feed_weights()
    active = jnp.maximum(
        jnp.dot(normed_mid_all, full_up, preferred_element_type=jnp.float32) + b_up, 0.0
    ).astype(jnp.bfloat16)
    feed_out = lax.psum_scatter(
        contract(active, full_down, 1, 1), "tp", scatter_dimension=0, tiled=True
    )
    output = hidden + feed_out + b_down
    weight_mask = valid_mask.astype(jnp.float32)
    deviation = output - teacher.astype(jnp.float32)
    valid_count, squares = lax.psum(
        (jnp.sum(weight_mask), jnp.sum(weight_mask[:, None] * deviation * deviation)),
        ("fsdp", "tp"),
    )
    mean_loss = squares / (valid_count * tokens.shape[1])
    total_tokens = tokens.shape[0] * lax.axis_size("fsdp") * lax.axis_size("tp")
    grad_output = 2.0 * total_tokens / valid_count * weight_mask[:, None] * deviation
    grad_feed_all = lax.all_gather(grad_output.astype(jnp.bfloat16), "tp", axis=0, tiled=True)
    full_up, full_down = feed_weights()
    grad_w_down = contract(grad_feed_all, active, 0, 0)
    grad_pre = jnp.where(
        active > 0, jnp.dot(grad_feed_all, full_down, preferred_element_type=jnp.float32), 0.0
    ).astype(jnp.bfloat16)
    grad_w_up = contract(normed_mid_all, grad_pre, 0, 0)
    grad_w_up, grad_w_down = (
        lax.psum_scatter(
            grad_w_up.astype(jnp.bfloat16), "fsdp", scatter_dimension=0, tiled=True
        ).astype(jnp.float32),
        lax.psum_scatter(
            grad_w_down.astype(jnp.bfloat16), "fsdp", scatter_dimension=0, tiled=True
        ).astype(jnp.float32),
    )
    grad_mid = lax.psum_scatter(
        contract(grad_pre, full_up, 1, 1), "tp", scatter_dimension=0, tiled=True
    )
    second_norm, second_pull = jax.vjp(layer_norm, hidden, norm2_gain, norm2_shift)
    grad_hidden_norm, grad_norm2_gain, grad_norm2_shift = second_pull(grad_mid)
    grad_hidden = grad_output + grad_hidden_norm
    grad_branch_all = lax.all_gather(grad_hidden.astype(jnp.bfloat16), "tp", axis=0, tiled=True)
    full_query, full_key, full_value, full_out = attention_weights()
    grad_w_out = contract(grad_branch_all, attended, 0, 0)
    grad_attended = jnp.dot(grad_branch_all, full_out, preferred_element_type=jnp.float32).astype(
        jnp.bfloat16
    )
    grad_queries, grad_keys, grad_values = attend_backward(
        queries, key_states, value_states, grad_attended, log_totals, tables
    )
    grad_pre_query = grad_queries * jnp.bfloat16(0.125)
    grad_w_query = contract(normed_all, grad_pre_query, 0, 0)
    grad_w_key = contract(normed_all, grad_keys, 0, 0)
    grad_w_value = contract(normed_all, grad_values, 0, 0)
    grad_w_query, grad_w_key, grad_w_value, grad_w_out = (
        lax.psum_scatter(grad_w_query, "fsdp", scatter_dimension=0, tiled=True),
        lax.psum_scatter(grad_w_key, "fsdp", scatter_dimension=0, tiled=True),
        lax.psum_scatter(grad_w_value, "fsdp", scatter_dimension=0, tiled=True),
        lax.psum_scatter(grad_w_out, "fsdp", scatter_dimension=0, tiled=True),
    )
    grad_normed = (
        contract(grad_pre_query, full_query, 1, 1)
        + contract(grad_keys, full_key, 1, 1)
        + contract(grad_values, full_value, 1, 1)
    )
    grad_normed = lax.psum_scatter(grad_normed, "tp", scatter_dimension=0, tiled=True)
    first_norm, first_pull = jax.vjp(layer_norm, inputs, norm1_gain, norm1_shift)
    grad_input_norm, grad_norm1_gain, grad_norm1_shift = first_pull(grad_normed)
    grad_tokens = grad_hidden + grad_input_norm
    column = lax.axis_index("tp")
    tp_count = lax.axis_size("tp")

    def widen(share_part):
        widened = jnp.zeros((share_part.shape[0] * tp_count,), jnp.float32)
        return lax.dynamic_update_slice_in_dim(widened, share_part, column * share_part.shape[0], 0)

    def narrow(widened, span_width):
        return lax.dynamic_slice_in_dim(widened, column * span_width, span_width, 0)

    summed = lax.psum(
        (
            grad_norm1_gain,
            grad_norm1_shift,
            widen(jnp.sum(grad_pre_query.astype(jnp.float32), axis=0)),
            widen(jnp.sum(grad_values.astype(jnp.float32), axis=0)),
            jnp.sum(grad_hidden, axis=0),
            grad_norm2_gain,
            grad_norm2_shift,
            widen(jnp.sum(grad_pre.astype(jnp.float32), axis=0)),
            jnp.sum(grad_output, axis=0),
        ),
        ("fsdp", "tp"),
    )
    return (
        output.astype(jnp.bfloat16),
        mean_loss,
        grad_tokens,
        summed[0],
        summed[1],
        grad_w_query,
        narrow(summed[2], b_query.shape[0]),
        grad_w_key,
        grad_w_value,
        narrow(summed[3], b_value.shape[0]),
        grad_w_out,
        summed[4],
        summed[5],
        summed[6],
        grad_w_up,
        narrow(summed[7], b_up.shape[0]),
        grad_w_down,
        summed[8],
    )


def solution(mesh):
    placed = (
        P(("fsdp", "tp"), None),
        P(),
        P(),
        P("fsdp", "tp"),
        P("tp"),
        P("fsdp", "tp"),
        P("fsdp", "tp"),
        P("tp"),
        P("fsdp", "tp"),
        P(),
        P(),
        P(),
        P("fsdp", "tp"),
        P("tp"),
        P("fsdp", "tp"),
        P(),
        P(("fsdp", "tp"), None),
        P(("fsdp", "tp")),
        P("fsdp", None),
        P("fsdp", None, None),
    )
    return jax.shard_map(
        body,
        mesh=mesh,
        in_specs=placed,
        out_specs=(
            P(("fsdp", "tp"), None),
            P(),
            P(("fsdp", "tp"), None),
            P(),
            P(),
            P("fsdp", "tp"),
            P("tp"),
            P("fsdp", "tp"),
            P("fsdp", "tp"),
            P("tp"),
            P("fsdp", "tp"),
            P(),
            P(),
            P(),
            P("fsdp", "tp"),
            P("tp"),
            P("fsdp", "tp"),
            P(),
        ),
        check_vma=False,
    )
```

profile of v0, /device:TPU:0, one launch (start us, length us, event | category | flops | bytes accessed | tf_op | source)
XLA Modules:
  0.0 1605.4 jit_solution(4273150163818574457)
XLA Ops:
  18.1 22.4 %all-gather.15.cloned.1.call-done = bf16[2048,512]{1,0:T(8,128)(2,1)} async-done(((bf16[256,512]{1,0:T(8,128)(2,1)}), bf16[2048,512]{1,0:T(8,128)(2,1)}) %all-gather.15.cloned.1.call-update) | async-done | bytes 2097168 | tf_op jit(solution)/shard_map/all_gather | solution.py:182
  40.6 82.9 %all-gather.11.cloned.1.call-done = bf16[1024,2048]{1,0:T(8,128)(2,1)} async-done(((bf16[256,2048]{1,0:T(8,128)(2,1)}), bf16[1024,2048]{1,0:T(8,128)(2,1)}) %all-gather.11.cloned.1.call-update) | async-done | bytes 4194320 | tf_op jit(solution)/shard_map/all_gather | solution.py:195
  128.7 22.9 %all-gather.17.cloned.1.call-done = bf16[2048,512]{1,0:T(8,128)(2,1)} async-done(((bf16[256,512]{1,0:T(8,128)(2,1)}), bf16[2048,512]{1,0:T(8,128)(2,1)}) %all-gather.17.cloned.1.call-update) | async-done | bytes 2097168 | tf_op jit(solution)/shard_map/all_gather | solution.py:183
  157.9 23.3 %all-gather.13.cloned.1.call-done = bf16[2048,512]{1,0:T(8,128)(2,1)} async-done(((bf16[256,512]{1,0:T(8,128)(2,1)}), bf16[2048,512]{1,0:T(8,128)(2,1)}) %all-gather.13.cloned.1.call-update) | async-done | bytes 2097168 | tf_op jit(solution)/shard_map/all_gather | solution.py:181
  187.5 34.7 %while.45 = (s32[]{:T(128)}, bf16[2,512,8,64]{1,3,2,0:T(8,128)(2,1)}, f32[2,8,512]{2,1,0:T(8,128)S(1)}, s32[2]{0:T(128)S(1)}, bf16[8,8]{1,0:T(8,128)(2,1)S(1)}, ...) while((s32[]{:T(128)}, ...), condition=%wide.region_9.10_spmd.clone, body=%wide.region_6.9_spmd.clone.sunk | while | flops 1123386368 | bytes 68315536 | solution.py:101
  225.2 7.6 fusion.97
  233.6 143.9 %reduce-scatter.11.cloned.1.call-done = f32[256,2048]{1,0:T(8,128)} async-done(((f32[1024,2048]{1,0:T(8,128)}), f32[256,2048]{1,0:T(8,128)}) %reduce-scatter.11.cloned.1.call-update) | async-done | bytes 2097168 | tf_op jit(solution)/shard_map/reduce_scatter | solution.py:208
  382.7 51.6 %all-gather.23.cloned.1.call-done = bf16[2048,2048]{1,0:T(8,128)(2,1)} async-done(((bf16[256,2048]{1,0:T(8,128)(2,1)}), bf16[2048,2048]{1,0:T(8,128)(2,1)}) %all-gather.23.cloned.1.call-update) | async-done | bytes 8388624 | tf_op jit(solution)/shard_map/all_gather | solution.py:189
  434.3 82.9 %all-gather.21.cloned.1.call-done = bf16[1024,2048]{1,0:T(8,128)(2,1)} async-done(((bf16[256,2048]{1,0:T(8,128)(2,1)}), bf16[1024,2048]{1,0:T(8,128)(2,1)}) %all-gather.21.cloned.1.call-update) | async-done | bytes 4194320 | tf_op jit(solution)/shard_map/all_gather | solution.py:213
  517.2 14.0 maximum_convert_fusion
  531.2 40.7 %all-gather.25.cloned.1.call-done = bf16[2048,2048]{1,0:T(8,128)(2,1)} async-done(((bf16[256,2048]{1,0:T(8,128)(2,1)}), bf16[2048,2048]{1,0:T(8,128)(2,1)}) %all-gather.25.cloned.1.call-update) | async-done | bytes 8388624 | tf_op jit(solution)/shard_map/all_gather | solution.py:190
  571.9 14.6 fusion.98
  587.8 44.5 %psum.78 = f32[]{:T(128)} all-reduce(f32[]{:T(128)} %convert_reduce_fusion.5), channel_id=1, replica_groups=mesh['fsdp'=8,'tp'=4] {'fsdp','tp'}, use_global_device_ids=true, to_apply=%region_17.18 | all-reduce | flops 1 | bytes 8 | tf_op jit(solution)/shard_map/psum | solution.py:224
  633.0 99.3 %reduce-scatter.13.cloned.1.call-done = f32[256,2048]{1,0:T(8,128)} async-done(((f32[1024,2048]{1,0:T(8,128)}), f32[256,2048]{1,0:T(8,128)}) %reduce-scatter.13.cloned.1.call-update) | async-done | bytes 2097168 | tf_op jit(solution)/shard_map/reduce_scatter | solution.py:218
  736.9 81.4 %all-gather.27.cloned.1.call-done = bf16[1024,2048]{1,0:T(8,128)(2,1)} async-done(((bf16[256,2048]{1,0:T(8,128)(2,1)}), bf16[1024,2048]{1,0:T(8,128)(2,1)}) %all-gather.27.cloned.1.call-update) | async-done | bytes 4194320 | tf_op jit(solution)/shard_map/all_gather | solution.py:231
  818.4 14.0 convert_reduce_fusion
  834.4 13.3 fusion.99
  847.8 143.2 %reduce-scatter.15.cloned.1.call-done = f32[256,2048]{1,0:T(8,128)} async-done(((f32[1024,2048]{1,0:T(8,128)}), f32[256,2048]{1,0:T(8,128)}) %reduce-scatter.15.cloned.1.call-update) | async-done | bytes 2097168 | tf_op jit(solution)/shard_map/reduce_scatter | solution.py:246
  999.9 14.5 convolution_convert_fusion.2
  1014.4 14.1 convolution_convert_fusion.1
  1028.6 52.8 %all-gather.29.cloned.1.call-done = bf16[1024,2048]{1,0:T(8,128)(2,1)} async-done(((bf16[256,2048]{1,0:T(8,128)(2,1)}), bf16[1024,2048]{1,0:T(8,128)(2,1)}) %all-gather.29.cloned.1.call-update) | async-done | bytes 4194320 | tf_op jit(solution)/shard_map/all_gather | solution.py:252
  1088.6 104.4 %while.47 = (s32[]{:T(128)}, f32[1024,8,64]{0,2,1:T(8,128)S(1)}, f32[1024,8,64]{0,2,1:T(8,128)}, bf16[2,512,8,64]{1,3,2,0:T(8,128)(2,1)}, s32[2]{0:T(128)S(1)}, ...) while((s32[]{:T(128)}, f32[1024,8,64]{0,2,1:T(8,128)S(1)}, ...), condition=%wide.region_23.24_spmd.clone, body=%wide.region_21.23_spmd.clone.sunk | while | flops 2748679168 | bytes 224012784 | solution.py:145
  1109.5 12.6 multiply_reduce_fusion.6
  1122.1 12.6 multiply_convert_fusion.4
  1160.0 15.1 multiply_reduce_fusion.6
  1175.2 12.8 multiply_convert_fusion.4
  1216.4 6.6 fusion.104
  1245.0 131.4 %reduce-scatter.17.cloned.1.call-done = f32[256,2048]{1,0:T(8,128)} async-done(((f32[1024,2048]{1,0:T(8,128)}), f32[256,2048]{1,0:T(8,128)}) %reduce-scatter.17.cloned.1.call-update) | async-done | bytes 2097168 | tf_op jit(solution)/shard_map/reduce_scatter | solution.py:276
  1379.8 43.2 %all-reduce.2 = (f32[]{:T(128)}, f32[2048]{0:T(1024)}, f32[2048]{0:T(1024)}, f32[2048]{0:T(1024)S(1)}, f32[2048]{0:T(1024)S(1)}, /*index=5*/f32[2048]{0:T(1024)}...) all-reduce(f32[]{:T(128)} %get-tuple-element.546, ...), channel_id=1, replica_groups=mesh['fsdp'=8,'tp'=4] {'fsdp','tp'}, use_global_device_ids=true, to_apply=%region_15.16 | all-reduce | flops 24577 | bytes 196616 | tf_op jit(solution)/shard_map/psum | solution.py:224
  1432.2 55.0 %reduce-scatter.23.cloned.1.call-done = f32[256,512]{1,0:T(8,128)} async-done(((f32[2048,512]{1,0:T(8,128)}), f32[256,512]{1,0:T(8,128)}) %reduce-scatter.23.cloned.1.call-update) | async-done | bytes 524304 | tf_op jit(solution)/shard_map/reduce_scatter | solution.py:268
  1487.1 55.1 %reduce-scatter.21.cloned.1.call-done = f32[256,512]{1,0:T(8,128)} async-done(((f32[2048,512]{1,0:T(8,128)}), f32[256,512]{1,0:T(8,128)}) %reduce-scatter.21.cloned.1.call-update) | async-done | bytes 524304 | tf_op jit(solution)/shard_map/reduce_scatter | solution.py:267
  1542.3 55.0 %reduce-scatter.19.cloned.1.call-done = f32[256,512]{1,0:T(8,128)} async-done(((f32[2048,512]{1,0:T(8,128)}), f32[256,512]{1,0:T(8,128)}) %reduce-scatter.19.cloned.1.call-update) | async-done | bytes 524304 | tf_op jit(solution)/shard_map/reduce_scatter | solution.py:266
  (292 shorter events, 196.8 us)
Async XLA Ops:
  7.2 33.3 %all-gather.15.cloned.1.call-start = ((), (), s32[]{:S(2)}) async-start(), calls=%async_computation.12 | async-start | bytes 2359296 | tf_op jit(solution)/shard_map/all_gather | solution.py:182
  8.0 115.5 %all-gather.11.cloned.1.call-start = ((), (), s32[]{:S(2)}) async-start(), calls=%async_computation.10 | async-start | bytes 5242880 | tf_op jit(solution)/shard_map/all_gather | solution.py:195
  13.7 137.9 %all-gather.17.cloned.1.call-start = ((), (), s32[]{:S(2)}) async-start(), calls=%async_computation.13 | async-start | bytes 2359296 | tf_op jit(solution)/shard_map/all_gather | solution.py:183
  14.5 166.8 %all-gather.13.cloned.1.call-start = ((), (), s32[]{:S(2)}) async-start(), calls=%async_computation.11 | async-start | bytes 2359296 | tf_op jit(solution)/shard_map/all_gather | solution.py:181
  15.0 210.1 %all-gather.19.cloned.1.call-start = ((), (), s32[]{:S(2)}) async-start(), calls=%async_computation.14 | async-start | bytes 2359296 | tf_op jit(solution)/shard_map/all_gather | solution.py:184
  15.6 361.9 %reduce-scatter.11.cloned.1.call-start = ((), (), s32[]{:S(2)}) async-start(), calls=%async_computation.15 | async-start | bytes 10485760 | tf_op jit(solution)/shard_map/reduce_scatter | solution.py:208
  18.1 133.5 %copy-start.47 = (f32[512]{0:T(512)S(1)}, f32[512]{0:T(512)}, u32[]{:S(2)}) copy-start(f32[512]{0:T(512)} %param.33) | copy-start | bytes 6148
  128.7 52.5 %copy-start.48 = (f32[512]{0:T(512)S(1)}, f32[512]{0:T(512)}, u32[]{:S(2)}) copy-start(f32[512]{0:T(512)} %param.30) | copy-start | bytes 6148
  232.8 144.8 %copy-start.38 = (f32[2048]{0:T(1024)S(1)}, f32[2048]{0:T(1024)}, u32[]{:S(2)}) copy-start(f32[2048]{0:T(1024)} %param.35) | copy-start | bytes 24580
  232.8 201.5 %all-gather.23.cloned.1.call-start = ((), (), s32[]{:S(2)}) async-start(), calls=%async_computation.17 | async-start | bytes 9437184 | tf_op jit(solution)/shard_map/all_gather | solution.py:189
  233.5 283.7 %all-gather.21.cloned.1.call-start = ((), (), s32[]{:S(2)}) async-start(), calls=%async_computation.16 | async-start | bytes 5242880 | tf_op jit(solution)/shard_map/all_gather | solution.py:213
  380.5 136.8 %copy-start.46 = (f32[2048]{0:T(1024)S(1)}, f32[2048]{0:T(1024)}, u32[]{:S(2)}) copy-start(f32[2048]{0:T(1024)} %param.39) | copy-start | bytes 24580
  381.9 190.0 %all-gather.25.cloned.1.call-start = ((), (), s32[]{:S(2)}) async-start(), calls=%async_computation.18 | async-start | bytes 9437184 | tf_op jit(solution)/shard_map/all_gather | solution.py:190
  382.6 349.7 %reduce-scatter.13.cloned.1.call-start = ((), (), s32[]{:S(2)}) async-start(), calls=%async_computation.19 | async-start | bytes 10485760 | tf_op jit(solution)/shard_map/reduce_scatter | solution.py:218
  586.5 145.8 %copy-start.41 = (f32[2048]{0:T(1024)S(1)}, f32[2048]{0:T(1024)}, u32[]{:S(2)}) copy-start(f32[2048]{0:T(1024)} %param.41) | copy-start | bytes 24580
  586.6 231.8 %all-gather.27.cloned.1.call-start = ((), (), s32[]{:S(2)}) async-start(), calls=%async_computation.20 | async-start | bytes 5242880 | tf_op jit(solution)/shard_map/all_gather | solution.py:231
  736.9 254.1 %reduce-scatter.15.cloned.1.call-start = ((), (), s32[]{:S(2)}) async-start(), calls=%async_computation.21 | async-start | bytes 10485760 | tf_op jit(solution)/shard_map/reduce_scatter | solution.py:246
  847.7 233.6 %all-gather.29.cloned.1.call-start = ((), (), s32[]{:S(2)}) async-start(), calls=%async_computation.22 | async-start | bytes 5242880 | tf_op jit(solution)/shard_map/all_gather | solution.py:252
  999.8 238.5 %reduce-scatter.27.cloned.1.call-start = ((), (), s32[]{:S(2)}) async-start(), calls=%async_computation.28 | async-start | bytes 9437184 | tf_op jit(solution)/shard_map/reduce_scatter | solution.py:239
  1014.3 226.9 %reduce-scatter.29.cloned.1.call-start = ((), (), s32[]{:S(2)}) async-start(), calls=%async_computation.29 | async-start | bytes 9437184 | tf_op jit(solution)/shard_map/reduce_scatter | solution.py:242
  1028.5 347.9 %reduce-scatter.17.cloned.1.call-start = ((), (), s32[]{:S(2)}) async-start(), calls=%async_computation.23 | async-start | bytes 10485760 | tf_op jit(solution)/shard_map/reduce_scatter | solution.py:276
  1175.2 12.8 copy-start.11
  1208.3 223.8 %reduce-scatter.25.cloned.1.call-start = ((), (), s32[]{:S(2)}) async-start(), calls=%async_computation.27 | async-start | bytes 4718592 | tf_op jit(solution)/shard_map/reduce_scatter | solution.py:269
  1216.1 271.0 %reduce-scatter.23.cloned.1.call-start = ((), (), s32[]{:S(2)}) async-start(), calls=%async_computation.26 | async-start | bytes 4718592 | tf_op jit(solution)/shard_map/reduce_scatter | solution.py:268
  1223.0 319.3 %reduce-scatter.21.cloned.1.call-start = ((), (), s32[]{:S(2)}) async-start(), calls=%async_computation.25 | async-start | bytes 4718592 | tf_op jit(solution)/shard_map/reduce_scatter | solution.py:267
  1230.7 366.5 %reduce-scatter.19.cloned.1.call-start = ((), (), s32[]{:S(2)}) async-start(), calls=%async_computation.24 | async-start | bytes 4718592 | tf_op jit(solution)/shard_map/reduce_scatter | solution.py:266
  1241.2 135.2 %copy-start.6 = (bf16[256,2048]{1,0:T(8,128)(2,1)S(1)}, bf16[256,2048]{1,0:T(8,128)(2,1)}, u32[]{:S(2)}) copy-start(bf16[256,2048]{1,0:T(8,128)(2,1)} %param.26) | copy-start | bytes 3145732
  1241.2 135.2 %copy-start.25 = (f32[2048]{0:T(1024)S(1)}, f32[2048]{0:T(1024)}, u32[]{:S(2)}) copy-start(f32[2048]{0:T(1024)} %param.27) | copy-start | bytes 24580
  1241.2 135.2 %copy-start.28 = (f32[256]{0:T(256)S(1)}, f32[256]{0:T(256)}, u32[]{:S(2)}) copy-start(f32[256]{0:T(256)} %copy-done.27) | copy-start | bytes 3076
  1244.1 134.6 %copy-start.36 = (f32[256]{0:T(256)S(1)}, f32[256]{0:T(256)}, u32[]{:S(2)}) copy-start(f32[256]{0:T(256)} %copy-done.35) | copy-start | bytes 3076
  1244.1 134.6 %copy-start.34 = (f32[256]{0:T(256)S(1)}, f32[256]{0:T(256)}, u32[]{:S(2)}) copy-start(f32[256]{0:T(256)} %copy-done.33) | copy-start | bytes 3076
  1378.7 46.9 %copy-start.9 = (f32[256,2048]{1,0:T(8,128)S(1)}, f32[256,2048]{1,0:T(8,128)}, u32[]{:S(2)}) copy-start(f32[256,2048]{1,0:T(8,128)} %copy-done.8) | copy-start | bytes 6291460
  (47 other events, 153.1 us)
Sparse Core Ops, SparseCore 0:
  9.9 30.5 all-gather.14
  42.7 80.7 all-gather.10
  125.4 26.2 all-gather.16
  153.4 27.7 all-gather.12
  183.0 27.7 all-gather.18
  232.9 144.5 reduce-scatter.10
  379.4 54.8 all-gather.22
  436.5 80.7 all-gather.20
  519.1 52.7 all-gather.24
  586.7 145.6 reduce-scatter.12
  737.0 81.2 all-gather.26
  847.8 143.0 reduce-scatter.14
  999.9 81.3 all-gather.28
  1084.6 70.0 reduce-scatter.26
  1158.0 71.4 reduce-scatter.28
  1231.7 144.6 reduce-scatter.16
  1380.2 51.9 reduce-scatter.24
  1435.9 51.1 reduce-scatter.22
  1491.0 51.1 reduce-scatter.20
  1546.0 51.1 reduce-scatter.18
where the time goes:
time: 1610 us
  waiting for transfers between devices  1150 us (71%)
  matrix products  230 us (14%)
  blocking collectives  87.7 us (5%)
  other arithmetic  71.5 us (4%)
  local copies, waits for them, and re-layouts  36.9 us (2%)
  between operations  18.2 us (1%)
    reduce_scatter x1, waiting for transfers between devices, body(): lax.psum_scatter(contract(attended, full_out, 1, 1), 'tp', scatter_dimens...  144 us
    reduce_scatter x1, waiting for transfers between devices, body(): lax.psum_scatter(contract(grad_pre, full_up, 1, 1), 'tp', scatter_dimensi...  143 us
    reduce_scatter x1, waiting for transfers between devices, body(): lax.psum_scatter(grad_normed, 'tp', scatter_dimension=0, tiled=True)  131 us
    dot_general x12, matrix products, contract(): lax.dot_general(left_side, right_side, (((left_dim,), (right_dim,)), ((),...  101 us
    reduce_scatter x1, waiting for transfers between devices, body(): lax.psum_scatter(contract(active, full_down, 1, 1), 'tp', scatter_dimensi...  99.3 us
    psum x2, blocking collectives, body(): lax.psum((jnp.sum(weight_mask), jnp.sum(weight_mask[:, None] * deviation...  87.7 us
    all_gather x1, waiting for transfers between devices, body(): normed_all = lax.all_gather(normed, 'tp', axis=0, tiled=True)  82.9 us
    all_gather x1, waiting for transfers between devices, body(): normed_mid_all = lax.all_gather(normed_mid, 'tp', axis=0, tiled=True)  82.9 us
  transfers between devices with their start and end apart: 20, of which 17 were waited for; matrix products, arithmetic and copies ran while one was open for 16% of the time, Pallas kernels for 0%

commit v1 on v0

--- a/solution.py
+++ b/solution.py
@@ -151,6 +151,13 @@
         key_sum.reshape(length, width).astype(jnp.bfloat16),
         value_sum.reshape(length, width).astype(jnp.bfloat16),
     )
+
+
+def scatter_narrow(partial_sums, axis):
+    narrow_sums = lax.psum_scatter(
+        partial_sums.astype(jnp.bfloat16), axis, scatter_dimension=0, tiled=True
+    )
+    return narrow_sums.astype(jnp.float32)
 
 
 def body(
@@ -205,9 +212,7 @@
     ).astype(jnp.bfloat16)
     tables = tree_tables(parents[0], summary[0], normed_all.shape[0])
     attended, log_totals = attend_forward(queries, key_states, value_states, tables)
-    branch = lax.psum_scatter(
-        contract(attended, full_out, 1, 1), "tp", scatter_dimension=0, tiled=True
-    )
+    branch = scatter_narrow(contract(attended, full_out, 1, 1), "tp")
     hidden = inputs + branch + b_out
     normed_mid = layer_norm(hidden, norm2_gain, norm2_shift).astype(jnp.bfloat16)
     normed_mid_all = lax.all_gather(normed_mid, "tp", axis=0, tiled=True)
@@ -215,9 +220,7 @@
     active = jnp.maximum(
         jnp.dot(normed_mid_all, full_up, preferred_element_type=jnp.float32) + b_up, 0.0
     ).astype(jnp.bfloat16)
-    feed_out = lax.psum_scatter(
-        contract(active, full_down, 1, 1), "tp", scatter_dimension=0, tiled=True
-    )
+    feed_out = scatter_narrow(contract(active, full_down, 1, 1), "tp")
     output = hidden + feed_out + b_down
     weight_mask = valid_mask.astype(jnp.float32)
     deviation = output - teacher.astype(jnp.float32)
@@ -243,9 +246,7 @@
             grad_w_down.astype(jnp.bfloat16), "fsdp", scatter_dimension=0, tiled=True
         ).astype(jnp.float32),
     )
-    grad_mid = lax.psum_scatter(
-        contract(grad_pre, full_up, 1, 1), "tp", scatter_dimension=0, tiled=True
-    )
+    grad_mid = scatter_narrow(contract(grad_pre, full_up, 1, 1), "tp")
     second_norm, second_pull = jax.vjp(layer_norm, hidden, norm2_gain, norm2_shift)
     grad_hidden_norm, grad_norm2_gain, grad_norm2_shift = second_pull(grad_mid)
     grad_hidden = grad_output + grad_hidden_norm
@@ -263,17 +264,17 @@
     grad_w_key = contract(normed_all, grad_keys, 0, 0)
     grad_w_value = contract(normed_all, grad_values, 0, 0)
     grad_w_query, grad_w_key, grad_w_value, grad_w_out = (
-        lax.psum_scatter(grad_w_query, "fsdp", scatter_dimension=0, tiled=True),
-        lax.psum_scatter(grad_w_key, "fsdp", scatter_dimension=0, tiled=True),
-        lax.psum_scatter(grad_w_value, "fsdp", scatter_dimension=0, tiled=True),
-        lax.psum_scatter(grad_w_out, "fsdp", scatter_dimension=0, tiled=True),
+        scatter_narrow(grad_w_query, "fsdp"),
+        scatter_narrow(grad_w_key, "fsdp"),
+        scatter_narrow(grad_w_value, "fsdp"),
+        scatter_narrow(grad_w_out, "fsdp"),
     )
     grad_normed = (
         contract(grad_pre_query, full_query, 1, 1)
         + contract(grad_keys, full_key, 1, 1)
         + contract(grad_values, full_value, 1, 1)
     )
-    grad_normed = lax.psum_scatter(grad_normed, "tp", scatter_dimension=0, tiled=True)
+    grad_normed = scatter_narrow(grad_normed, "tp")
     first_norm, first_pull = jax.vjp(layer_norm, inputs, norm1_gain, norm1_shift)
     grad_input_norm, grad_norm1_gain, grad_norm1_shift = first_pull(grad_normed)
     grad_tokens = grad_hidden + grad_input_norm

time: 1610 us -> 1350 us (0.84)
  waiting for transfers between devices: 1150 us -> 883 us
    reduce_scatter x8, waiting for transfers between devices: 686 us -> 418 us  [scatter_narrow(): lax.psum_scatter(partial_sums.astype(jnp.bfloat16), axis, scatter_dimensi...]
  transfers between devices with their start and end apart: 20 -> 20, of which waited for: 17 -> 17; matrix products, arithmetic and copies ran while one was open for 16% -> 19% of each run, Pallas kernels for 0% -> 0%
where the time goes in v1:
time: 1350 us; the launch traced here: 1340 us
  waiting for transfers between devices  883 us (65%)
  matrix products  225 us (17%)
  blocking collectives  87.6 us (6%)
  other arithmetic  83.4 us (6%)
  local copies, waits for them, and re-layouts  33.8 us (3%)
  between operations  18.4 us (1%)
    reduce_scatter x8, waiting for transfers between devices, scatter_narrow(): lax.psum_scatter(partial_sums.astype(jnp.bfloat16), axis, scatter_dimensi...  418 us
    dot_general x12, matrix products, contract(): lax.dot_general(left_side, right_side, (((left_dim,), (right_dim,)), ((),...  96 us
    psum x2, blocking collectives, body(): lax.psum((jnp.sum(weight_mask), jnp.sum(weight_mask[:, None] * deviation...  87.6 us
    all_gather x1, waiting for transfers between devices, body(): normed_all = lax.all_gather(normed, 'tp', axis=0, tiled=True)  82.9 us
    all_gather x1, waiting for transfers between devices, body(): normed_mid_all = lax.all_gather(normed_mid, 'tp', axis=0, tiled=True)  82.9 us
    all_gather x1, waiting for transfers between devices, body(): lax.all_gather(grad_output.astype(jnp.bfloat16), 'tp', axis=0, tiled=True)  81.3 us
    all_gather x1, waiting for transfers between devices, body(): lax.all_gather(grad_hidden.astype(jnp.bfloat16), 'tp', axis=0, tiled=True)  52.7 us
    all_gather x1, waiting for transfers between devices, feed_weights(): lax.all_gather(w_up, 'fsdp', axis=0, tiled=True)  51.9 us
  transfers between devices with their start and end apart: 20, of which 17 were waited for; matrix products, arithmetic and copies ran while one was open for 19% of the time, Pallas kernels for 0%

profile of v1, /device:TPU:0, one launch (start us, length us, event | category | flops | bytes accessed | tf_op | source)
XLA Modules:
  0.0 1341.7 jit_solution(14886706895732890239)
XLA Ops:
  18.1 22.4 %all-gather.15.cloned.1.call-done = bf16[2048,512]{1,0:T(8,128)(2,1)} async-done(((bf16[256,512]{1,0:T(8,128)(2,1)}), bf16[2048,512]{1,0:T(8,128)(2,1)}) %all-gather.15.cloned.1.call-update) | async-done | bytes 2097168 | tf_op jit(solution)/shard_map/all_gather | solution.py:189
  40.6 82.9 %all-gather.11.cloned.1.call-done = bf16[1024,2048]{1,0:T(8,128)(2,1)} async-done(((bf16[256,2048]{1,0:T(8,128)(2,1)}), bf16[1024,2048]{1,0:T(8,128)(2,1)}) %all-gather.11.cloned.1.call-update) | async-done | bytes 4194320 | tf_op jit(solution)/shard_map/all_gather | solution.py:202
  128.7 22.9 %all-gather.17.cloned.1.call-done = bf16[2048,512]{1,0:T(8,128)(2,1)} async-done(((bf16[256,512]{1,0:T(8,128)(2,1)}), bf16[2048,512]{1,0:T(8,128)(2,1)}) %all-gather.17.cloned.1.call-update) | async-done | bytes 2097168 | tf_op jit(solution)/shard_map/all_gather | solution.py:190
  157.9 23.3 %all-gather.13.cloned.1.call-done = bf16[2048,512]{1,0:T(8,128)(2,1)} async-done(((bf16[256,512]{1,0:T(8,128)(2,1)}), bf16[2048,512]{1,0:T(8,128)(2,1)}) %all-gather.13.cloned.1.call-update) | async-done | bytes 2097168 | tf_op jit(solution)/shard_map/all_gather | solution.py:188
  187.5 34.6 %while.45 = (s32[]{:T(128)}, bf16[2,512,8,64]{1,3,2,0:T(8,128)(2,1)}, f32[2,8,512]{2,1,0:T(8,128)S(1)}, s32[2]{0:T(128)S(1)}, bf16[8,8]{1,0:T(8,128)(2,1)S(1)}, ...) while((s32[]{:T(128)}, ...), condition=%wide.region_9.10_spmd.clone, body=%wide.region_6.9_spmd.clone.sunk | while | flops 1123386368 | bytes 68315536 | solution.py:101
  232.3 76.1 %reduce-scatter.11.cloned.1.call-done = bf16[256,2048]{1,0:T(8,128)(2,1)} async-done(((bf16[1024,2048]{1,0:T(8,128)(2,1)}), bf16[256,2048]{1,0:T(8,128)(2,1)}) %reduce-scatter.11.cloned.1.call-update) | async-done | bytes 1048592 | tf_op jit(solution)/shard_map/reduce_scatter | solution.py:157
  313.3 51.9 %all-gather.23.cloned.1.call-done = bf16[2048,2048]{1,0:T(8,128)(2,1)} async-done(((bf16[256,2048]{1,0:T(8,128)(2,1)}), bf16[2048,2048]{1,0:T(8,128)(2,1)}) %all-gather.23.cloned.1.call-update) | async-done | bytes 8388624 | tf_op jit(solution)/shard_map/all_gather | solution.py:196
  365.1 82.9 %all-gather.21.cloned.1.call-done = bf16[1024,2048]{1,0:T(8,128)(2,1)} async-done(((bf16[256,2048]{1,0:T(8,128)(2,1)}), bf16[1024,2048]{1,0:T(8,128)(2,1)}) %all-gather.21.cloned.1.call-update) | async-done | bytes 4194320 | tf_op jit(solution)/shard_map/all_gather | solution.py:218
  448.1 14.0 %maximum_convert_fusion = bf16[1024,2048]{1,0:T(8,128)(2,1)} fusion(f32[2048]{0:T(1024)S(1)} %copy-done.46, bf16[1024,2048]{1,0:T(8,128)(2,1)} %all-gather.21.cloned.1.call-done, bf16[2048,2048]{1,0:T(8,128)(2,1)} %all-gather.23.cloned.1.call-done), kind=kOutput, calls=%fused_computation.104 | convolution fusion | flops 8596226048 | bytes 16785408 | tf_op jit(solution)/shard_map/dot_general | solution.py:221
  462.0 40.7 %all-gather.25.cloned.1.call-done = bf16[2048,2048]{1,0:T(8,128)(2,1)} async-done(((bf16[256,2048]{1,0:T(8,128)(2,1)}), bf16[2048,2048]{1,0:T(8,128)(2,1)}) %all-gather.25.cloned.1.call-update) | async-done | bytes 8388624 | tf_op jit(solution)/shard_map/all_gather | solution.py:197
  502.7 13.9 %convolution_convert_fusion.4 = bf16[1024,2048]{1,0:T(8,128)(2,1)} fusion(bf16[1024,2048]{1,0:T(8,128)(2,1)} %maximum_convert_fusion, bf16[2048,2048]{1,0:T(8,128)(2,1)} %all-gather.25.cloned.1.call-done), kind=kOutput, calls=%fused_computation.108 | convolution fusion | flops 8592031744 | bytes 16777216 | tf_op jit(solution)/shard_map/dot_general | solution.py:68
  517.9 44.5 %psum.78 = f32[]{:T(128)} all-reduce(f32[]{:T(128)} %convert_reduce_fusion.7), channel_id=1, replica_groups=mesh['fsdp'=8,'tp'=4] {'fsdp','tp'}, use_global_device_ids=true, to_apply=%region_17.18 | all-reduce | flops 1 | bytes 8 | tf_op jit(solution)/shard_map/psum | solution.py:227
  563.1 31.5 %reduce-scatter.13.cloned.1.call-done = bf16[256,2048]{1,0:T(8,128)(2,1)} async-done(((bf16[1024,2048]{1,0:T(8,128)(2,1)}), bf16[256,2048]{1,0:T(8,128)(2,1)}) %reduce-scatter.13.cloned.1.call-update) | async-done | bytes 1048592 | tf_op jit(solution)/shard_map/reduce_scatter | solution.py:157
  599.2 81.3 %all-gather.27.cloned.1.call-done = bf16[1024,2048]{1,0:T(8,128)(2,1)} async-done(((bf16[256,2048]{1,0:T(8,128)(2,1)}), bf16[1024,2048]{1,0:T(8,128)(2,1)}) %all-gather.27.cloned.1.call-update) | async-done | bytes 4194320 | tf_op jit(solution)/shard_map/all_gather | solution.py:234
  680.4 14.0 %convert_reduce_fusion = (f32[2048]{0:T(1024)}, bf16[1024,2048]{1,0:T(8,128)(2,1)S(1)}) fusion(bf16[1024,2048]{1,0:T(8,128)(2,1)} %all-gather.27.cloned.1.call-done, bf16[2048,2048]{1,0:T(8,128)(2,1)} %all-gather.25.cloned.1.call-done, bf16[1024,2048]{1,0:T(8,128)(2,1)} %maximum_convert_fusion), kind=kOutput, calls=%fused_computation.101 | convolution fusion | flops 8600418304 | bytes 20979712 | tf_op jit(solution)/shard_map/dot_general | solution.py:238
  696.4 12.6 convolution_convert_fusion.3
  709.1 75.4 %reduce-scatter.15.cloned.1.call-done = bf16[256,2048]{1,0:T(8,128)(2,1)} async-done(((bf16[1024,2048]{1,0:T(8,128)(2,1)}), bf16[256,2048]{1,0:T(8,128)(2,1)}) %reduce-scatter.15.cloned.1.call-update) | async-done | bytes 1048592 | tf_op jit(solution)/shard_map/reduce_scatter | solution.py:157
  794.3 14.4 %convolution_convert_fusion.1 = bf16[2048,2048]{1,0:T(8,128)(2,1)} fusion(bf16[1024,2048]{1,0:T(8,128)(2,1)} %all-gather.27.cloned.1.call-done, bf16[1024,2048]{1,0:T(8,128)(2,1)} %maximum_convert_fusion), kind=kOutput, calls=%fused_computation.105 | convolution fusion | flops 8594128896 | bytes 16777216 | tf_op jit(solution)/shard_map/dot_general | solution.py:68
  808.8 14.1 %convolution_convert_fusion.2 = bf16[2048,2048]{1,0:T(8,128)(2,1)} fusion(bf16[1024,2048]{1,0:T(8,128)(2,1)} %all-gather.21.cloned.1.call-done, bf16[1024,2048]{1,0:T(8,128)(2,1)} %copy-done.50), kind=kOutput, calls=%fused_computation.106 | convolution fusion | flops 8594128896 | bytes 16777216 | tf_op jit(solution)/shard_map/dot_general | solution.py:68
  823.0 52.7 %all-gather.29.cloned.1.call-done = bf16[1024,2048]{1,0:T(8,128)(2,1)} async-done(((bf16[256,2048]{1,0:T(8,128)(2,1)}), bf16[1024,2048]{1,0:T(8,128)(2,1)}) %all-gather.29.cloned.1.call-update) | async-done | bytes 4194320 | tf_op jit(solution)/shard_map/all_gather | solution.py:253
  881.9 6.9 convolution_convert_fusion.10
  889.9 104.8 %while.47 = (s32[]{:T(128)}, f32[1024,8,64]{0,2,1:T(8,128)S(1)}, f32[1024,8,64]{0,2,1:T(8,128)}, bf16[2,512,8,64]{1,3,2,0:T(8,128)(2,1)}, s32[2]{0:T(128)S(1)}, ...) while((s32[]{:T(128)}, f32[1024,8,64]{0,2,1:T(8,128)S(1)}, ...), condition=%wide.region_23.24_spmd.clone, body=%wide.region_21.23_spmd.clone.sunk | while | flops 2748679168 | bytes 224012784 | solution.py:145
  910.9 12.9 multiply_reduce_fusion.4
  923.8 12.7 multiply_convert_fusion.4
  961.8 14.8 %multiply_reduce_fusion.4 = (f32[8,512]{1,0:T(8,128)S(1)}, f32[8,512,1024]{2,1,0:T(8,128)}) fusion(f32[8,512,1024]{2,1,0:T(8,128)} %copy-done, f32[8,512]{1,0:T(8,128)S(1)} %dynamic-slice_bitcast_fusion.2, pred[512,1024]{1,0:T(8,128)(4,1)S(1)} %copy-done.4, bf16[1024,8,64]{0,2,1:T(8,128)(2,1)} %get-tuple-element.828, ...), kind=kOutput, calls=%fused_computation.51.clone.1 | convolution fusion | flops 553644032 | bytes 35684356 | tf_op jit(solution)/shard_map/while/body/eval_jaxpr/qhd,khd->hqk/dot_general | solution.py:124
  976.6 13.2 multiply_convert_fusion.4
  1038.1 30.0 %reduce-scatter.25.cloned.1.call-done = bf16[256,512]{1,0:T(8,128)(2,1)} async-done(((bf16[2048,512]{1,0:T(8,128)(2,1)}), bf16[256,512]{1,0:T(8,128)(2,1)}) %reduce-scatter.25.cloned.1.call-update) | async-done | bytes 262160 | tf_op jit(solution)/shard_map/reduce_scatter | solution.py:157
  1069.9 42.5 %reduce-scatter.23.cloned.1.call-done = bf16[256,512]{1,0:T(8,128)(2,1)} async-done(((bf16[2048,512]{1,0:T(8,128)(2,1)}), bf16[256,512]{1,0:T(8,128)(2,1)}) %reduce-scatter.23.cloned.1.call-update) | async-done | bytes 262160 | tf_op jit(solution)/shard_map/reduce_scatter | solution.py:157
  1114.2 42.5 %reduce-scatter.19.cloned.1.call-done = bf16[256,512]{1,0:T(8,128)(2,1)} async-done(((bf16[2048,512]{1,0:T(8,128)(2,1)}), bf16[256,512]{1,0:T(8,128)(2,1)}) %reduce-scatter.19.cloned.1.call-update) | async-done | bytes 262160 | tf_op jit(solution)/shard_map/reduce_scatter | solution.py:157
  1158.5 42.6 %reduce-scatter.21.cloned.1.call-done = bf16[256,512]{1,0:T(8,128)(2,1)} async-done(((bf16[2048,512]{1,0:T(8,128)(2,1)}), bf16[256,512]{1,0:T(8,128)(2,1)}) %reduce-scatter.21.cloned.1.call-update) | async-done | bytes 262160 | tf_op jit(solution)/shard_map/reduce_scatter | solution.py:157
  1202.9 77.1 %reduce-scatter.17.cloned.1.call-done = bf16[256,2048]{1,0:T(8,128)(2,1)} async-done(((bf16[1024,2048]{1,0:T(8,128)(2,1)}), bf16[256,2048]{1,0:T(8,128)(2,1)}) %reduce-scatter.17.cloned.1.call-update) | async-done | bytes 1048592 | tf_op jit(solution)/shard_map/reduce_scatter | solution.py:157
  1284.3 43.1 %all-reduce.2 = (f32[]{:T(128)}, f32[2048]{0:T(1024)}, f32[2048]{0:T(1024)}, f32[2048]{0:T(1024)S(1)}, f32[2048]{0:T(1024)S(1)}, /*index=5*/f32[2048]{0:T(1024)}...) all-reduce(f32[]{:T(128)} %get-tuple-element.543, ...), channel_id=1, replica_groups=mesh['fsdp'=8,'tp'=4] {'fsdp','tp'}, use_global_device_ids=true, to_apply=%region_15.16 | all-reduce | flops 24577 | bytes 196616 | tf_op jit(solution)/shard_map/psum | solution.py:227
  (296 shorter events, 206.5 us)
Async XLA Ops:
  7.2 33.3 %all-gather.15.cloned.1.call-start = ((), (), s32[]{:S(2)}) async-start(), calls=%async_computation.12 | async-start | bytes 2359296 | tf_op jit(solution)/shard_map/all_gather | solution.py:189
  8.0 115.5 %all-gather.11.cloned.1.call-start = ((), (), s32[]{:S(2)}) async-start(), calls=%async_computation.10 | async-start | bytes 5242880 | tf_op jit(solution)/shard_map/all_gather | solution.py:202
  13.7 137.9 %all-gather.17.cloned.1.call-start = ((), (), s32[]{:S(2)}) async-start(), calls=%async_computation.13 | async-start | bytes 2359296 | tf_op jit(solution)/shard_map/all_gather | solution.py:190
  14.5 166.8 %all-gather.13.cloned.1.call-start = ((), (), s32[]{:S(2)}) async-start(), calls=%async_computation.11 | async-start | bytes 2359296 | tf_op jit(solution)/shard_map/all_gather | solution.py:188
  15.0 210.1 %all-gather.19.cloned.1.call-start = ((), (), s32[]{:S(2)}) async-start(), calls=%async_computation.14 | async-start | bytes 2359296 | tf_op jit(solution)/shard_map/all_gather | solution.py:191
  15.6 292.8 %reduce-scatter.11.cloned.1.call-start = ((), (), s32[]{:S(2)}) async-start(), calls=%async_computation.15 | async-start | bytes 5242880 | tf_op jit(solution)/shard_map/reduce_scatter | solution.py:157
  18.1 133.5 %copy-start.47 = (f32[512]{0:T(512)S(1)}, f32[512]{0:T(512)}, u32[]{:S(2)}) copy-start(f32[512]{0:T(512)} %param.33) | copy-start | bytes 6148
  231.5 133.6 %all-gather.23.cloned.1.call-start = ((), (), s32[]{:S(2)}) async-start(), calls=%async_computation.17 | async-start | bytes 9437184 | tf_op jit(solution)/shard_map/all_gather | solution.py:196
  232.3 215.8 %all-gather.21.cloned.1.call-start = ((), (), s32[]{:S(2)}) async-start(), calls=%async_computation.16 | async-start | bytes 5242880 | tf_op jit(solution)/shard_map/all_gather | solution.py:218
  310.8 137.2 %copy-start.46 = (f32[2048]{0:T(1024)S(1)}, f32[2048]{0:T(1024)}, u32[]{:S(2)}) copy-start(f32[2048]{0:T(1024)} %param.39) | copy-start | bytes 24580
  312.5 190.2 %all-gather.25.cloned.1.call-start = ((), (), s32[]{:S(2)}) async-start(), calls=%async_computation.18 | async-start | bytes 9437184 | tf_op jit(solution)/shard_map/all_gather | solution.py:197
  313.2 281.4 %reduce-scatter.13.cloned.1.call-start = ((), (), s32[]{:S(2)}) async-start(), calls=%async_computation.19 | async-start | bytes 5242880 | tf_op jit(solution)/shard_map/reduce_scatter | solution.py:157
  516.7 163.7 %all-gather.27.cloned.1.call-start = ((), (), s32[]{:S(2)}) async-start(), calls=%async_computation.20 | async-start | bytes 5242880 | tf_op jit(solution)/shard_map/all_gather | solution.py:234
  599.1 185.4 %reduce-scatter.15.cloned.1.call-start = ((), (), s32[]{:S(2)}) async-start(), calls=%async_computation.21 | async-start | bytes 5242880 | tf_op jit(solution)/shard_map/reduce_scatter | solution.py:157
  709.0 166.6 %all-gather.29.cloned.1.call-start = ((), (), s32[]{:S(2)}) async-start(), calls=%async_computation.22 | async-start | bytes 5242880 | tf_op jit(solution)/shard_map/all_gather | solution.py:253
  794.3 237.1 %reduce-scatter.29.cloned.1.call-start = ((), (), s32[]{:S(2)}) async-start(), calls=%async_computation.29 | async-start | bytes 9437184 | tf_op jit(solution)/shard_map/reduce_scatter | solution.py:245
  808.8 225.5 %reduce-scatter.27.cloned.1.call-start = ((), (), s32[]{:S(2)}) async-start(), calls=%async_computation.28 | async-start | bytes 9437184 | tf_op jit(solution)/shard_map/reduce_scatter | solution.py:242
  822.9 245.2 %reduce-scatter.25.cloned.1.call-start = ((), (), s32[]{:S(2)}) async-start(), calls=%async_computation.27 | async-start | bytes 2359296 | tf_op jit(solution)/shard_map/reduce_scatter | solution.py:157
  881.9 230.5 %reduce-scatter.23.cloned.1.call-start = ((), (), s32[]{:S(2)}) async-start(), calls=%async_computation.26 | async-start | bytes 2359296 | tf_op jit(solution)/shard_map/reduce_scatter | solution.py:157
  1003.6 153.0 %reduce-scatter.19.cloned.1.call-start = ((), (), s32[]{:S(2)}) async-start(), calls=%async_computation.24 | async-start | bytes 2359296 | tf_op jit(solution)/shard_map/reduce_scatter | solution.py:157
  1011.1 189.9 %reduce-scatter.21.cloned.1.call-start = ((), (), s32[]{:S(2)}) async-start(), calls=%async_computation.25 | async-start | bytes 2359296 | tf_op jit(solution)/shard_map/reduce_scatter | solution.py:157
  1017.3 262.7 %reduce-scatter.17.cloned.1.call-start = ((), (), s32[]{:S(2)}) async-start(), calls=%async_computation.23 | async-start | bytes 5242880 | tf_op jit(solution)/shard_map/reduce_scatter | solution.py:157
  1037.2 242.9 %copy-start.3 = (bf16[256,2048]{1,0:T(8,128)(2,1)S(1)}, bf16[256,2048]{1,0:T(8,128)(2,1)}, u32[]{:S(2)}) copy-start(bf16[256,2048]{1,0:T(8,128)(2,1)} %param.26) | copy-start | bytes 3145732
  1037.2 242.9 %copy-start.26 = (f32[2048]{0:T(1024)S(1)}, f32[2048]{0:T(1024)}, u32[]{:S(2)}) copy-start(f32[2048]{0:T(1024)} %param.27) | copy-start | bytes 24580
  1037.2 242.9 %copy-start.29 = (f32[256]{0:T(256)S(1)}, f32[256]{0:T(256)}, u32[]{:S(2)}) copy-start(f32[256]{0:T(256)} %copy-done.28) | copy-start | bytes 3076
  1069.9 212.1 %copy-start.37 = (f32[256]{0:T(256)S(1)}, f32[256]{0:T(256)}, u32[]{:S(2)}) copy-start(f32[256]{0:T(256)} %copy-done.36) | copy-start | bytes 3076
  1069.9 212.1 %copy-start.35 = (f32[256]{0:T(256)S(1)}, f32[256]{0:T(256)}, u32[]{:S(2)}) copy-start(f32[256]{0:T(256)} %copy-done.34) | copy-start | bytes 3076
  1202.9 81.4 %copy-start.30 = (f32[2048]{0:T(1024)S(1)}, f32[2048]{0:T(1024)}, u32[]{:S(2)}) copy-start(f32[2048]{0:T(1024)} %get-tuple-element.460) | copy-start | bytes 24580
  1202.9 81.4 %copy-start.31 = (f32[2048]{0:T(1024)S(1)}, f32[2048]{0:T(1024)}, u32[]{:S(2)}) copy-start(f32[2048]{0:T(1024)} %get-tuple-element.454) | copy-start | bytes 24580
  1202.9 81.4 %copy-start.32 = (f32[2048]{0:T(1024)S(1)}, f32[2048]{0:T(1024)}, u32[]{:S(2)}) copy-start(f32[2048]{0:T(1024)} %get-tuple-element.528) | copy-start | bytes 24580
  1202.9 81.4 %copy-start.33 = (f32[2048]{0:T(1024)S(1)}, f32[2048]{0:T(1024)}, u32[]{:S(2)}) copy-start(f32[2048]{0:T(1024)} %get-tuple-element.544) | copy-start | bytes 24580
  1202.9 127.1 %copy-start.10 = (f32[256,2048]{1,0:T(8,128)S(1)}, f32[256,2048]{1,0:T(8,128)}, u32[]{:S(2)}) copy-start(f32[256,2048]{1,0:T(8,128)} %copy-done.9) | copy-start | bytes 6291460
  (47 other events, 600.3 us)
Sparse Core Ops, SparseCore 0:
  9.9 30.5 all-gather.14
  42.7 80.7 all-gather.10
  125.4 26.2 all-gather.16
  153.4 27.7 all-gather.12
  183.0 27.7 all-gather.18
  231.6 76.7 reduce-scatter.10
  310.4 54.7 all-gather.22
  367.3 80.7 all-gather.20
  449.9 52.7 all-gather.24
  516.8 77.8 reduce-scatter.12
  599.2 81.1 all-gather.26
  709.1 75.2 reduce-scatter.14
  794.4 81.2 all-gather.28
  879.0 70.0 reduce-scatter.28
  952.3 71.4 reduce-scatter.26
  1026.9 41.1 reduce-scatter.24
  1071.2 41.0 reduce-scatter.22
  1115.5 41.1 reduce-scatter.18
  1159.9 41.0 reduce-scatter.20
  1203.2 76.7 reduce-scatter.16

commit v2 on v1

v2 whole, which is shorter than its diff:
```python
import jax
import jax.numpy as jnp
from jax import lax
from jax.experimental import pallas as pl
from jax.experimental.pallas import tpu as pltpu
from jax.sharding import PartitionSpec as P

HD = 64
PAIR = 2 * HD
EPSILON = 1e-05
MASKED_SCORE = -1e30
KEY_PAD = 128


def layer_norm(vectors, norm_gain, norm_shift):
    centre = jnp.mean(vectors, axis=-1, keepdims=True)
    centred = vectors - centre
    spread = jnp.mean(centred * centred, axis=-1, keepdims=True)
    return centred * lax.rsqrt(spread + EPSILON) * norm_gain + norm_shift


def contract(left_side, right_side, left_dim, right_dim):
    return lax.dot_general(
        left_side,
        right_side,
        (((left_dim,), (right_dim,)), ((), ())),
        preferred_element_type=jnp.float32,
    )


def narrow(values):
    return values.astype(jnp.bfloat16)


def bits_below(count, first):
    bits = []
    bit = first
    while bit < count:
        bits.append(bit)
        bit *= 2
    return bits


def segment_scores(q_ref, k_ref, ks_ref, seen_ref, row, seg, tree, place):
    rows = pl.ds(row, seg)
    lane = lax.broadcasted_iota(jnp.int32, (seg, PAIR), 1)
    first_head = lane < HD
    query = q_ref[rows, :]
    none = jnp.zeros_like(query)
    both = jnp.concatenate(
        [jnp.where(first_head, query, none), jnp.where(first_head, none, query)], axis=0
    )
    keys = jnp.concatenate([k_ref[rows, :], ks_ref[tree]], axis=0)
    scores = contract(both, keys, 1, 1)
    width = seg + KEY_PAD
    column = lax.broadcasted_iota(jnp.int32, (2 * seg, width), 1)
    position = lax.broadcasted_iota(jnp.int32, (2 * seg, width), 0)
    position = jnp.where(position >= seg, position - seg, position)
    seen = jnp.concatenate(
        [jnp.ones((1, seg), jnp.float32), seen_ref[pl.ds(place, 1), :]], axis=1
    )
    reach = jnp.where(column < seg, position, width)
    allowed = (column <= reach) & (seen > 0.5)
    scores = jnp.where(allowed, scores, MASKED_SCORE)
    highest = jnp.max(scores, axis=1, keepdims=True)
    raised = jnp.exp(scores - highest)
    probs = raised * (1.0 / jnp.sum(raised, axis=1, keepdims=True))
    return rows, first_head, both, keys, probs


def walk_segments(blocks, rows, seg, step):
    per = rows // seg
    for block in range(blocks):
        tree, far = block % 2, block // 2
        for inner in range(per):
            step(block * rows + inner * seg, tree, (tree * 2 + far) * per + inner)


def forward_kernel(rows, seg, q_ref, k_ref, v_ref, ks_ref, vs_ref, seen_ref, out_ref):
    def step(row, tree, place):
        at, first_head, both, keys, probs = segment_scores(
            q_ref, k_ref, ks_ref, seen_ref, row, seg, tree, place
        )
        values = jnp.concatenate([v_ref[at, :], vs_ref[tree]], axis=0)
        mixed = contract(narrow(probs), values, 1, 0)
        out_ref[at, :] = narrow(jnp.where(first_head, mixed[:seg], mixed[seg:]))

    walk_segments(4, rows, seg, step)


def backward_kernel(
    rows, seg, q_ref, k_ref, v_ref, go_ref, ks_ref, vs_ref, seen_ref, gq_ref, gk_ref, gv_ref, gks_ref, gvs_ref
):
    gks_ref[...] = jnp.zeros_like(gks_ref)
    gvs_ref[...] = jnp.zeros_like(gvs_ref)

    def step(row, tree, place):
        at, first_head, both, keys, probs = segment_scores(
            q_ref, k_ref, ks_ref, seen_ref, row, seg, tree, place
        )
        values = jnp.concatenate([v_ref[at, :], vs_ref[tree]], axis=0)
        grad_out = go_ref[at, :]
        none = jnp.zeros_like(grad_out)
        grad_both = jnp.concatenate(
            [jnp.where(first_head, grad_out, none), jnp.where(first_head, none, grad_out)], axis=0
        )
        grad_probs = contract(grad_both, values, 1, 1)
        inner = jnp.sum(probs * grad_probs, axis=1, keepdims=True)
        grad_scores = narrow(probs * (grad_probs - inner))
        grad_query = contract(grad_scores, keys, 1, 0)
        grad_query = narrow(jnp.where(first_head, grad_query[:seg], grad_query[seg:]))
        gq_ref[at, :] = grad_query * jnp.bfloat16(0.125)
        grad_keys = contract(grad_scores, both, 0, 0)
        gk_ref[at, :] = narrow(grad_keys[:seg])
        gks_ref[tree] += grad_keys[seg:]
        grad_values = contract(narrow(probs), grad_both, 0, 0)
        gv_ref[at, :] = narrow(grad_values[:seg])
        gvs_ref[tree] += grad_values[seg:]

    walk_segments(4, rows, seg, step)


def attend(kernel, rows, seg, operands, key_sums, seen, outputs, sums):
    count, width = operands[0].shape
    column_block = pl.BlockSpec((count, PAIR), lambda pair: (0, pair))
    sum_block = pl.BlockSpec((2, KEY_PAD, PAIR), lambda pair: (0, 0, pair))
    return pl.pallas_call(
        lambda *refs: kernel(rows, seg, *refs),
        grid=(width // PAIR,),
        in_specs=[column_block] * len(operands)
        + [sum_block] * 2
        + [pl.BlockSpec(seen.shape, lambda pair: (0, 0))],
        out_specs=[column_block] * outputs + [sum_block] * sums,
        out_shape=[jax.ShapeDtypeStruct((count, width), jnp.bfloat16)] * outputs
        + [jax.ShapeDtypeStruct((2, KEY_PAD, width), jnp.float32)] * sums,
        name="attend_forward" if sums == 0 else "attend_backward",
    )(*operands, *key_sums, seen)


def make_body(fsdp, tp):
    world = fsdp * tp
    low = 1
    top = tp // 2
    middle = bits_below(top, 2)
    mate = tp
    plane = bits_below(world, 2 * tp)

    def swap(values, mask):
        return lax.ppermute(values, ("fsdp", "tp"), [(i, i ^ mask) for i in range(world)])

    def agrees(i):
        return (i // tp) % 2 == (i % tp) // top

    def send(values, mask, alike):
        pairs = [(i, i ^ mask) for i in range(world) if agrees(i) == alike]
        return lax.ppermute(values, ("fsdp", "tp"), pairs)

    def everyone(values):
        for mask in bits_below(world, 1):
            values = values + swap(values, mask)
        return values

    def body(
        tokens,
        norm1_gain,
        norm1_shift,
        w_query,
        b_query,
        w_key,
        w_value,
        b_value,
        w_out,
        b_out,
        norm2_gain,
        norm2_shift,
        w_up,
        b_up,
        w_down,
        b_down,
        teacher,
        valid_mask,
        parents,
        summary,
    ):
        rows, depth = tokens.shape
        strip = depth // fsdp
        half = depth // 2
        column = lax.axis_index("tp")
        device = lax.axis_index("fsdp")
        core = device % 2
        spot = device // 2
        upper = column // top
        alike = core == upper
        segments = parents.shape[1]
        marks = summary.shape[2]
        seg = rows * tp // segments
        per = rows // seg

        def mirrored(k):
            mirror, found = 0, 0
            for i in range(len(plane)):
                found = (k >> i) & 1
                mirror = mirror * 2 + found
            return mirror

        blocks = fsdp // 2

        def to_relative(values):
            parts = []
            for side in range(2):
                for k in range(blocks):
                    away = k if side == 0 else mirrored(k)
                    start = (2 * (spot ^ away) + side) * strip
                    parts.append(lax.dynamic_slice_in_dim(values, start, strip, values.ndim - 1))
            return jnp.concatenate(parts, axis=-1)

        def to_absolute(values):
            parts = []
            for place in range(blocks):
                away = spot ^ place
                back = jnp.zeros_like(away)
                for i in range(len(plane)):
                    back = back * 2 + ((away >> i) & 1)
                for side in range(2):
                    start = (away if side == 0 else blocks + back) * strip
                    parts.append(lax.dynamic_slice_in_dim(values, start, strip, values.ndim - 1))
            return jnp.concatenate(parts, axis=-1)

        def gather_weight(shard):
            near = send(shard, mate, False)
            far_same = send(shard, top, True)
            far_other = send(shard, mate | top, False)
            same = jnp.where(alike, shard, far_same)
            other = jnp.where(alike, near, far_other)
            for mask in middle:
                same = jnp.concatenate([same, swap(same, mask)], axis=1)
                other = jnp.concatenate([other, swap(other, mask)], axis=1)
            pieces = []
            for side, order in enumerate((plane, plane[::-1])):
                held = [jnp.where(core == side, same, other)]
                for mask in order:
                    now = held[0] if len(held) == 1 else jnp.concatenate(held, axis=0)
                    held.append(swap(now, mask))
                pieces += held
            return jnp.concatenate(pieces, axis=0)

        def scatter_weight(left, right):
            outs = []
            firsts = []
            for side, order in enumerate((plane, plane[::-1])):
                base = side * half
                away = narrow(contract(left[:, base + half // 2 : base + half], right, 0, 0))
                firsts.append((base, order, swap(away, order[-1])))
            for base, order, came in firsts:
                kept = contract(left[:, base : base + half // 2], right, 0, 0) + came
                for mask in order[-2::-1]:
                    size = kept.shape[0] // 2
                    kept = kept[:size] + swap(narrow(kept[size:]), mask)
                outs.append(kept)
            same = narrow(jnp.where(core == 0, outs[0], outs[1]))
            other = narrow(jnp.where(core == 0, outs[1], outs[0]))
            for mask in middle[::-1]:
                size = same.shape[1] // 2
                same = narrow(same[:, :size].astype(jnp.float32) + swap(same[:, size:], mask))
                other = narrow(other[:, :size].astype(jnp.float32) + swap(other[:, size:], mask))
            near = send(other, mate, True)
            far_same = send(same, top, False)
            far_other = send(other, mate | top, False)
            own = jnp.where(alike, same, jnp.zeros_like(same)).astype(jnp.float32)
            return own + near + far_same + far_other

        def gather_bias(part):
            part = jnp.where(alike, part, swap(part, top))
            for mask in middle:
                part = jnp.concatenate([part, swap(part, mask)], axis=1)
            return part

        def spread_rows(own):
            across = swap(own, low)
            near = jnp.concatenate([own, swap(own, mate)], axis=0)
            far = jnp.concatenate([across, swap(across, mate)], axis=0)
            return near, far

        def collect_rows(partial):
            far_mate = swap(narrow(partial(3)), mate)
            crossing = swap(narrow(partial(2) + far_mate), low)
            near_mate = swap(narrow(partial(1)), mate)
            return partial(0) + near_mate + crossing

        def row_block(values, block):
            return values[block * rows : (block + 1) * rows]

        inputs = to_relative(tokens).astype(jnp.float32)
        target = to_relative(teacher).astype(jnp.float32)
        vectors = to_relative(
            jnp.stack([norm1_gain, norm1_shift, b_out, norm2_gain, norm2_shift, b_down])
        )
        gain1, shift1, bias_out, gain2, shift2, bias_down = [vectors[i] for i in range(6)]
        weight_mask = valid_mask.astype(jnp.float32)[:, None]
        counted = everyone(jnp.full((8, 128), jnp.sum(weight_mask), jnp.float32))
        valid_count = counted[0, 0]

        slices = tp // 4
        w_kv = gather_weight(jnp.concatenate([w_key, w_value], axis=1))
        w_qo = gather_weight(jnp.concatenate([w_query, w_out], axis=1))
        full_up = gather_weight(w_up)
        full_down = gather_weight(w_down)

        def split_two(joined):
            parts = joined.reshape(joined.shape[0], slices, 2, -1)
            return [parts[:, :, i].reshape(joined.shape[0], -1) for i in range(2)]

        full_key, full_value = split_two(w_kv)
        full_query, full_out = split_two(w_qo)
        head_bias = gather_bias(jnp.stack([b_query, b_value]))
        bias_query, bias_value = head_bias[0], head_bias[1]
        bias_up = gather_bias(b_up[None])[0]

        tables = jnp.concatenate([parents[0][:, None], summary[0]], axis=1)
        tables = jnp.stack([tables, swap(tables, mate)])
        seg_ids = jnp.arange(segments, dtype=jnp.int32)
        moved = seg_ids ^ (column * per)
        picks = moved[:, None] == seg_ids[None, :]
        tables = jnp.sum(jnp.where(picks[None, :, :, None], tables[:, None], 0), axis=2)
        parent_rel = jnp.where(tables[:, :, 0] >= 0, tables[:, :, 0] ^ (column * per), -1)
        offsets_rel = tables[:, :, 1:]
        reach = (parent_rel[:, :, None] == seg_ids[None, None, :]).astype(jnp.float32)
        unit = (seg_ids[:, None] == seg_ids[None, :]).astype(jnp.float32)[None]
        closure = reach + unit
        steps = 1
        while steps < segments:
            closure = jnp.einsum("tij,tjk->tik", closure, closure)
            closure = jnp.minimum(closure, 1.0)
            steps *= 2
        closure = closure - unit
        local = 2 * per
        seen = jnp.repeat(closure[:, :local], marks, axis=2)
        seen = jnp.pad(seen, ((0, 0), (0, 0), (0, KEY_PAD - segments * marks)))
        seen = seen.reshape(2 * local, KEY_PAD)
        far_id = jnp.arange(local, dtype=jnp.int32) // per
        inner_id = jnp.arange(local, dtype=jnp.int32) % per
        tree_id = jnp.arange(2, dtype=jnp.int32)
        start = (far_id[None, :] * 2 + tree_id[:, None]) * rows + inner_id[None, :] * seg
        summary_row = (start[:, :, None] + offsets_rel[:, :local]).reshape(-1)
        chosen = narrow(summary_row[:, None] == jnp.arange(4 * rows, dtype=jnp.int32)[None, :])

        def spread_sums(part):
            for mask in middle + [top]:
                part = jnp.concatenate([part, swap(part, mask)], axis=1)
            return jnp.pad(part, ((0, 0), (0, KEY_PAD - part.shape[1]), (0, 0)))

        def collect_sums(whole):
            whole = whole[:, : segments * marks]
            for mask in [top] + middle[::-1]:
                size = whole.shape[1] // 2
                whole = whole[:, :size] + swap(narrow(whole[:, size:]), mask)
            return whole

        normed = narrow(layer_norm(inputs, gain1, shift1))
        normed_near, normed_far = spread_rows(normed)
        normed_all = jnp.concatenate([normed_near, normed_far], axis=0)
        key_states = narrow(contract(normed_all, full_key, 1, 0))
        value_states = narrow(contract(normed_all, full_value, 1, 0) + bias_value)
        queries = narrow((contract(normed_all, full_query, 1, 0) + bias_query) * 0.125)
        width = queries.shape[1]
        picked = jnp.concatenate(
            [narrow(contract(chosen, key_states, 1, 0)), narrow(contract(chosen, value_states, 1, 0))],
            axis=1,
        )
        picked = spread_sums(picked.reshape(2, local * marks, 2 * width))
        key_sums = (picked[:, :, :width], picked[:, :, width:])
        (attended,) = attend(
            forward_kernel, rows, seg, (queries, key_states, value_states), key_sums, seen, 1, 0
        )
        branch = collect_rows(lambda b: contract(row_block(attended, b), full_out, 1, 1))
        hidden = inputs + branch + bias_out

        normed_mid = narrow(layer_norm(hidden, gain2, shift2))
        mid_near, mid_far = spread_rows(normed_mid)
        active = [
            narrow(jnp.maximum(contract(part, full_up, 1, 0) + bias_up, 0.0))
            for part in (mid_near, mid_far)
        ]
        active_all = jnp.concatenate(active, axis=0)
        mid_all = jnp.concatenate([mid_near, mid_far], axis=0)
        feed_out = collect_rows(lambda b: contract(row_block(active_all, b), full_down, 1, 1))
        output = hidden + feed_out + bias_down

        deviation = output - target
        squares = jnp.sum(weight_mask * deviation * deviation)
        total_tokens = rows * world
        grad_output = (2.0 * total_tokens / valid_count) * weight_mask * deviation

        feed_near, feed_far = spread_rows(narrow(grad_output))
        feed_all = jnp.concatenate([feed_near, feed_far], axis=0)
        grad_pre = [
            narrow(jnp.where(kept > 0, contract(part, full_down, 1, 0), 0.0))
            for part, kept in zip((feed_near, feed_far), active)
        ]
        grad_pre_all = jnp.concatenate(grad_pre, axis=0)
        grad_mid = collect_rows(lambda b: contract(row_block(grad_pre_all, b), full_up, 1, 1))
        grad_w_down = scatter_weight(feed_all, active_all)
        grad_w_up = scatter_weight(mid_all, grad_pre_all)
        second_norm, second_pull = jax.vjp(layer_norm, hidden, gain2, shift2)
        grad_hidden_norm, grad_gain2, grad_shift2 = second_pull(grad_mid)
        grad_hidden = grad_output + grad_hidden_norm

        branch_near, branch_far = spread_rows(narrow(grad_hidden))
        branch_all = jnp.concatenate([branch_near, branch_far], axis=0)
        grad_attended = narrow(contract(branch_all, full_out, 1, 0))
        grad_w_out = scatter_weight(branch_all, attended)
        grad_pre_query, grad_keys, grad_values, key_part, value_part = attend(
            backward_kernel,
            rows,
            seg,
            (queries, key_states, value_states, grad_attended),
            key_sums,
            seen,
            3,
            2,
        )
        grad_w_query = scatter_weight(normed_all, grad_pre_query)
        parts = collect_sums(jnp.concatenate([key_part, value_part], axis=2))
        parts = narrow(parts.reshape(-1, 2 * width))
        grad_keys = narrow(grad_keys + contract(chosen, parts[:, :width], 0, 0))
        grad_values = narrow(grad_values + contract(chosen, parts[:, width:], 0, 0))
        grad_w_key = scatter_weight(normed_all, grad_keys)
        grad_w_value = scatter_weight(normed_all, grad_values)
        grad_normed = collect_rows(
            lambda b: contract(row_block(grad_pre_query, b), full_query, 1, 1)
            + contract(row_block(grad_keys, b), full_key, 1, 1)
            + contract(row_block(grad_values, b), full_value, 1, 1)
        )
        first_norm, first_pull = jax.vjp(layer_norm, inputs, gain1, shift1)
        grad_input_norm, grad_gain1, grad_shift1 = first_pull(grad_normed)
        grad_tokens = grad_hidden + grad_input_norm

        def vector_sums(feature_rows, head_rows):
            features = to_absolute(jnp.stack(feature_rows))
            lines = features.shape[0]
            joined = jnp.concatenate([features.reshape(-1, 128)] + [v.reshape(-1, 128) for v in head_rows])
            cut = lines * depth // 128
            for mask in plane + [top]:
                joined = joined + swap(joined, mask)
            tail = joined[cut:]
            sizes = [v.shape[0] // 128 for v in head_rows]
            pieces = []
            offset = 0
            for size in sizes:
                pieces.append(tail[offset : offset + size])
                offset += size
            for mask in middle[::-1]:
                kept = []
                for piece in pieces:
                    size = piece.shape[0] // 2
                    kept.append(piece[:size] + swap(piece[size:], mask))
                pieces = kept
            tail = jnp.concatenate(pieces)
            features = joined[:cut]
            both = jnp.concatenate([features, tail])
            came = swap(both, mate)
            features = features + came[:cut]
            tail = jnp.where(alike, tail, came[cut:])
            for mask in middle + [low]:
                features = features + swap(features, mask)
            outs = []
            offset = 0
            for piece in pieces:
                outs.append(tail[offset : offset + piece.shape[0]].reshape(-1))
                offset += piece.shape[0]
            return features.reshape(lines, depth), outs

        squares_row = jnp.full((depth,), squares, jnp.float32)
        early, (grad_b_up,) = vector_sums(
            [
                grad_gain2,
                grad_shift2,
                jnp.sum(grad_hidden, axis=0),
                jnp.sum(grad_output, axis=0),
                squares_row,
            ],
            [jnp.sum(grad_pre_all.astype(jnp.float32), axis=0)],
        )
        late, (grad_b_query, grad_b_value) = vector_sums(
            [grad_gain1, grad_shift1],
            [
                jnp.sum(grad_pre_query.astype(jnp.float32), axis=0),
                jnp.sum(grad_values.astype(jnp.float32), axis=0),
            ],
        )
        mean_loss = early[4, 0] / (valid_count * depth)
        return (
            to_absolute(narrow(output)),
            mean_loss,
            to_absolute(grad_tokens),
            late[0],
            late[1],
            grad_w_query,
            grad_b_query,
            grad_w_key,
            grad_w_value,
            grad_b_value,
            grad_w_out,
            early[2],
            early[0],
            early[1],
            grad_w_up,
            grad_b_up,
            grad_w_down,
            early[3],
        )

    return body


def solution(mesh):
    placed = (
        P(("fsdp", "tp"), None),
        P(),
        P(),
        P("fsdp", "tp"),
        P("tp"),
        P("fsdp", "tp"),
        P("fsdp", "tp"),
        P("tp"),
        P("fsdp", "tp"),
        P(),
        P(),
        P(),
        P("fsdp", "tp"),
        P("tp"),
        P("fsdp", "tp"),
        P(),
        P(("fsdp", "tp"), None),
        P(("fsdp", "tp")),
        P("fsdp", None),
        P("fsdp", None, None),
    )
    return jax.shard_map(
        make_body(mesh.shape["fsdp"], mesh.shape["tp"]),
        mesh=mesh,
        in_specs=placed,
        out_specs=(
            P(("fsdp", "tp"), None),
            P(),
            P(("fsdp", "tp"), None),
            P(),
            P(),
            P("fsdp", "tp"),
            P("tp"),
            P("fsdp", "tp"),
            P("fsdp", "tp"),
            P("tp"),
            P("fsdp", "tp"),
            P(),
            P(),
            P(),
            P("fsdp", "tp"),
            P("tp"),
            P("fsdp", "tp"),
            P(),
        ),
        check_vma=False,
    )
```

time: 1350 us -> 993 us (0.74)
  waiting for transfers between devices: 883 us -> 420 us
  starting transfers between devices: 1.06 us -> 277 us
  blocking collectives: 87.6 us -> 0 us
  matrix products: 225 us -> 147 us
  Pallas kernels: 0 us -> 29.2 us
  other arithmetic: 83.4 us -> 58.2 us
  local copies, waits for them, and re-layouts: 33.8 us -> 49.3 us
    all_gather x10 -> x0, waiting for transfers between devices: 461 us -> none  [the longest x1 82.9 us: body(): normed_all = lax.all_gather(normed, 'tp', axis=0, tiled=True)]
    ppermute x0 -> x114, waiting for transfers between devices: none -> 420 us  [the longest x84 321 us: swap(): lax.ppermute(values, ('fsdp', 'tp'), [(i, i ^ mask) for i in range(world)])]
    reduce_scatter x10 -> x0, waiting for transfers between devices: 418 us -> none  [the longest x8 418 us: scatter_narrow(): lax.psum_scatter(partial_sums.astype(jnp.bfloat16), axis, scatter_dimensi...]
    ppermute x0 -> x114, starting transfers between devices: none -> 277 us  [the longest x84 175 us: swap(): lax.ppermute(values, ('fsdp', 'tp'), [(i, i ^ mask) for i in range(world)])]
    dot_general x24 -> x2, matrix products: 129 us -> 0.42 us  [body(): closure = jnp.einsum('tij,tjk->tik', closure, closure)]
    psum x2 -> x0, blocking collectives: 87.6 us -> none  [body(): lax.psum((jnp.sum(weight_mask), jnp.sum(weight_mask[:, None] * deviation...]
    dot_general x12 -> x60, matrix products: 96 us -> 146 us  [contract(): lax.dot_general(left_side, right_side, (((left_dim,), (right_dim,)), ((),...]
    convert_element_type x14 -> x12, other arithmetic: 47.7 us -> 7.52 us  [the longest x10 7.51 us: narrow(): return values.astype(jnp.bfloat16)]
  transfers between devices with their start and end apart: 20 -> 114, of which waited for: 17 -> 47; matrix products, arithmetic and copies ran while one was open for 19% -> 22% of each run, Pallas kernels for 0% -> 1%
where the time goes in v2:
time: 993 us; the launch traced here: 988 us
  waiting for transfers between devices  420 us (42%)
  starting transfers between devices  277 us (28%)
  matrix products  147 us (15%)
  other arithmetic  58.2 us (6%)
  local copies, waits for them, and re-layouts  49.3 us (5%)
  Pallas kernels  29.2 us (3%)
    ppermute x84, waiting for transfers between devices, swap(): lax.ppermute(values, ('fsdp', 'tp'), [(i, i ^ mask) for i in range(world)])  321 us
    ppermute x84, starting transfers between devices, swap(): lax.ppermute(values, ('fsdp', 'tp'), [(i, i ^ mask) for i in range(world)])  175 us
    dot_general x60, matrix products, contract(): lax.dot_general(left_side, right_side, (((left_dim,), (right_dim,)), ((),...  146 us
    ppermute x30, starting transfers between devices, send(): return lax.ppermute(values, ('fsdp', 'tp'), pairs)  103 us
    ppermute x30, waiting for transfers between devices, send(): return lax.ppermute(values, ('fsdp', 'tp'), pairs)  98.7 us
    unnamed x256, local copies, waits for them, and re-layouts  35 us
    pallas_call x2, Pallas kernels, attend(): pl.pallas_call(lambda *refs: kernel(rows, seg, *refs), grid=(width // PAI...  29.2 us
  transfers between devices with their start and end apart: 114, of which 47 were waited for; matrix products, arithmetic and copies ran while one was open for 22% of the time, Pallas kernels for 1%

profile of v2, /device:TPU:0, one launch (start us, length us, event | category | flops | bytes accessed | tf_op | source)
XLA Modules:
  0.0 987.5 jit_solution(15264648618109313101)
XLA Ops:
  6.7 8.5 collective-permute-start.3
  38.1 21.3 %collective-permute-start.32 = (bf16[256,2048]{1,0:T(8,128)(2,1)S(1)}, bf16[256,2048]{1,0:T(8,128)(2,1)}, u32[]{:S(2)}, u32[]{:S(2)}) collective-permute-start(bf16[256,2048]{1,0:T(8,128)(2,1)S(1)} %copy-done.15), channel_id=1, source_target_pairs={{0,2},{1,3},{6,4},{7,5},{8,10},{9,11},{14,12},{15,13},{16,18},{17,... | collective-permute-start | bytes 3145736 | tf_op jit(solution)/shard_map/ppermute | solution.py:156
  59.4 20.0 %collective-permute-start.10 = (f32[2,512]{1,0:T(2,128)S(1)}, f32[2,512]{1,0:T(2,128)S(1)}, u32[]{:S(2)}, u32[]{:S(2)}) collective-permute-start(f32[2,512]{1,0:T(2,128)S(1)} %pad_maximum_fusion.19), channel_id=1, source_target_pairs={{0,2},{1,3},{2,0},{3,1},{4,6},{5,7},{6,4},{7,5},{8,10},{9,11},{10,... | collective-permute-start | bytes 12296 | tf_op jit(solution)/shard_map/ppermute | solution.py:149
  84.5 18.0 %collective-permute-done.10 = f32[2,512]{1,0:T(2,128)S(1)} collective-permute-done((f32[2,512]{1,0:T(2,128)S(1)}, f32[2,512]{1,0:T(2,128)S(1)}, u32[]{:S(2)}, u32[]{:S(2)}) %collective-permute-start.10) | collective-permute-done | bytes 4128 | tf_op jit(solution)/shard_map/ppermute | solution.py:149
  107.5 10.5 %collective-permute-done.14 = bf16[256,1024]{0,1:T(8,128)(2,1)} collective-permute-done((bf16[256,1024]{0,1:T(8,128)(2,1)}, bf16[256,1024]{0,1:T(8,128)(2,1)}, u32[]{:S(2)}, u32[]{:S(2)}) %collective-permute-start.14) | collective-permute-done | bytes 524320 | tf_op jit(solution)/shard_map/ppermute | solution.py:149
  134.5 13.8 %collective-permute-done.24 = bf16[256,2048]{1,0:T(8,128)(2,1)S(1)} collective-permute-done((bf16[256,2048]{1,0:T(8,128)(2,1)}, bf16[256,2048]{1,0:T(8,128)(2,1)S(1)}, u32[]{:S(2)}, u32[]{:S(2)}) %collective-permute-start.24) | collective-permute-done | bytes 1048608 | tf_op jit(solution)/shard_map/ppermute | solution.py:156
  154.6 17.2 %collective-permute-done.1 = bf16[256,2048]{1,0:T(8,128)(2,1)S(1)} collective-permute-done((bf16[256,2048]{1,0:T(8,128)(2,1)S(1)}, bf16[256,2048]{1,0:T(8,128)(2,1)S(1)}, u32[]{:S(2)}, u32[]{:S(2)}) %collective-permute-start.1) | collective-permute-done | bytes 1048608 | tf_op jit(solution)/shard_map/ppermute | solution.py:149
  202.0 18.5 %collective-permute-done.17 = bf16[512,1024]{0,1:T(8,128)(2,1)S(1)} collective-permute-done((bf16[512,1024]{0,1:T(8,128)(2,1)S(1)}, bf16[512,1024]{0,1:T(8,128)(2,1)S(1)}, u32[]{:S(2)}, u32[]{:S(2)}) %collective-permute-start.17) | collective-permute-done | bytes 1048608 | tf_op jit(solution)/shard_map/ppermute | solution.py:149
  228.3 18.8 %collective-permute-start.19 = (bf16[2,48,1024]{2,1,0:T(8,128)(2,1)S(1)}, bf16[2,48,1024]{2,1,0:T(8,128)(2,1)S(1)}, u32[]{:S(2)}, u32[]{:S(2)}) collective-permute-start(bf16[2,48,1024]{2,1,0:T(8,128)(2,1)S(1)} %bitcast.165), channel_id=1, source_target_pairs={{0,2},{1,3},{2,0},{3,1},{4,6},{5,7},{6,4},{7,5},{8,10},{9,11},{10,... | collective-permute-start | bytes 589832 | tf_op jit(solution)/shard_map/ppermute | solution.py:149
  255.8 8.7 attend_forward.1
  291.0 26.5 %collective-permute-start.22 = (bf16[256,2048]{1,0:T(8,128)(2,1)S(1)}, bf16[256,2048]{1,0:T(8,128)(2,1)S(1)}, u32[]{:S(2)}, u32[]{:S(2)}) collective-permute-start(bf16[256,2048]{1,0:T(8,128)(2,1)S(1)} %fusion.15), channel_id=1, source_target_pairs={{0,1},{1,0},{2,3},{3,2},{4,5},{5,4},{6,7},{7,6},{8,9},{9,8},{10,11... | collective-permute-start | bytes 3145736 | tf_op jit(solution)/shard_map/ppermute | solution.py:149
  319.3 8.4 collective-permute-done.29
  330.0 10.6 %collective-permute-done.22 = bf16[256,2048]{1,0:T(8,128)(2,1)S(1)} collective-permute-done((bf16[256,2048]{1,0:T(8,128)(2,1)S(1)}, bf16[256,2048]{1,0:T(8,128)(2,1)S(1)}, u32[]{:S(2)}, u32[]{:S(2)}) %collective-permute-start.22) | collective-permute-done | bytes 1048608 | tf_op jit(solution)/shard_map/ppermute | solution.py:149
  342.7 15.7 %collective-permute-start.40 = (bf16[256,2048]{1,0:T(8,128)(2,1)S(1)}, bf16[256,2048]{1,0:T(8,128)(2,1)S(1)}, u32[]{:S(2)}, u32[]{:S(2)}) collective-permute-start(bf16[256,2048]{1,0:T(8,128)(2,1)S(1)} %add_convert_fusion.2), channel_id=1, source_target_pairs={{0,1},{1,0},{2,3},{3,2},{4,5},{5,4},{6,7},{7,6},{8,9},{9,8},{10,11... | collective-permute-start | bytes 3145736 | tf_op jit(solution)/shard_map/ppermute | solution.py:149
  361.3 19.6 %collective-permute-done.31 = f32[1,2048]{1,0:T(1,128)S(1)} collective-permute-done((f32[1,2048]{1,0:T(1,128)S(1)}, f32[1,2048]{1,0:T(1,128)S(1)}, u32[]{:S(2)}, u32[]{:S(2)}) %collective-permute-start.31) | collective-permute-done | bytes 8224 | tf_op jit(solution)/shard_map/ppermute | solution.py:149
  383.4 17.0 %collective-permute-done.30 = bf16[512,2048]{1,0:T(8,128)(2,1)S(1)} collective-permute-done((bf16[512,2048]{1,0:T(8,128)(2,1)S(1)}, bf16[512,2048]{1,0:T(8,128)(2,1)S(1)}, u32[]{:S(2)}, u32[]{:S(2)}) %collective-permute-start.30) | collective-permute-done | bytes 2097184 | tf_op jit(solution)/shard_map/ppermute | solution.py:149
  402.1 9.3 maximum_convert_fusion
  413.7 10.7 %collective-permute-start.42 = (bf16[256,2048]{1,0:T(8,128)(2,1)S(1)}, bf16[256,2048]{1,0:T(8,128)(2,1)S(1)}, u32[]{:S(2)}, u32[]{:S(2)}) collective-permute-start(bf16[256,2048]{1,0:T(8,128)(2,1)S(1)} %convolution_convert_fusion.8), channel_id=1, source_target_pairs={{0,4},{1,5},{2,6},{3,7},{4,0},{5,1},{6,2},{7,3},{8,12},{9,13},{10,... | collective-permute-start | bytes 3145736 | tf_op jit(solution)/shard_map/ppermute | solution.py:149
  424.5 9.0 maximum_convert_fusion.1
  438.4 14.3 %collective-permute-start.43 = (bf16[256,2048]{1,0:T(8,128)(2,1)S(1)}, bf16[256,2048]{1,0:T(8,128)(2,1)S(1)}, u32[]{:S(2)}, u32[]{:S(2)}) collective-permute-start(bf16[256,2048]{1,0:T(8,128)(2,1)S(1)} %fusion.13), channel_id=1, source_target_pairs={{0,1},{1,0},{2,3},{3,2},{4,5},{5,4},{6,7},{7,6},{8,9},{9,8},{10,11... | collective-permute-start | bytes 3145736 | tf_op jit(solution)/shard_map/ppermute | solution.py:149
  453.5 21.9 %collective-permute-done.45 = f32[8,128]{1,0:T(8,128)S(1)} collective-permute-done((f32[8,128]{1,0:T(8,128)S(1)}, f32[8,128]{1,0:T(8,128)S(1)}, u32[]{:S(2)}, u32[]{:S(2)}) %collective-permute-start.45) | collective-permute-done | bytes 4128 | tf_op jit(solution)/shard_map/ppermute | solution.py:149
  496.3 17.4 %collective-permute-done.51 = bf16[256,2048]{1,0:T(8,128)(2,1)} collective-permute-done((bf16[256,2048]{1,0:T(8,128)(2,1)}, bf16[256,2048]{1,0:T(8,128)(2,1)}, u32[]{:S(2)}, u32[]{:S(2)}) %collective-permute-start.51) | collective-permute-done | bytes 1048608 | tf_op jit(solution)/shard_map/ppermute | solution.py:149
  513.7 8.6 select_convert_fusion.1
  570.8 27.4 %collective-permute-done.100 = bf16[512,2048]{1,0:T(8,128)(2,1)S(1)} collective-permute-done((bf16[512,2048]{1,0:T(8,128)(2,1)S(1)}, bf16[512,2048]{1,0:T(8,128)(2,1)S(1)}, u32[]{:S(2)}, u32[]{:S(2)}) %collective-permute-start.100) | collective-permute-done | bytes 2097184 | tf_op jit(solution)/shard_map/ppermute | solution.py:149
  611.9 30.8 %collective-permute-done.107 = bf16[512,2048]{1,0:T(8,128)(2,1)} collective-permute-done((bf16[512,2048]{1,0:T(8,128)(2,1)}, bf16[512,2048]{1,0:T(8,128)(2,1)}, u32[]{:S(2)}, u32[]{:S(2)}) %collective-permute-start.107) | collective-permute-done | bytes 2097184 | tf_op jit(solution)/shard_map/ppermute | solution.py:149
  678.9 8.9 collective-permute-done.108
  693.1 8.9 collective-permute-done.61
  704.9 44.8 %collective-permute-done.105 = bf16[256,2048]{1,0:T(8,128)(2,1)S(1)} collective-permute-done((bf16[256,2048]{1,0:T(8,128)(2,1)S(1)}, bf16[256,2048]{1,0:T(8,128)(2,1)S(1)}, u32[]{:S(2)}, u32[]{:S(2)}) %collective-permute-start.105) | collective-permute-done | bytes 1048608 | tf_op jit(solution)/shard_map/ppermute | solution.py:156
  752.2 20.0 %collective-permute-done.112 = bf16[256,2048]{1,0:T(8,128)(2,1)S(1)} collective-permute-done((bf16[256,2048]{1,0:T(8,128)(2,1)S(1)}, bf16[256,2048]{1,0:T(8,128)(2,1)S(1)}, u32[]{:S(2)}, u32[]{:S(2)}) %collective-permute-start.112) | collective-permute-done | bytes 1048608 | tf_op jit(solution)/shard_map/ppermute | solution.py:156
  779.5 20.5 %attend_backward.1 = (bf16[1024,512]{1,0:T(8,128)(2,1)}, bf16[1024,512]{1,0:T(8,128)(2,1)}, bf16[1024,512]{1,0:T(8,128)(2,1)}, f32[2,128,512]{2,1,0:T(8,128)}, f32[2,128,512]{2,1,0:T(8,128)}) custom-call(bf16[1024,512]{1,0:T(8,128)(2,1)} %multiply_convert_fusion.refs_0_, bf16[1024,512]{1,0:T(8,128)(2,1)} %copy-done.11, bf16[1024,512]{1,0:T(8,128)(2,1)} %copy-done.10, ...), custom_call_target="tpu_custom_call" | custom-call | tf_op jit(solution)/shard_map/attend_backward/pallas_call | solution.py:127
  836.5 9.3 collective-permute-done.79
  916.9 17.1 %collective-permute-start.90 = (bf16[256,512]{1,0:T(8,128)(2,1)S(1)}, bf16[256,512]{1,0:T(8,128)(2,1)S(1)}, u32[]{:S(2)}, u32[]{:S(2)}) collective-permute-start(bf16[256,512]{1,0:T(8,128)(2,1)S(1)} %get-tuple-element.68), channel_id=1, source_target_pairs={{0,4},{1,5},{6,2},{7,3},{8,12},{9,13},{14,10},{15,11},{16,20},{17,... | collective-permute-start | bytes 786440 | tf_op jit(solution)/shard_map/ppermute | solution.py:156
  (666 shorter events, 448.3 us)
Async XLA Ops:
  26.6 52.8 %collective-permute-start.11 = (bf16[256,1024]{0,1:T(8,128)(2,1)}, bf16[256,1024]{0,1:T(8,128)(2,1)}, u32[]{:S(2)}, u32[]{:S(2)}) collective-permute-start(bf16[256,1024]{0,1:T(8,128)(2,1)} %pad_maximum_fusion.15), channel_id=1, source_target_pairs={{0,2},{1,3},{6,4},{7,5},{8,10},{9,11},{14,12},{15,13},{16,18},{17,... | collective-permute-start | bytes 1572872 | tf_op jit(solution)/shard_map/ppermute | solution.py:156
  32.8 85.9 %collective-permute-start.33 = (bf16[256,2048]{1,0:T(8,128)(2,1)S(1)}, bf16[256,2048]{1,0:T(8,128)(2,1)}, u32[]{:S(2)}, u32[]{:S(2)}) collective-permute-start(bf16[256,2048]{1,0:T(8,128)(2,1)S(1)} %copy-done.15), channel_id=1, source_target_pairs={{2,6},{3,7},{4,0},{5,1},{10,14},{11,15},{12,8},{13,9},{18,22},{19,... | collective-permute-start | bytes 3145736 | tf_op jit(solution)/shard_map/ppermute | solution.py:156
  34.1 91.9 %collective-permute-start.34 = (bf16[256,2048]{1,0:T(8,128)(2,1)S(1)}, bf16[256,2048]{1,0:T(8,128)(2,1)}, u32[]{:S(2)}, u32[]{:S(2)}) collective-permute-start(bf16[256,2048]{1,0:T(8,128)(2,1)S(1)} %copy-done.15), channel_id=1, source_target_pairs={{2,4},{3,5},{4,2},{5,3},{10,12},{11,13},{12,10},{13,11},{18,20},{1... | collective-permute-start | bytes 3145736 | tf_op jit(solution)/shard_map/ppermute | solution.py:156
  38.1 89.7 %collective-permute-start.32 = (bf16[256,2048]{1,0:T(8,128)(2,1)S(1)}, bf16[256,2048]{1,0:T(8,128)(2,1)}, u32[]{:S(2)}, u32[]{:S(2)}) collective-permute-start(bf16[256,2048]{1,0:T(8,128)(2,1)S(1)} %copy-done.15), channel_id=1, source_target_pairs={{0,2},{1,3},{6,4},{7,5},{8,10},{9,11},{14,12},{15,13},{16,18},{17,... | collective-permute-start | bytes 3145736 | tf_op jit(solution)/shard_map/ppermute | solution.py:156
  126.1 45.7 %collective-permute-start.1 = (bf16[256,2048]{1,0:T(8,128)(2,1)S(1)}, bf16[256,2048]{1,0:T(8,128)(2,1)S(1)}, u32[]{:S(2)}, u32[]{:S(2)}) collective-permute-start(bf16[256,2048]{1,0:T(8,128)(2,1)S(1)} %copy-done.25), channel_id=1, source_target_pairs={{0,1},{1,0},{2,3},{3,2},{4,5},{5,4},{6,7},{7,6},{8,9},{9,8},{10,11... | collective-permute-start | bytes 3145736 | tf_op jit(solution)/shard_map/ppermute | solution.py:149
  127.8 46.3 %collective-permute-start.15 = (bf16[512,1024]{0,1:T(8,128)(2,1)S(1)}, bf16[512,1024]{0,1:T(8,128)(2,1)S(1)}, u32[]{:S(2)}, u32[]{:S(2)}) collective-permute-start(bf16[512,1024]{0,1:T(8,128)(2,1)S(1)} %pad_maximum_fusion.12), channel_id=1, source_target_pairs={{0,16},{1,17},{2,18},{3,19},{4,20},{5,21},{6,22},{7,23},{8,24},{9,... | collective-permute-start | bytes 3145736 | tf_op jit(solution)/shard_map/ppermute | solution.py:149
  133.8 88.9 %collective-permute-start = (bf16[256,2048]{1,0:T(8,128)(2,1)S(1)}, bf16[256,2048]{1,0:T(8,128)(2,1)S(1)}, u32[]{:S(2)}, u32[]{:S(2)}) collective-permute-start(bf16[256,2048]{1,0:T(8,128)(2,1)S(1)} %copy-done.25), channel_id=1, source_target_pairs={{0,4},{1,5},{2,6},{3,7},{4,0},{5,1},{6,2},{7,3},{8,12},{9,13},{10,... | collective-permute-start | bytes 3145736 | tf_op jit(solution)/shard_map/ppermute | solution.py:149
  174.1 48.7 %collective-permute-start.2 = (bf16[256,2048]{1,0:T(8,128)(2,1)S(1)}, bf16[256,2048]{1,0:T(8,128)(2,1)S(1)}, u32[]{:S(2)}, u32[]{:S(2)}) collective-permute-start(bf16[256,2048]{1,0:T(8,128)(2,1)S(1)} %collective-permute-done.1), channel_id=1, source_target_pairs={{0,4},{1,5},{2,6},{3,7},{4,0},{5,1},{6,2},{7,3},{8,12},{9,13},{10,... | collective-permute-start | bytes 3145736 | tf_op jit(solution)/shard_map/ppermute | solution.py:149
  198.1 72.3 %collective-permute-start.36 = (bf16[512,2048]{1,0:T(8,128)(2,1)}, bf16[512,2048]{1,0:T(8,128)(2,1)}, u32[]{:S(2)}, u32[]{:S(2)}) collective-permute-start(bf16[512,2048]{1,0:T(8,128)(2,1)} %pad_maximum_fusion.8), channel_id=1, source_target_pairs={{0,16},{1,17},{2,18},{3,19},{4,20},{5,21},{6,22},{7,23},{8,24},{9,... | collective-permute-start | bytes 6291464 | tf_op jit(solution)/shard_map/ppermute | solution.py:149
  201.5 81.2 %collective-permute-start.28 = (bf16[512,2048]{1,0:T(8,128)(2,1)S(1)}, bf16[512,2048]{1,0:T(8,128)(2,1)}, u32[]{:S(2)}, u32[]{:S(2)}) collective-permute-start(bf16[512,2048]{1,0:T(8,128)(2,1)S(1)} %pad_maximum_fusion.6), channel_id=1, source_target_pairs={{0,16},{1,17},{2,18},{3,19},{4,20},{5,21},{6,22},{7,23},{8,24},{9,... | collective-permute-start | bytes 6291464 | tf_op jit(solution)/shard_map/ppermute | solution.py:149
  270.4 59.7 %collective-permute-start.20 = (bf16[256,2048]{1,0:T(8,128)(2,1)S(1)}, bf16[256,2048]{1,0:T(8,128)(2,1)S(1)}, u32[]{:S(2)}, u32[]{:S(2)}) collective-permute-start(bf16[256,2048]{1,0:T(8,128)(2,1)S(1)} %convolution_convert_fusion.5), channel_id=1, source_target_pairs={{0,4},{1,5},{2,6},{3,7},{4,0},{5,1},{6,2},{7,3},{8,12},{9,13},{10,... | collective-permute-start | bytes 3145736 | tf_op jit(solution)/shard_map/ppermute | solution.py:149
  291.0 49.6 %collective-permute-start.22 = (bf16[256,2048]{1,0:T(8,128)(2,1)S(1)}, bf16[256,2048]{1,0:T(8,128)(2,1)S(1)}, u32[]{:S(2)}, u32[]{:S(2)}) collective-permute-start(bf16[256,2048]{1,0:T(8,128)(2,1)S(1)} %fusion.15), channel_id=1, source_target_pairs={{0,1},{1,0},{2,3},{3,2},{4,5},{5,4},{6,7},{7,6},{8,9},{9,8},{10,11... | collective-permute-start | bytes 3145736 | tf_op jit(solution)/shard_map/ppermute | solution.py:149
  317.8 65.5 %collective-permute-start.38 = (bf16[512,2048]{1,0:T(8,128)(2,1)S(1)}, bf16[512,2048]{1,0:T(8,128)(2,1)S(1)}, u32[]{:S(2)}, u32[]{:S(2)}) collective-permute-start(bf16[512,2048]{1,0:T(8,128)(2,1)S(1)} %pad_maximum_fusion.9), channel_id=1, source_target_pairs={{0,8},{1,9},{2,10},{3,11},{4,12},{5,13},{6,14},{7,15},{8,0},{9,1},... | collective-permute-start | bytes 6291464 | tf_op jit(solution)/shard_map/ppermute | solution.py:149
  327.9 72.5 %collective-permute-start.30 = (bf16[512,2048]{1,0:T(8,128)(2,1)S(1)}, bf16[512,2048]{1,0:T(8,128)(2,1)S(1)}, u32[]{:S(2)}, u32[]{:S(2)}) collective-permute-start(bf16[512,2048]{1,0:T(8,128)(2,1)S(1)} %pad_maximum_fusion.7), channel_id=1, source_target_pairs={{0,8},{1,9},{2,10},{3,11},{4,12},{5,13},{6,14},{7,15},{8,0},{9,1},... | collective-permute-start | bytes 6291464 | tf_op jit(solution)/shard_map/ppermute | solution.py:149
  359.7 93.0 %collective-permute-start.44 = (f32[8,128]{1,0:T(8,128)S(1)}, f32[8,128]{1,0:T(8,128)S(1)}, u32[]{:S(2)}, u32[]{:S(2)}) collective-permute-start(f32[8,128]{1,0:T(8,128)S(1)} %broadcast_in_dim.47), channel_id=1, source_target_pairs={{0,1},{1,0},{2,3},{3,2},{4,5},{5,4},{6,7},{7,6},{8,9},{9,8},{10,11... | collective-permute-start | bytes 12296 | tf_op jit(solution)/shard_map/ppermute | solution.py:149
  435.9 49.9 %collective-permute-start.39 = (bf16[256,2048]{1,0:T(8,128)(2,1)S(1)}, bf16[256,2048]{1,0:T(8,128)(2,1)S(1)}, u32[]{:S(2)}, u32[]{:S(2)}) collective-permute-start(bf16[256,2048]{1,0:T(8,128)(2,1)S(1)} %convolution_convert_fusion.9), channel_id=1, source_target_pairs={{0,4},{1,5},{2,6},{3,7},{4,0},{5,1},{6,2},{7,3},{8,12},{9,13},{10,... | collective-permute-start | bytes 3145736 | tf_op jit(solution)/shard_map/ppermute | solution.py:149
  438.4 47.4 %collective-permute-start.43 = (bf16[256,2048]{1,0:T(8,128)(2,1)S(1)}, bf16[256,2048]{1,0:T(8,128)(2,1)S(1)}, u32[]{:S(2)}, u32[]{:S(2)}) collective-permute-start(bf16[256,2048]{1,0:T(8,128)(2,1)S(1)} %fusion.13), channel_id=1, source_target_pairs={{0,1},{1,0},{2,3},{3,2},{4,5},{5,4},{6,7},{7,6},{8,9},{9,8},{10,11... | collective-permute-start | bytes 3145736 | tf_op jit(solution)/shard_map/ppermute | solution.py:149
  528.9 125.6 %collective-permute-start.50 = (bf16[256,2048]{1,0:T(8,128)(2,1)S(1)}, bf16[256,2048]{1,0:T(8,128)(2,1)S(1)}, u32[]{:S(2)}, u32[]{:S(2)}) collective-permute-start(bf16[256,2048]{1,0:T(8,128)(2,1)S(1)} %convolution_convert_fusion.7), channel_id=1, source_target_pairs={{0,4},{1,5},{2,6},{3,7},{4,0},{5,1},{6,2},{7,3},{8,12},{9,13},{10,... | collective-permute-start | bytes 3145736 | tf_op jit(solution)/shard_map/ppermute | solution.py:149
  549.6 48.6 %collective-permute-start.100 = (bf16[512,2048]{1,0:T(8,128)(2,1)S(1)}, bf16[512,2048]{1,0:T(8,128)(2,1)S(1)}, u32[]{:S(2)}, u32[]{:S(2)}) collective-permute-start(bf16[512,2048]{1,0:T(8,128)(2,1)S(1)} %convolution_convert_fusion.3), channel_id=1, source_target_pairs={{0,16},{1,17},{2,18},{3,19},{4,20},{5,21},{6,22},{7,23},{8,24},{9,... | collective-permute-start | bytes 6291464 | tf_op jit(solution)/shard_map/ppermute | solution.py:149
  550.1 55.0 %collective-permute-start.102 = (bf16[512,2048]{1,0:T(8,128)(2,1)S(1)}, bf16[512,2048]{1,0:T(8,128)(2,1)}, u32[]{:S(2)}, u32[]{:S(2)}) collective-permute-start(bf16[512,2048]{1,0:T(8,128)(2,1)S(1)} %convolution_convert_fusion.2), channel_id=1, source_target_pairs={{0,8},{1,9},{2,10},{3,11},{4,12},{5,13},{6,14},{7,15},{8,0},{9,1},... | collective-permute-start | bytes 6291464 | tf_op jit(solution)/shard_map/ppermute | solution.py:149
  557.1 85.6 %collective-permute-start.107 = (bf16[512,2048]{1,0:T(8,128)(2,1)}, bf16[512,2048]{1,0:T(8,128)(2,1)}, u32[]{:S(2)}, u32[]{:S(2)}) collective-permute-start(bf16[512,2048]{1,0:T(8,128)(2,1)} %convolution_convert_fusion.1), channel_id=1, source_target_pairs={{0,16},{1,17},{2,18},{3,19},{4,20},{5,21},{6,22},{7,23},{8,24},{9,... | collective-permute-start | bytes 6291464 | tf_op jit(solution)/shard_map/ppermute | solution.py:149
  563.2 85.0 %collective-permute-start.109 = (bf16[512,2048]{1,0:T(8,128)(2,1)}, bf16[512,2048]{1,0:T(8,128)(2,1)}, u32[]{:S(2)}, u32[]{:S(2)}) collective-permute-start(bf16[512,2048]{1,0:T(8,128)(2,1)} %convolution_convert_fusion), channel_id=1, source_target_pairs={{0,8},{1,9},{2,10},{3,11},{4,12},{5,13},{6,14},{7,15},{8,0},{9,1},... | collective-permute-start | bytes 6291464 | tf_op jit(solution)/shard_map/ppermute | solution.py:149
  599.6 56.7 %collective-permute-start.54 = (bf16[256,2048]{1,0:T(8,128)(2,1)}, bf16[256,2048]{1,0:T(8,128)(2,1)}, u32[]{:S(2)}, u32[]{:S(2)}) collective-permute-start(bf16[256,2048]{1,0:T(8,128)(2,1)} %fusion.14), channel_id=1, source_target_pairs={{0,1},{1,0},{2,3},{3,2},{4,5},{5,4},{6,7},{7,6},{8,9},{9,8},{10,11... | collective-permute-start | bytes 3145736 | tf_op jit(solution)/shard_map/ppermute | solution.py:149
  605.1 62.1 %collective-permute-start.101 = (bf16[256,2048]{1,0:T(8,128)(2,1)}, bf16[256,2048]{1,0:T(8,128)(2,1)}, u32[]{:S(2)}, u32[]{:S(2)}) collective-permute-start(bf16[256,2048]{1,0:T(8,128)(2,1)} %slice.770), channel_id=1, source_target_pairs={{0,8},{1,9},{2,10},{3,11},{4,12},{5,13},{6,14},{7,15},{8,0},{9,1},... | collective-permute-start | bytes 3145736 | tf_op jit(solution)/shard_map/ppermute | solution.py:149
  672.2 77.5 %collective-permute-start.104 = (bf16[256,2048]{1,0:T(8,128)(2,1)S(1)}, bf16[256,2048]{1,0:T(8,128)(2,1)S(1)}, u32[]{:S(2)}, u32[]{:S(2)}) collective-permute-start(bf16[256,2048]{1,0:T(8,128)(2,1)S(1)} %get-tuple-element.62), channel_id=1, source_target_pairs={{0,4},{1,5},{6,2},{7,3},{8,12},{9,13},{14,10},{15,11},{16,20},{17,... | collective-permute-start | bytes 3145736 | tf_op jit(solution)/shard_map/ppermute | solution.py:156
  687.8 61.9 %collective-permute-start.105 = (bf16[256,2048]{1,0:T(8,128)(2,1)S(1)}, bf16[256,2048]{1,0:T(8,128)(2,1)S(1)}, u32[]{:S(2)}, u32[]{:S(2)}) collective-permute-start(bf16[256,2048]{1,0:T(8,128)(2,1)S(1)} %get-tuple-element.61), channel_id=1, source_target_pairs={{2,0},{3,1},{4,6},{5,7},{10,8},{11,9},{12,14},{13,15},{18,16},{19,... | collective-permute-start | bytes 3145736 | tf_op jit(solution)/shard_map/ppermute | solution.py:156
  692.4 59.8 %collective-permute-start.113 = (bf16[256,2048]{1,0:T(8,128)(2,1)S(1)}, bf16[256,2048]{1,0:T(8,128)(2,1)S(1)}, u32[]{:S(2)}, u32[]{:S(2)}) collective-permute-start(bf16[256,2048]{1,0:T(8,128)(2,1)S(1)} %get-tuple-element.60), channel_id=1, source_target_pairs={{2,4},{3,5},{4,2},{5,3},{10,12},{11,13},{12,10},{13,11},{18,20},{1... | collective-permute-start | bytes 3145736 | tf_op jit(solution)/shard_map/ppermute | solution.py:156
  702.0 70.1 %collective-permute-start.111 = (bf16[256,2048]{1,0:T(8,128)(2,1)S(1)}, bf16[256,2048]{1,0:T(8,128)(2,1)S(1)}, u32[]{:S(2)}, u32[]{:S(2)}) collective-permute-start(bf16[256,2048]{1,0:T(8,128)(2,1)S(1)} %get-tuple-element.60), channel_id=1, source_target_pairs={{0,4},{1,5},{6,2},{7,3},{8,12},{9,13},{14,10},{15,11},{16,20},{17,... | collective-permute-start | bytes 3145736 | tf_op jit(solution)/shard_map/ppermute | solution.py:156
  703.4 68.8 %collective-permute-start.112 = (bf16[256,2048]{1,0:T(8,128)(2,1)S(1)}, bf16[256,2048]{1,0:T(8,128)(2,1)S(1)}, u32[]{:S(2)}, u32[]{:S(2)}) collective-permute-start(bf16[256,2048]{1,0:T(8,128)(2,1)S(1)} %get-tuple-element.59), channel_id=1, source_target_pairs={{2,0},{3,1},{4,6},{5,7},{10,8},{11,9},{12,14},{13,15},{18,16},{19,... | collective-permute-start | bytes 3145736 | tf_op jit(solution)/shard_map/ppermute | solution.py:156
  825.8 62.1 %collective-permute-start.65 = (bf16[256,2048]{1,0:T(8,128)(2,1)S(1)}, bf16[256,2048]{1,0:T(8,128)(2,1)S(1)}, u32[]{:S(2)}, u32[]{:S(2)}) collective-permute-start(bf16[256,2048]{1,0:T(8,128)(2,1)S(1)} %fusion.18), channel_id=1, source_target_pairs={{0,4},{1,5},{2,6},{3,7},{4,0},{5,1},{6,2},{7,3},{8,12},{9,13},{10,... | collective-permute-start | bytes 3145736 | tf_op jit(solution)/shard_map/ppermute | solution.py:149
  829.5 114.6 %collective-permute-start.64 = (bf16[256,2048]{1,0:T(8,128)(2,1)S(1)}, bf16[256,2048]{1,0:T(8,128)(2,1)S(1)}, u32[]{:S(2)}, u32[]{:S(2)}) collective-permute-start(bf16[256,2048]{1,0:T(8,128)(2,1)S(1)} %fusion.16), channel_id=1, source_target_pairs={{0,4},{1,5},{2,6},{3,7},{4,0},{5,1},{6,2},{7,3},{8,12},{9,13},{10,... | collective-permute-start | bytes 3145736 | tf_op jit(solution)/shard_map/ppermute | solution.py:149
  898.2 45.9 %collective-permute-start.66 = (bf16[256,2048]{1,0:T(8,128)(2,1)S(1)}, bf16[256,2048]{1,0:T(8,128)(2,1)S(1)}, u32[]{:S(2)}, u32[]{:S(2)}) collective-permute-start(bf16[256,2048]{1,0:T(8,128)(2,1)S(1)} %fusion.17), channel_id=1, source_target_pairs={{0,1},{1,0},{2,3},{3,2},{4,5},{5,4},{6,7},{7,6},{8,9},{9,8},{10,11... | collective-permute-start | bytes 3145736 | tf_op jit(solution)/shard_map/ppermute | solution.py:149
  (182 other events, 3675.7 us)

commit v3 on v2

--- a/solution.py
+++ b/solution.py
@@ -30,6 +30,10 @@
 
 def narrow(values):
     return values.astype(jnp.bfloat16)
+
+
+def after(values, *needed):
+    return lax.optimization_barrier((values, needed))[0]
 
 
 def bits_below(count, first):
@@ -133,6 +137,7 @@
         out_specs=[column_block] * outputs + [sum_block] * sums,
         out_shape=[jax.ShapeDtypeStruct((count, width), jnp.bfloat16)] * outputs
         + [jax.ShapeDtypeStruct((2, KEY_PAD, width), jnp.float32)] * sums,
+        cost_estimate=pl.CostEstimate(flops=1, bytes_accessed=1, transcendentals=0),
         name="attend_forward" if sums == 0 else "attend_backward",
     )(*operands, *key_sums, seen)
 
@@ -148,15 +153,8 @@
     def swap(values, mask):
         return lax.ppermute(values, ("fsdp", "tp"), [(i, i ^ mask) for i in range(world)])
 
-    def agrees(i):
-        return (i // tp) % 2 == (i % tp) // top
-
-    def send(values, mask, alike):
-        pairs = [(i, i ^ mask) for i in range(world) if agrees(i) == alike]
-        return lax.ppermute(values, ("fsdp", "tp"), pairs)
-
     def everyone(values):
-        for mask in bits_below(world, 1):
+        for mask in bits_below(world, tp) + bits_below(tp, 1):
             values = values + swap(values, mask)
         return values
 
@@ -226,48 +224,90 @@
                     parts.append(lax.dynamic_slice_in_dim(values, start, strip, values.ndim - 1))
             return jnp.concatenate(parts, axis=-1)
 
-        def gather_weight(shard):
-            near = send(shard, mate, False)
-            far_same = send(shard, top, True)
-            far_other = send(shard, mate | top, False)
-            same = jnp.where(alike, shard, far_same)
-            other = jnp.where(alike, near, far_other)
+        lane = []
+        gate = []
+        sent = []
+
+        def ship(items):
+            values = after([value for value, _ in items], lane[-2:-1], gate)
+            sent.append(values)
+            got = [swap(value, mask) for value, (_, mask) in zip(values, items)]
+            lane.append(got)
+            return got
+
+        orders = (plane, plane[::-1])
+        slices = tp // 4
+
+        def bring_weight(shard, across):
+            mine = jnp.where(alike, shard, across)
+            came = swap(jnp.where(alike, across, shard), mate)
             for mask in middle:
-                same = jnp.concatenate([same, swap(same, mask)], axis=1)
-                other = jnp.concatenate([other, swap(other, mask)], axis=1)
-            pieces = []
-            for side, order in enumerate((plane, plane[::-1])):
-                held = [jnp.where(core == side, same, other)]
-                for mask in order:
-                    now = held[0] if len(held) == 1 else jnp.concatenate(held, axis=0)
-                    held.append(swap(now, mask))
-                pieces += held
-            return jnp.concatenate(pieces, axis=0)
-
-        def scatter_weight(left, right):
-            outs = []
-            firsts = []
-            for side, order in enumerate((plane, plane[::-1])):
-                base = side * half
-                away = narrow(contract(left[:, base + half // 2 : base + half], right, 0, 0))
-                firsts.append((base, order, swap(away, order[-1])))
-            for base, order, came in firsts:
-                kept = contract(left[:, base : base + half // 2], right, 0, 0) + came
-                for mask in order[-2::-1]:
-                    size = kept.shape[0] // 2
-                    kept = kept[:size] + swap(narrow(kept[size:]), mask)
-                outs.append(kept)
-            same = narrow(jnp.where(core == 0, outs[0], outs[1]))
-            other = narrow(jnp.where(core == 0, outs[1], outs[0]))
+                mine = jnp.concatenate([mine, swap(mine, mask)], axis=1)
+                came = jnp.concatenate([came, swap(came, mask)], axis=1)
+            return [jnp.where(core == side, mine, came) for side in range(2)]
+
+        def run(stages, *needed):
+            gate[:] = needed
+            next(stages, None)
+            gate.clear()
+
+        def finish(stages, *needed):
+            gate[:] = needed
+            for _ in stages:
+                pass
+            gate.clear()
+
+        def gather_weight(both, full):
+            sides = [[both[0]], [both[1]]]
+            for level in range(len(plane)):
+                held = [
+                    pieces[0] if level == 0 else jnp.concatenate(pieces, axis=0) for pieces in sides
+                ]
+                got = ship([(held[side], orders[side][level]) for side in range(2)])
+                yield
+                got = after(got, gate)
+                for side in range(2):
+                    sides[side].append(got[side])
+            full.append(jnp.concatenate(sides[0] + sides[1], axis=0))
+
+        def scatter_weight(pairs, total, *ahead):
+            def rows_of(start, stop, needed):
+                parts = [
+                    contract(after(left, needed)[:, start:stop], right, 0, 0) for left, right in pairs
+                ]
+                if len(parts) == 1:
+                    return parts[0]
+                parts = [part.reshape(stop - start, slices, -1) for part in parts]
+                return jnp.concatenate(parts, axis=2).reshape(stop - start, -1)
+
+            sums = []
+            for level in reversed(range(len(plane))):
+                size = half >> (len(plane) - level)
+                if sums:
+                    away = [narrow(sums[side][size:]) for side in range(2)]
+                else:
+                    away = [narrow(rows_of(side * half + size, (side + 1) * half, ahead)) for side in range(2)]
+                got = ship([(away[side], orders[side][level]) for side in range(2)])
+                yield
+                got = after(got, gate)
+                if sums:
+                    sums = [sums[side][:size] + got[side] for side in range(2)]
+                else:
+                    sums = [rows_of(side * half, side * half + size, away) + got[side] for side in range(2)]
+            kept = [narrow(sums[side]) for side in range(2)]
+            mine = jnp.where(core == 0, kept[0], kept[1])
+            other = jnp.where(core == 0, kept[1], kept[0])
             for mask in middle[::-1]:
-                size = same.shape[1] // 2
-                same = narrow(same[:, :size].astype(jnp.float32) + swap(same[:, size:], mask))
-                other = narrow(other[:, :size].astype(jnp.float32) + swap(other[:, size:], mask))
-            near = send(other, mate, True)
-            far_same = send(same, top, False)
-            far_other = send(other, mate | top, False)
-            own = jnp.where(alike, same, jnp.zeros_like(same)).astype(jnp.float32)
-            return own + near + far_same + far_other
+                width = mine.shape[1] // 2
+                mine = narrow(mine[:, :width].astype(jnp.float32) + swap(mine[:, width:], mask))
+                other = narrow(other[:, :width].astype(jnp.float32) + swap(other[:, width:], mask))
+            came = swap(other, mate)
+            give = jnp.where(alike, came, mine)
+            keep = jnp.where(alike, mine, came)
+            given.append(give)
+            total.append(keep.astype(jnp.float32) + swap(give, top))
+
+        given = []
 
         def gather_bias(part):
             part = jnp.where(alike, part, swap(part, top))
@@ -281,11 +321,18 @@
             far = jnp.concatenate([across, swap(across, mate)], axis=0)
             return near, far
 
-        def collect_rows(partial):
-            far_mate = swap(narrow(partial(3)), mate)
-            crossing = swap(narrow(partial(2) + far_mate), low)
-            near_mate = swap(narrow(partial(1)), mate)
-            return partial(0) + near_mate + crossing
+        def start_collect(values, partial):
+            far_mate = swap(narrow(partial(row_block(values, 3))), mate)
+            leaving = narrow(partial(row_block(values, 2)) + far_mate)
+            crossing = swap(leaving, low)
+            values = after(values, leaving)
+            near_mate = swap(narrow(partial(row_block(values, 1))), mate)
+            own = partial(row_block(values, 0))
+
+            def complete(*needed):
+                return own + near_mate + after(crossing, needed)
+
+            return leaving, complete
 
         def row_block(values, block):
             return values[block * rows : (block + 1) * rows]
@@ -300,11 +347,39 @@
         counted = everyone(jnp.full((8, 128), jnp.sum(weight_mask), jnp.float32))
         valid_count = counted[0, 0]
 
-        slices = tp // 4
-        w_kv = gather_weight(jnp.concatenate([w_key, w_value], axis=1))
-        w_qo = gather_weight(jnp.concatenate([w_query, w_out], axis=1))
-        full_up = gather_weight(w_up)
-        full_down = gather_weight(w_down)
+        shards = [
+            jnp.concatenate([w_key, w_value], axis=1),
+            jnp.concatenate([w_query, w_out], axis=1),
+            w_up,
+            w_down,
+        ]
+        crossed = []
+
+        gathered = [[], [], [], []]
+
+        leaving_shards = []
+
+        def cross(which, *needed):
+            leaving_shards.append(after(shards[which], needed))
+            crossed.append(swap(leaving_shards[-1], top))
+
+        def fetch(which, *needed):
+            across = after(crossed[which], needed)
+            return gather_weight(bring_weight(shards[which], across), gathered[which])
+
+        cross(0)
+        kv_stages = fetch(0)
+        run(kv_stages)
+        cross(1, crossed[0])
+        run(kv_stages)
+        cross(2, lane[0])
+        qo_stages = fetch(1, sent[-1])
+        run(qo_stages)
+        finish(kv_stages)
+        finish(qo_stages)
+        up_stages = fetch(2, lane[-1])
+        run(up_stages)
+        w_kv, w_qo = gathered[0][0], gathered[1][0]
 
         def split_two(joined):
             parts = joined.reshape(joined.shape[0], slices, 2, -1)
@@ -312,9 +387,11 @@
 
         full_key, full_value = split_two(w_kv)
         full_query, full_out = split_two(w_qo)
-        head_bias = gather_bias(jnp.stack([b_query, b_value]))
-        bias_query, bias_value = head_bias[0], head_bias[1]
-        bias_up = gather_bias(b_up[None])[0]
+        bias = gather_bias(jnp.concatenate([b_query, b_value, b_up])[None]).reshape(slices, -1)
+        heads = b_query.shape[0]
+        bias_query = bias[:, :heads].reshape(-1)
+        bias_value = bias[:, heads : 2 * heads].reshape(-1)
+        bias_up = bias[:, 2 * heads :].reshape(-1)
 
         tables = jnp.concatenate([parents[0][:, None], summary[0]], axis=1)
         tables = jnp.stack([tables, swap(tables, mate)])
@@ -344,9 +421,9 @@
         summary_row = (start[:, :, None] + offsets_rel[:, :local]).reshape(-1)
         chosen = narrow(summary_row[:, None] == jnp.arange(4 * rows, dtype=jnp.int32)[None, :])
 
-        def spread_sums(part):
+        def spread_sums(part, needed):
             for mask in middle + [top]:
-                part = jnp.concatenate([part, swap(part, mask)], axis=1)
+                part = jnp.concatenate([part, after(swap(part, mask), needed)], axis=1)
             return jnp.pad(part, ((0, 0), (0, KEY_PAD - part.shape[1]), (0, 0)))
 
         def collect_sums(whole):
@@ -357,7 +434,7 @@
             return whole
 
         normed = narrow(layer_norm(inputs, gain1, shift1))
-        normed_near, normed_far = spread_rows(normed)
+        normed_near, normed_far = spread_rows(after(normed, crossed[0], valid_count, bias, tables))
         normed_all = jnp.concatenate([normed_near, normed_far], axis=0)
         key_states = narrow(contract(normed_all, full_key, 1, 0))
         value_states = narrow(contract(normed_all, full_value, 1, 0) + bias_value)
@@ -367,23 +444,37 @@
             [narrow(contract(chosen, key_states, 1, 0)), narrow(contract(chosen, value_states, 1, 0))],
             axis=1,
         )
-        picked = spread_sums(picked.reshape(2, local * marks, 2 * width))
+        picked = picked.reshape(2, local * marks, 2 * width)
+        cross(3, crossed[2], picked)
+        queries = after(queries, leaving_shards[-1], sent[-1])
+        picked = spread_sums(picked, queries)
         key_sums = (picked[:, :, :width], picked[:, :, width:])
         (attended,) = attend(
             forward_kernel, rows, seg, (queries, key_states, value_states), key_sums, seen, 1, 0
         )
-        branch = collect_rows(lambda b: contract(row_block(attended, b), full_out, 1, 1))
+        leaving, complete = start_collect(attended, lambda block: contract(block, full_out, 1, 1))
+        run(up_stages, leaving)
+        branch = complete(sent[-1])
         hidden = inputs + branch + bias_out
 
         normed_mid = narrow(layer_norm(hidden, gain2, shift2))
+        down_stages = fetch(3, normed_mid)
+        run(down_stages)
+        finish(up_stages, normed_mid)
         mid_near, mid_far = spread_rows(normed_mid)
-        active = [
-            narrow(jnp.maximum(contract(part, full_up, 1, 0) + bias_up, 0.0))
-            for part in (mid_near, mid_far)
-        ]
+        mid_far = after(mid_far, sent[-1])
+        full_up = gathered[2][0]
+        active = []
+        for part in (mid_near, mid_far):
+            part = after(part, active)
+            active.append(narrow(jnp.maximum(contract(part, full_up, 1, 0) + bias_up, 0.0)))
+        run(down_stages, active)
+        finish(down_stages)
+        full_down = gathered[3][0]
         active_all = jnp.concatenate(active, axis=0)
         mid_all = jnp.concatenate([mid_near, mid_far], axis=0)
-        feed_out = collect_rows(lambda b: contract(row_block(active_all, b), full_down, 1, 1))
+        _, complete = start_collect(active_all, lambda block: contract(block, full_down, 1, 1))
+        feed_out = complete()
         output = hidden + feed_out + bias_down
 
         deviation = output - target
@@ -393,22 +484,30 @@
 
         feed_near, feed_far = spread_rows(narrow(grad_output))
         feed_all = jnp.concatenate([feed_near, feed_far], axis=0)
-        grad_pre = [
-            narrow(jnp.where(kept > 0, contract(part, full_down, 1, 0), 0.0))
-            for part, kept in zip((feed_near, feed_far), active)
-        ]
+        totals = [[], [], [], []]
+        down_stages = scatter_weight([(feed_all, active_all)], totals[0])
+        run(down_stages)
+        feed_near, feed_far = after((feed_near, feed_far), sent[-1])
+        grad_pre = []
+        for part, kept in zip((feed_near, feed_far), active):
+            part = after(part, grad_pre)
+            grad_pre.append(narrow(jnp.where(kept > 0, contract(part, full_down, 1, 0), 0.0)))
         grad_pre_all = jnp.concatenate(grad_pre, axis=0)
-        grad_mid = collect_rows(lambda b: contract(row_block(grad_pre_all, b), full_up, 1, 1))
-        grad_w_down = scatter_weight(feed_all, active_all)
-        grad_w_up = scatter_weight(mid_all, grad_pre_all)
+        mid_leaving, complete = start_collect(grad_pre_all, lambda block: contract(block, full_up, 1, 1))
+        up_stages = scatter_weight([(mid_all, grad_pre_all)], totals[1], mid_leaving)
+        run(up_stages)
+        run(down_stages, sent[-1])
+        grad_mid = complete(sent[-1])
         second_norm, second_pull = jax.vjp(layer_norm, hidden, gain2, shift2)
         grad_hidden_norm, grad_gain2, grad_shift2 = second_pull(grad_mid)
         grad_hidden = grad_output + grad_hidden_norm
 
-        branch_near, branch_far = spread_rows(narrow(grad_hidden))
+        grad_branch = narrow(grad_hidden)
+        branch_near, branch_far = spread_rows(grad_branch)
+        run(up_stages, grad_branch)
+        branch_far = after(branch_far, sent[-1])
         branch_all = jnp.concatenate([branch_near, branch_far], axis=0)
         grad_attended = narrow(contract(branch_all, full_out, 1, 0))
-        grad_w_out = scatter_weight(branch_all, attended)
         grad_pre_query, grad_keys, grad_values, key_part, value_part = attend(
             backward_kernel,
             rows,
@@ -419,95 +518,107 @@
             3,
             2,
         )
-        grad_w_query = scatter_weight(normed_all, grad_pre_query)
         parts = collect_sums(jnp.concatenate([key_part, value_part], axis=2))
         parts = narrow(parts.reshape(-1, 2 * width))
         grad_keys = narrow(grad_keys + contract(chosen, parts[:, :width], 0, 0))
         grad_values = narrow(grad_values + contract(chosen, parts[:, width:], 0, 0))
-        grad_w_key = scatter_weight(normed_all, grad_keys)
-        grad_w_value = scatter_weight(normed_all, grad_values)
-        grad_normed = collect_rows(
-            lambda b: contract(row_block(grad_pre_query, b), full_query, 1, 1)
-            + contract(row_block(grad_keys, b), full_key, 1, 1)
-            + contract(row_block(grad_values, b), full_value, 1, 1)
-        )
+        joined_grads = jnp.concatenate([grad_keys, grad_values, grad_pre_query], axis=1)
+
+        def normed_part(block):
+            return (
+                contract(block[:, :width], full_key, 1, 1)
+                + contract(block[:, width : 2 * width], full_value, 1, 1)
+                + contract(block[:, 2 * width :], full_query, 1, 1)
+            )
+
+        normed_leaving, complete = start_collect(joined_grads, normed_part)
+        first_stages = scatter_weight(
+            [(branch_all, attended), (normed_all, grad_pre_query)], totals[2], normed_leaving
+        )
+        run(first_stages, normed_leaving)
+        last_stages = scatter_weight(
+            [(normed_all, grad_keys), (normed_all, grad_values)], totals[3], sent[-1]
+        )
+        finish(down_stages, normed_leaving)
+        run(last_stages, given[0])
+        finish(up_stages, given[0])
+        grad_normed = complete(sent[-1])
         first_norm, first_pull = jax.vjp(layer_norm, inputs, gain1, shift1)
         grad_input_norm, grad_gain1, grad_shift1 = first_pull(grad_normed)
         grad_tokens = grad_hidden + grad_input_norm
 
-        def vector_sums(feature_rows, head_rows):
-            features = to_absolute(jnp.stack(feature_rows))
-            lines = features.shape[0]
-            joined = jnp.concatenate([features.reshape(-1, 128)] + [v.reshape(-1, 128) for v in head_rows])
-            cut = lines * depth // 128
-            for mask in plane + [top]:
-                joined = joined + swap(joined, mask)
-            tail = joined[cut:]
-            sizes = [v.shape[0] // 128 for v in head_rows]
-            pieces = []
-            offset = 0
-            for size in sizes:
-                pieces.append(tail[offset : offset + size])
-                offset += size
-            for mask in middle[::-1]:
-                kept = []
-                for piece in pieces:
-                    size = piece.shape[0] // 2
-                    kept.append(piece[:size] + swap(piece[size:], mask))
-                pieces = kept
-            tail = jnp.concatenate(pieces)
-            features = joined[:cut]
-            both = jnp.concatenate([features, tail])
-            came = swap(both, mate)
-            features = features + came[:cut]
-            tail = jnp.where(alike, tail, came[cut:])
-            for mask in middle + [low]:
-                features = features + swap(features, mask)
-            outs = []
-            offset = 0
-            for piece in pieces:
-                outs.append(tail[offset : offset + piece.shape[0]].reshape(-1))
-                offset += piece.shape[0]
-            return features.reshape(lines, depth), outs
-
-        squares_row = jnp.full((depth,), squares, jnp.float32)
-        early, (grad_b_up,) = vector_sums(
-            [
-                grad_gain2,
-                grad_shift2,
-                jnp.sum(grad_hidden, axis=0),
-                jnp.sum(grad_output, axis=0),
-                squares_row,
-            ],
-            [jnp.sum(grad_pre_all.astype(jnp.float32), axis=0)],
-        )
-        late, (grad_b_query, grad_b_value) = vector_sums(
-            [grad_gain1, grad_shift1],
-            [
-                jnp.sum(grad_pre_query.astype(jnp.float32), axis=0),
-                jnp.sum(grad_values.astype(jnp.float32), axis=0),
-            ],
-        )
-        mean_loss = early[4, 0] / (valid_count * depth)
+        feature_rows = [
+            grad_gain2,
+            grad_shift2,
+            jnp.sum(grad_hidden, axis=0),
+            jnp.sum(grad_output, axis=0),
+            jnp.full((depth,), squares, jnp.float32),
+            grad_gain1,
+            grad_shift1,
+        ]
+        head_rows = [
+            jnp.sum(grad_pre_all.astype(jnp.float32), axis=0),
+            jnp.sum(grad_pre_query.astype(jnp.float32), axis=0),
+            jnp.sum(grad_values.astype(jnp.float32), axis=0),
+        ]
+        lines = len(feature_rows)
+        cut = lines * depth // 128
+        joined = to_absolute(jnp.stack(feature_rows)).reshape(-1, 128)
+        joined = jnp.concatenate([joined] + [v.reshape(-1, 128) for v in head_rows])
+        turns = [first_stages, last_stages]
+        for turn, mask in enumerate(plane):
+            came = swap(joined, mask)
+            run(turns[turn % 2], given[1])
+            joined = joined + after(came, sent[-1])
+        came = swap(joined, mate)
+        finish(first_stages)
+        came = after(came, given[2])
+        features = joined[:cut] + came[:cut]
+        tails = [jnp.where(alike, joined[cut:], came[cut:]), jnp.where(alike, came[cut:], joined[cut:])]
+        sizes = [v.shape[0] // 128 for v in head_rows]
+        for mask in middle[::-1]:
+            for which, tail in enumerate(tails):
+                keep, give, offset = [], [], 0
+                for size in sizes:
+                    keep.append(tail[offset : offset + size // 2])
+                    give.append(tail[offset + size // 2 : offset + size])
+                    offset += size
+                tails[which] = jnp.concatenate(keep) + swap(jnp.concatenate(give), mask)
+            sizes = [size // 2 for size in sizes]
+        for mask in middle + [low]:
+            came = swap(features, mask)
+            finish(last_stages)
+            features = features + after(came, given[3])
+        came = swap(jnp.concatenate([features, tails[1]]), top)
+        features = (features + came[:cut]).reshape(lines, depth)
+        tail = tails[0] + came[cut:]
+        ends = [sum(sizes[: i + 1]) for i in range(len(sizes))]
+        grad_b_up, grad_b_query, grad_b_value = [
+            tail[end - size : end].reshape(-1) for end, size in zip(ends, sizes)
+        ]
+        grad_w_down, grad_w_up = totals[0][0], totals[1][0]
+        grad_w_out, grad_w_query = jnp.split(totals[2][0], 2, axis=1)
+        grad_w_key, grad_w_value = jnp.split(totals[3][0], 2, axis=1)
+        mean_loss = features[4, 0] / (valid_count * depth)
         return (
             to_absolute(narrow(output)),
             mean_loss,
             to_absolute(grad_tokens),
-            late[0],
-            late[1],
+            features[5],
+            features[6],
             grad_w_query,
             grad_b_query,
             grad_w_key,
             grad_w_value,
             grad_b_value,
             grad_w_out,
-            early[2],
-            early[0],
-            early[1],
+            features[2],
+            features[0],
+            features[1],
             grad_w_up,
             grad_b_up,
             grad_w_down,
-            early[3],
+            features[3],
         )
 
     return body

time: 993 us -> 816 us (0.82)
  starting transfers between devices: 277 us -> 69.1 us
  matrix products: 147 us -> 162 us
    ppermute x84 -> x86, starting transfers between devices: 175 us -> 69.1 us  [swap(): lax.ppermute(values, ('fsdp', 'tp'), [(i, i ^ mask) for i in range(world)])]
    ppermute x30 -> x0, starting transfers between devices: 103 us -> none  [send(): return lax.ppermute(values, ('fsdp', 'tp'), pairs)]
    ppermute x30 -> x0, waiting for transfers between devices: 98.7 us -> none  [send(): return lax.ppermute(values, ('fsdp', 'tp'), pairs)]
    ppermute x84 -> x86, waiting for transfers between devices: 321 us -> 419 us  [swap(): lax.ppermute(values, ('fsdp', 'tp'), [(i, i ^ mask) for i in range(world)])]
    dot_general x60, matrix products: 146 us -> 161 us  [contract(): lax.dot_general(left_side, right_side, (((left_dim,), (right_dim,)), ((),...]
    select_n x1 -> x13, other arithmetic: 0.01 us -> 12.6 us  [the longest x4 7.44 us: scatter_weight(): other = jnp.where(core == 0, kept[1], kept[0])]
    unnamed x16 -> x6, other arithmetic: 17.4 us -> 6.97 us
    unnamed x256 -> x279, local copies, waits for them, and re-layouts: 35 us -> 40.3 us
  transfers between devices with their start and end apart: 114 -> 86, of which waited for: 47 -> 38; matrix products, arithmetic and copies ran while one was open for 22% -> 25% of each run, Pallas kernels for 1% -> 3%
where the time goes in v3:
time: 816 us; the launch traced here: 805 us
  waiting for transfers between devices  419 us (51%)
  matrix products  162 us (20%)
  starting transfers between devices  69.1 us (8%)
  other arithmetic  62.7 us (8%)
  local copies, waits for them, and re-layouts  57 us (7%)
  Pallas kernels  28.9 us (4%)
    ppermute x86, waiting for transfers between devices, swap(): lax.ppermute(values, ('fsdp', 'tp'), [(i, i ^ mask) for i in range(world)])  419 us
    dot_general x60, matrix products, contract(): lax.dot_general(left_side, right_side, (((left_dim,), (right_dim,)), ((),...  161 us
    ppermute x86, starting transfers between devices, swap(): lax.ppermute(values, ('fsdp', 'tp'), [(i, i ^ mask) for i in range(world)])  69.1 us
    unnamed x279, local copies, waits for them, and re-layouts  40.3 us
    pallas_call x2, Pallas kernels, attend(): pl.pallas_call(lambda *refs: kernel(rows, seg, *refs), grid=(width // PAI...  28.9 us
  transfers between devices with their start and end apart: 86, of which 38 were waited for; matrix products, arithmetic and copies ran while one was open for 25% of the time, Pallas kernels for 3%

profile of v3, /device:TPU:0, one launch (start us, length us, event | category | flops | bytes accessed | tf_op | source)
XLA Modules:
  0.0 805.5 jit_solution(6654565020480455063)
XLA Ops:
  24.4 9.9 %collective-permute-done = bf16[256,1024]{0,1:T(8,128)(2,1)S(1)} collective-permute-done((bf16[256,1024]{0,1:T(8,128)(2,1)}, bf16[256,1024]{0,1:T(8,128)(2,1)S(1)}, u32[]{:S(2)}, u32[]{:S(2)}) %collective-permute-start) | collective-permute-done | bytes 524320 | tf_op jit(solution)/shard_map/ppermute | solution.py:154
  53.1 6.9 collective-permute-done.13
  62.7 7.1 collective-permute-done.11
  77.7 10.0 %collective-permute-done.9 = bf16[256,2048]{1,0:T(8,128)(2,1)} collective-permute-done((bf16[256,2048]{1,0:T(8,128)(2,1)S(1)}, bf16[256,2048]{1,0:T(8,128)(2,1)}, u32[]{:S(2)}, u32[]{:S(2)}) %collective-permute-start.9) | collective-permute-done | bytes 1048608 | tf_op jit(solution)/shard_map/ppermute | solution.py:154
  90.4 19.8 %collective-permute-done.16 = bf16[256,1024]{0,1:T(8,128)(2,1)S(1)} collective-permute-done((bf16[256,1024]{0,1:T(8,128)(2,1)S(1)}, bf16[256,1024]{0,1:T(8,128)(2,1)S(1)}, u32[]{:S(2)}, u32[]{:S(2)}) %collective-permute-start.16) | collective-permute-done | bytes 524320 | tf_op jit(solution)/shard_map/ppermute | solution.py:154
  121.5 39.6 %collective-permute-done.22 = bf16[256,2048]{1,0:T(8,128)(2,1)S(1)} collective-permute-done((bf16[256,2048]{1,0:T(8,128)(2,1)S(1)}, bf16[256,2048]{1,0:T(8,128)(2,1)S(1)}, u32[]{:S(2)}, u32[]{:S(2)}) %collective-permute-start.22) | collective-permute-done | bytes 1048608 | tf_op jit(solution)/shard_map/ppermute | solution.py:154
  168.5 8.3 %attend_forward.1 = bf16[1024,512]{1,0:T(8,128)(2,1)} custom-call(bf16[1024,512]{1,0:T(8,128)(2,1)} %multiply_convert_fusion.refs_0_, bf16[1024,512]{1,0:T(8,128)(2,1)} %copy-done.16, bf16[1024,512]{1,0:T(8,128)(2,1)} %copy-done.15, bf16[2,128,512]{2,1,0:T(8,128)(2,1)} %get-tuple-element.330.refs_3_.refs_4_, ...), custom_call_target="tpu_custom_call" | custom-call | flops 1 | bytes 1 | tf_op jit(solution)/shard_map/attend_forward/pallas_call | solution.py:131
  188.4 16.6 %collective-permute-done.28 = bf16[256,2048]{1,0:T(8,128)(2,1)S(1)} collective-permute-done((bf16[256,2048]{1,0:T(8,128)(2,1)S(1)}, bf16[256,2048]{1,0:T(8,128)(2,1)S(1)}, u32[]{:S(2)}, u32[]{:S(2)}) %collective-permute-start.28) | collective-permute-done | bytes 1048608 | tf_op jit(solution)/shard_map/ppermute | solution.py:154
  208.5 22.6 %collective-permute-done.27 = bf16[256,2048]{1,0:T(8,128)(2,1)S(1)} collective-permute-done((bf16[256,2048]{1,0:T(8,128)(2,1)S(1)}, bf16[256,2048]{1,0:T(8,128)(2,1)S(1)}, u32[]{:S(2)}, u32[]{:S(2)}) %collective-permute-start.27) | collective-permute-done | bytes 1048608 | tf_op jit(solution)/shard_map/ppermute | solution.py:154
  241.6 18.9 %collective-permute-done.33 = bf16[256,2048]{1,0:T(8,128)(2,1)S(1)} collective-permute-done((bf16[256,2048]{1,0:T(8,128)(2,1)S(1)}, bf16[256,2048]{1,0:T(8,128)(2,1)S(1)}, u32[]{:S(2)}, u32[]{:S(2)}) %collective-permute-start.33) | collective-permute-done | bytes 1048608 | tf_op jit(solution)/shard_map/ppermute | solution.py:154
  279.6 42.2 %collective-permute-done.39 = bf16[512,2048]{1,0:T(8,128)(2,1)S(1)} collective-permute-done((bf16[512,2048]{1,0:T(8,128)(2,1)S(1)}, bf16[512,2048]{1,0:T(8,128)(2,1)S(1)}, u32[]{:S(2)}, u32[]{:S(2)}) %collective-permute-start.39) | collective-permute-done | bytes 2097184 | tf_op jit(solution)/shard_map/ppermute | solution.py:154
  328.1 5.9 convolution_convert_fusion.9
  336.7 6.8 fusion.8
  343.5 6.8 convolution_convert_fusion.8
  355.9 13.1 %collective-permute-done.43 = bf16[256,2048]{1,0:T(8,128)(2,1)} collective-permute-done((bf16[256,2048]{1,0:T(8,128)(2,1)}, bf16[256,2048]{1,0:T(8,128)(2,1)}, u32[]{:S(2)}, u32[]{:S(2)}) %collective-permute-start.43) | collective-permute-done | bytes 1048608 | tf_op jit(solution)/shard_map/ppermute | solution.py:154
  369.1 8.9 %multiply_convert_fusion.1 = (bf16[256,2048]{1,0:T(8,128)(2,1)S(1)}, f32[256,2048]{1,0:T(8,128)}) fusion(f32[256]{0:T(256)S(1)} %broadcast_multiply_fusion, bf16[256,2048]{1,0:T(8,128)(2,1)} %constant_dynamic-update-slice_fusion.52, f32[2048]{0:T(1024)S(1)} %bitcast.244, f32[256,2048]{1,0:T(8,128)S(1)} %get-tuple-element.313, ...), kind=kOutput, calls=%fused_computation.116 | convolution fusion | flops 2152726528 | bytes 17835008 | tf_op jit(solution)/shard_map/dot_general | solution.py:23
  378.2 24.1 %collective-permute-done.45 = bf16[256,2048]{1,0:T(8,128)(2,1)S(1)} collective-permute-done((bf16[256,2048]{1,0:T(8,128)(2,1)S(1)}, bf16[256,2048]{1,0:T(8,128)(2,1)S(1)}, u32[]{:S(2)}, u32[]{:S(2)}) %collective-permute-start.45) | collective-permute-done | bytes 1048608 | tf_op jit(solution)/shard_map/ppermute | solution.py:154
  413.5 9.2 %select_convert_fusion.1 = bf16[512,2048]{1,0:T(8,128)(2,1)} fusion(bf16[512,2048]{1,0:T(8,128)(2,1)S(1)} %copy-done.47, bf16[512,2048]{1,0:T(8,128)(2,1)S(1)} %pad_maximum_fusion.12, bf16[2048,2048]{1,0:T(8,128)(2,1)} %constant_dynamic-update-slice_fusion.38), kind=kOutput, calls=%fused_computation.11 | convolution fusion | flops 4298113024 | bytes 14680064 | tf_op jit(solution)/shard_map/dot_general | solution.py:23
  422.8 8.2 %select_convert_fusion = bf16[512,2048]{1,0:T(8,128)(2,1)S(1)} fusion(bf16[512,2048]{1,0:T(8,128)(2,1)S(1)} %copy-done.50, bf16[512,2048]{1,0:T(8,128)(2,1)S(1)} %pad_maximum_fusion.13, bf16[2048,2048]{1,0:T(8,128)(2,1)} %constant_dynamic-update-slice_fusion.38), kind=kOutput, calls=%fused_computation.10 | convolution fusion | flops 4298113024 | bytes 14680064 | tf_op jit(solution)/shard_map/dot_general | solution.py:23
  439.7 6.0 fusion.9
  453.8 6.9 convolution_convert_fusion.6
  462.1 24.6 %collective-permute-done.50 = bf16[512,2048]{1,0:T(8,128)(2,1)} collective-permute-done((bf16[512,2048]{1,0:T(8,128)(2,1)}, bf16[512,2048]{1,0:T(8,128)(2,1)}, u32[]{:S(2)}, u32[]{:S(2)}) %collective-permute-start.50) | collective-permute-done | bytes 2097184 | tf_op jit(solution)/shard_map/ppermute | solution.py:154
  499.6 6.8 multiply_reduce_fusion.1
  514.9 16.8 %collective-permute-done.55 = bf16[512,2048]{1,0:T(8,128)(2,1)} collective-permute-done((bf16[512,2048]{1,0:T(8,128)(2,1)}, bf16[512,2048]{1,0:T(8,128)(2,1)}, u32[]{:S(2)}, u32[]{:S(2)}) %collective-permute-start.55) | collective-permute-done | bytes 2097184 | tf_op jit(solution)/shard_map/ppermute | solution.py:154
  554.4 20.5 %attend_backward.1 = (bf16[1024,512]{1,0:T(8,128)(2,1)}, bf16[1024,512]{1,0:T(8,128)(2,1)}, bf16[1024,512]{1,0:T(8,128)(2,1)}, f32[2,128,512]{2,1,0:T(8,128)}, f32[2,128,512]{2,1,0:T(8,128)}) custom-call(bf16[1024,512]{1,0:T(8,128)(2,1)} %multiply_convert_fusion.refs_0_, bf16[1024,512]{1,0:T(8,128)(2,1)} %copy-done.16, bf16[1024,512]{1,0:T(8,128)(2,1)} %copy-done.15, ...), custom_call_target="tpu_custom_call" | custom-call | flops 1 | bytes 1 | tf_op jit(solution)/shard_map/attend_backward/pallas_call | solution.py:131
  580.8 8.8 %collective-permute-done.57 = bf16[2,48,1024]{2,1,0:T(8,128)(2,1)S(1)} collective-permute-done((bf16[2,48,1024]{2,1,0:T(8,128)(2,1)S(1)}, bf16[2,48,1024]{2,1,0:T(8,128)(2,1)S(1)}, u32[]{:S(2)}, u32[]{:S(2)}) %collective-permute-start.57) | collective-permute-done | bytes 196640 | tf_op jit(solution)/shard_map/ppermute | solution.py:154
  655.2 8.1 %collective-permute-done.67 = bf16[512,1024]{0,1:T(8,128)(2,1)} collective-permute-done((bf16[512,1024]{0,1:T(8,128)(2,1)}, bf16[512,1024]{0,1:T(8,128)(2,1)}, u32[]{:S(2)}, u32[]{:S(2)}) %collective-permute-start.67) | collective-permute-done | bytes 1048608 | tf_op jit(solution)/shard_map/ppermute | solution.py:154
  670.3 19.5 %collective-permute-done.66 = f32[136,128]{1,0:T(8,128)S(1)} collective-permute-done((f32[136,128]{1,0:T(8,128)S(1)}, f32[136,128]{1,0:T(8,128)S(1)}, u32[]{:S(2)}, u32[]{:S(2)}) %collective-permute-start.66) | collective-permute-done | bytes 69664 | tf_op jit(solution)/shard_map/ppermute | solution.py:154
  704.6 20.1 %collective-permute-done.85 = bf16[256,2048]{1,0:T(8,128)(2,1)S(1)} collective-permute-done((bf16[256,2048]{1,0:T(8,128)(2,1)S(1)}, bf16[256,2048]{1,0:T(8,128)(2,1)S(1)}, u32[]{:S(2)}, u32[]{:S(2)}) %collective-permute-start.85) | collective-permute-done | bytes 1048608 | tf_op jit(solution)/shard_map/ppermute | solution.py:154
  732.6 9.9 %collective-permute-done.77 = f32[112,128]{1,0:T(8,128)S(1)} collective-permute-done((f32[112,128]{1,0:T(8,128)S(1)}, f32[112,128]{1,0:T(8,128)S(1)}, u32[]{:S(2)}, u32[]{:S(2)}) %collective-permute-start.77) | collective-permute-done | bytes 57376 | tf_op jit(solution)/shard_map/ppermute | solution.py:154
  746.0 25.2 %collective-permute-done.84 = bf16[256,2048]{1,0:T(8,128)(2,1)S(1)} collective-permute-done((bf16[256,2048]{1,0:T(8,128)(2,1)S(1)}, bf16[256,2048]{1,0:T(8,128)(2,1)S(1)}, u32[]{:S(2)}, u32[]{:S(2)}) %collective-permute-start.84) | collective-permute-done | bytes 1048608 | tf_op jit(solution)/shard_map/ppermute | solution.py:154
  773.1 21.2 %collective-permute-done.81 = f32[136,128]{1,0:T(8,128)S(1)} collective-permute-done((f32[136,128]{1,0:T(8,128)S(1)}, f32[136,128]{1,0:T(8,128)S(1)}, u32[]{:S(2)}, u32[]{:S(2)}) %collective-permute-start.81) | collective-permute-done | bytes 69664 | tf_op jit(solution)/shard_map/ppermute | solution.py:154
  (635 shorter events, 319.6 us)
Async XLA Ops:
  10.0 41.4 %collective-permute-start.6 = (f32[1,3072]{1,0:T(1,128)S(1)}, f32[1,3072]{1,0:T(1,128)S(1)}, u32[]{:S(2)}, u32[]{:S(2)}) collective-permute-start(f32[1,3072]{1,0:T(1,128)S(1)} %bitcast.221), channel_id=1, source_target_pairs={{0,2},{1,3},{2,0},{3,1},{4,6},{5,7},{6,4},{7,5},{8,10},{9,11},{10,... | collective-permute-start | bytes 36872 | tf_op jit(solution)/shard_map/ppermute | solution.py:154
  71.8 38.5 %collective-permute-start.18 = (bf16[512,1024]{0,1:T(8,128)(2,1)}, bf16[512,1024]{0,1:T(8,128)(2,1)S(1)}, u32[]{:S(2)}, u32[]{:S(2)}) collective-permute-start(bf16[512,1024]{0,1:T(8,128)(2,1)} %get-tuple-element.128), channel_id=1, source_target_pairs={{0,16},{1,17},{2,18},{3,19},{4,20},{5,21},{6,22},{7,23},{8,24},{9,... | collective-permute-start | bytes 3145736 | tf_op jit(solution)/shard_map/ppermute | solution.py:154
  73.4 36.9 %collective-permute-start.19 = (bf16[512,1024]{0,1:T(8,128)(2,1)}, bf16[512,1024]{0,1:T(8,128)(2,1)S(1)}, u32[]{:S(2)}, u32[]{:S(2)}) collective-permute-start(bf16[512,1024]{0,1:T(8,128)(2,1)} %get-tuple-element.129), channel_id=1, source_target_pairs={{0,8},{1,9},{2,10},{3,11},{4,12},{5,13},{6,14},{7,15},{8,0},{9,1},... | collective-permute-start | bytes 3145736 | tf_op jit(solution)/shard_map/ppermute | solution.py:154
  110.2 51.0 %collective-permute-start.22 = (bf16[256,2048]{1,0:T(8,128)(2,1)S(1)}, bf16[256,2048]{1,0:T(8,128)(2,1)S(1)}, u32[]{:S(2)}, u32[]{:S(2)}) collective-permute-start(bf16[256,2048]{1,0:T(8,128)(2,1)S(1)} %copy-done.33), channel_id=1, source_target_pairs={{0,2},{1,3},{2,0},{3,1},{4,6},{5,7},{6,4},{7,5},{8,10},{9,11},{10,... | collective-permute-start | bytes 3145736 | tf_op jit(solution)/shard_map/ppermute | solution.py:154
  110.4 50.8 %collective-permute-start.20 = (bf16[512,1024]{0,1:T(8,128)(2,1)S(1)}, bf16[512,1024]{0,1:T(8,128)(2,1)S(1)}, u32[]{:S(2)}, u32[]{:S(2)}) collective-permute-start(bf16[512,1024]{0,1:T(8,128)(2,1)S(1)} %pad_maximum_fusion.17), channel_id=1, source_target_pairs={{0,16},{1,17},{2,18},{3,19},{4,20},{5,21},{6,22},{7,23},{8,24},{9,... | collective-permute-start | bytes 3145736 | tf_op jit(solution)/shard_map/ppermute | solution.py:154
  111.0 50.2 %collective-permute-start.21 = (bf16[512,1024]{0,1:T(8,128)(2,1)S(1)}, bf16[512,1024]{0,1:T(8,128)(2,1)S(1)}, u32[]{:S(2)}, u32[]{:S(2)}) collective-permute-start(bf16[512,1024]{0,1:T(8,128)(2,1)S(1)} %pad_maximum_fusion.18), channel_id=1, source_target_pairs={{0,8},{1,9},{2,10},{3,11},{4,12},{5,13},{6,14},{7,15},{8,0},{9,1},... | collective-permute-start | bytes 3145736 | tf_op jit(solution)/shard_map/ppermute | solution.py:154
  118.5 48.9 %collective-permute-start.24 = (bf16[2,48,1024]{2,1,0:T(8,128)(2,1)S(1)}, bf16[2,48,1024]{2,1,0:T(8,128)(2,1)S(1)}, u32[]{:S(2)}, u32[]{:S(2)}) collective-permute-start(bf16[2,48,1024]{2,1,0:T(8,128)(2,1)S(1)} %bitcast.206), channel_id=1, source_target_pairs={{0,2},{1,3},{2,0},{3,1},{4,6},{5,7},{6,4},{7,5},{8,10},{9,11},{10,... | collective-permute-start | bytes 589832 | tf_op jit(solution)/shard_map/ppermute | solution.py:154
  184.5 46.5 %collective-permute-start.27 = (bf16[256,2048]{1,0:T(8,128)(2,1)S(1)}, bf16[256,2048]{1,0:T(8,128)(2,1)S(1)}, u32[]{:S(2)}, u32[]{:S(2)}) collective-permute-start(bf16[256,2048]{1,0:T(8,128)(2,1)S(1)} %add_convert_fusion.4), channel_id=1, source_target_pairs={{0,1},{1,0},{2,3},{3,2},{4,5},{5,4},{6,7},{7,6},{8,9},{9,8},{10,11... | collective-permute-start | bytes 3145736 | tf_op jit(solution)/shard_map/ppermute | solution.py:154
  185.3 45.7 %collective-permute-start.26 = (bf16[256,2048]{1,0:T(8,128)(2,1)S(1)}, bf16[256,2048]{1,0:T(8,128)(2,1)S(1)}, u32[]{:S(2)}, u32[]{:S(2)}) collective-permute-start(bf16[256,2048]{1,0:T(8,128)(2,1)S(1)} %convolution_convert_fusion.4), channel_id=1, source_target_pairs={{0,4},{1,5},{2,6},{3,7},{4,0},{5,1},{6,2},{7,3},{8,12},{9,13},{10,... | collective-permute-start | bytes 3145736 | tf_op jit(solution)/shard_map/ppermute | solution.py:154
  185.8 48.9 %collective-permute-start.35 = (bf16[256,2048]{1,0:T(8,128)(2,1)S(1)}, bf16[256,2048]{1,0:T(8,128)(2,1)S(1)}, u32[]{:S(2)}, u32[]{:S(2)}) collective-permute-start(bf16[256,2048]{1,0:T(8,128)(2,1)S(1)} %copy-done.34), channel_id=1, source_target_pairs={{0,2},{1,3},{2,0},{3,1},{4,6},{5,7},{6,4},{7,5},{8,10},{9,11},{10,... | collective-permute-start | bytes 3145736 | tf_op jit(solution)/shard_map/ppermute | solution.py:154
  206.6 53.9 %collective-permute-start.31 = (bf16[512,2048]{1,0:T(8,128)(2,1)S(1)}, bf16[512,2048]{1,0:T(8,128)(2,1)S(1)}, u32[]{:S(2)}, u32[]{:S(2)}) collective-permute-start(bf16[512,2048]{1,0:T(8,128)(2,1)S(1)} %pad_maximum_fusion.6), channel_id=1, source_target_pairs={{0,16},{1,17},{2,18},{3,19},{4,20},{5,21},{6,22},{7,23},{8,24},{9,... | collective-permute-start | bytes 6291464 | tf_op jit(solution)/shard_map/ppermute | solution.py:154
  207.2 53.3 %collective-permute-start.32 = (bf16[512,2048]{1,0:T(8,128)(2,1)S(1)}, bf16[512,2048]{1,0:T(8,128)(2,1)S(1)}, u32[]{:S(2)}, u32[]{:S(2)}) collective-permute-start(bf16[512,2048]{1,0:T(8,128)(2,1)S(1)} %pad_maximum_fusion.7), channel_id=1, source_target_pairs={{0,8},{1,9},{2,10},{3,11},{4,12},{5,13},{6,14},{7,15},{8,0},{9,1},... | collective-permute-start | bytes 6291464 | tf_op jit(solution)/shard_map/ppermute | solution.py:154
  276.3 45.5 %collective-permute-start.39 = (bf16[512,2048]{1,0:T(8,128)(2,1)S(1)}, bf16[512,2048]{1,0:T(8,128)(2,1)S(1)}, u32[]{:S(2)}, u32[]{:S(2)}) collective-permute-start(bf16[512,2048]{1,0:T(8,128)(2,1)S(1)} %pad_maximum_fusion.10), channel_id=1, source_target_pairs={{0,16},{1,17},{2,18},{3,19},{4,20},{5,21},{6,22},{7,23},{8,24},{9,... | collective-permute-start | bytes 6291464 | tf_op jit(solution)/shard_map/ppermute | solution.py:154
  277.9 45.1 %collective-permute-start.40 = (bf16[512,2048]{1,0:T(8,128)(2,1)S(1)}, bf16[512,2048]{1,0:T(8,128)(2,1)S(1)}, u32[]{:S(2)}, u32[]{:S(2)}) collective-permute-start(bf16[512,2048]{1,0:T(8,128)(2,1)S(1)} %pad_maximum_fusion.11), channel_id=1, source_target_pairs={{0,8},{1,9},{2,10},{3,11},{4,12},{5,13},{6,14},{7,15},{8,0},{9,1},... | collective-permute-start | bytes 6291464 | tf_op jit(solution)/shard_map/ppermute | solution.py:154
  437.8 48.9 %collective-permute-start.50 = (bf16[512,2048]{1,0:T(8,128)(2,1)}, bf16[512,2048]{1,0:T(8,128)(2,1)}, u32[]{:S(2)}, u32[]{:S(2)}) collective-permute-start(bf16[512,2048]{1,0:T(8,128)(2,1)} %convolution_convert_fusion.3), channel_id=1, source_target_pairs={{0,16},{1,17},{2,18},{3,19},{4,20},{5,21},{6,22},{7,23},{8,24},{9,... | collective-permute-start | bytes 6291464 | tf_op jit(solution)/shard_map/ppermute | solution.py:154
  438.5 48.9 %collective-permute-start.51 = (bf16[512,2048]{1,0:T(8,128)(2,1)}, bf16[512,2048]{1,0:T(8,128)(2,1)}, u32[]{:S(2)}, u32[]{:S(2)}) collective-permute-start(bf16[512,2048]{1,0:T(8,128)(2,1)} %convolution_convert_fusion.2), channel_id=1, source_target_pairs={{0,8},{1,9},{2,10},{3,11},{4,12},{5,13},{6,14},{7,15},{8,0},{9,1},... | collective-permute-start | bytes 6291464 | tf_op jit(solution)/shard_map/ppermute | solution.py:154
  445.6 54.0 %collective-permute-start.49 = (bf16[256,2048]{1,0:T(8,128)(2,1)S(1)}, bf16[256,2048]{1,0:T(8,128)(2,1)S(1)}, u32[]{:S(2)}, u32[]{:S(2)}) collective-permute-start(bf16[256,2048]{1,0:T(8,128)(2,1)S(1)} %fusion.9), channel_id=1, source_target_pairs={{0,1},{1,0},{2,3},{3,2},{4,5},{5,4},{6,7},{7,6},{8,9},{9,8},{10,11... | collective-permute-start | bytes 3145736 | tf_op jit(solution)/shard_map/ppermute | solution.py:154
  460.7 38.9 %collective-permute-start.48 = (bf16[256,2048]{1,0:T(8,128)(2,1)}, bf16[256,2048]{1,0:T(8,128)(2,1)}, u32[]{:S(2)}, u32[]{:S(2)}) collective-permute-start(bf16[256,2048]{1,0:T(8,128)(2,1)} %convolution_convert_fusion.6), channel_id=1, source_target_pairs={{0,4},{1,5},{2,6},{3,7},{4,0},{5,1},{6,2},{7,3},{8,12},{9,13},{10,... | collective-permute-start | bytes 3145736 | tf_op jit(solution)/shard_map/ppermute | solution.py:154
  460.7 71.0 %collective-permute-start.55 = (bf16[512,2048]{1,0:T(8,128)(2,1)}, bf16[512,2048]{1,0:T(8,128)(2,1)}, u32[]{:S(2)}, u32[]{:S(2)}) collective-permute-start(bf16[512,2048]{1,0:T(8,128)(2,1)} %convolution_convert_fusion.1), channel_id=1, source_target_pairs={{0,16},{1,17},{2,18},{3,19},{4,20},{5,21},{6,22},{7,23},{8,24},{9,... | collective-permute-start | bytes 6291464 | tf_op jit(solution)/shard_map/ppermute | solution.py:154
  486.7 48.8 %collective-permute-start.56 = (bf16[512,2048]{1,0:T(8,128)(2,1)}, bf16[512,2048]{1,0:T(8,128)(2,1)}, u32[]{:S(2)}, u32[]{:S(2)}) collective-permute-start(bf16[512,2048]{1,0:T(8,128)(2,1)} %convolution_convert_fusion), channel_id=1, source_target_pairs={{0,8},{1,9},{2,10},{3,11},{4,12},{5,13},{6,14},{7,15},{8,0},{9,1},... | collective-permute-start | bytes 6291464 | tf_op jit(solution)/shard_map/ppermute | solution.py:154
  512.6 94.7 %collective-permute-start.61 = (bf16[256,2048]{1,0:T(8,128)(2,1)}, bf16[256,2048]{1,0:T(8,128)(2,1)}, u32[]{:S(2)}, u32[]{:S(2)}) collective-permute-start(bf16[256,2048]{1,0:T(8,128)(2,1)} %slice.707), channel_id=1, source_target_pairs={{0,8},{1,9},{2,10},{3,11},{4,12},{5,13},{6,14},{7,15},{8,0},{9,1},... | collective-permute-start | bytes 3145736 | tf_op jit(solution)/shard_map/ppermute | solution.py:154
  514.1 93.2 %collective-permute-start.62 = (bf16[256,2048]{1,0:T(8,128)(2,1)}, bf16[256,2048]{1,0:T(8,128)(2,1)}, u32[]{:S(2)}, u32[]{:S(2)}) collective-permute-start(bf16[256,2048]{1,0:T(8,128)(2,1)} %slice.706), channel_id=1, source_target_pairs={{0,16},{1,17},{2,18},{3,19},{4,20},{5,21},{6,22},{7,23},{8,24},{9,... | collective-permute-start | bytes 3145736 | tf_op jit(solution)/shard_map/ppermute | solution.py:154
  546.9 92.5 %collective-permute-start.63 = (bf16[256,2048]{1,0:T(8,128)(2,1)}, bf16[256,2048]{1,0:T(8,128)(2,1)}, u32[]{:S(2)}, u32[]{:S(2)}) collective-permute-start(bf16[256,2048]{1,0:T(8,128)(2,1)} %slice.705), channel_id=1, source_target_pairs={{0,8},{1,9},{2,10},{3,11},{4,12},{5,13},{6,14},{7,15},{8,0},{9,1},... | collective-permute-start | bytes 3145736 | tf_op jit(solution)/shard_map/ppermute | solution.py:154
  553.7 86.8 %collective-permute-start.64 = (bf16[256,2048]{1,0:T(8,128)(2,1)}, bf16[256,2048]{1,0:T(8,128)(2,1)}, u32[]{:S(2)}, u32[]{:S(2)}) collective-permute-start(bf16[256,2048]{1,0:T(8,128)(2,1)} %slice.704), channel_id=1, source_target_pairs={{0,16},{1,17},{2,18},{3,19},{4,20},{5,21},{6,22},{7,23},{8,24},{9,... | collective-permute-start | bytes 3145736 | tf_op jit(solution)/shard_map/ppermute | solution.py:154
  601.1 39.9 %collective-permute-start.60 = (bf16[256,2048]{1,0:T(8,128)(2,1)S(1)}, bf16[256,2048]{1,0:T(8,128)(2,1)S(1)}, u32[]{:S(2)}, u32[]{:S(2)}) collective-permute-start(bf16[256,2048]{1,0:T(8,128)(2,1)S(1)} %add_convert_fusion), channel_id=1, source_target_pairs={{0,1},{1,0},{2,3},{3,2},{4,5},{5,4},{6,7},{7,6},{8,9},{9,8},{10,11... | collective-permute-start | bytes 3145736 | tf_op jit(solution)/shard_map/ppermute | solution.py:154
  640.5 49.9 %collective-permute-start.71 = (bf16[512,1024]{0,1:T(8,128)(2,1)}, bf16[512,1024]{0,1:T(8,128)(2,1)}, u32[]{:S(2)}, u32[]{:S(2)}) collective-permute-start(bf16[512,1024]{0,1:T(8,128)(2,1)} %maximum_bitcast_fusion.6), channel_id=1, source_target_pairs={{0,16},{1,17},{2,18},{3,19},{4,20},{5,21},{6,22},{7,23},{8,24},{9,... | collective-permute-start | bytes 3145736 | tf_op jit(solution)/shard_map/ppermute | solution.py:154
  641.1 51.5 %collective-permute-start.72 = (bf16[512,1024]{0,1:T(8,128)(2,1)}, bf16[512,1024]{0,1:T(8,128)(2,1)}, u32[]{:S(2)}, u32[]{:S(2)}) collective-permute-start(bf16[512,1024]{0,1:T(8,128)(2,1)} %maximum_bitcast_fusion.7), channel_id=1, source_target_pairs={{0,8},{1,9},{2,10},{3,11},{4,12},{5,13},{6,14},{7,15},{8,0},{9,1},... | collective-permute-start | bytes 3145736 | tf_op jit(solution)/shard_map/ppermute | solution.py:154
  652.9 71.8 %collective-permute-start.85 = (bf16[256,2048]{1,0:T(8,128)(2,1)S(1)}, bf16[256,2048]{1,0:T(8,128)(2,1)S(1)}, u32[]{:S(2)}, u32[]{:S(2)}) collective-permute-start(bf16[256,2048]{1,0:T(8,128)(2,1)S(1)} %copy-done.60), channel_id=1, source_target_pairs={{0,2},{1,3},{2,0},{3,1},{4,6},{5,7},{6,4},{7,5},{8,10},{9,11},{10,... | collective-permute-start | bytes 3145736 | tf_op jit(solution)/shard_map/ppermute | solution.py:154
  690.5 80.7 %collective-permute-start.84 = (bf16[256,2048]{1,0:T(8,128)(2,1)S(1)}, bf16[256,2048]{1,0:T(8,128)(2,1)S(1)}, u32[]{:S(2)}, u32[]{:S(2)}) collective-permute-start(bf16[256,2048]{1,0:T(8,128)(2,1)S(1)} %broadcast_select_fusion.2), channel_id=1, source_target_pairs={{0,2},{1,3},{2,0},{3,1},{4,6},{5,7},{6,4},{7,5},{8,10},{9,11},{10,... | collective-permute-start | bytes 3145736 | tf_op jit(solution)/shard_map/ppermute | solution.py:154
  728.7 68.7 %collective-permute-start.82 = (bf16[256,1024]{0,1:T(8,128)(2,1)}, bf16[256,1024]{0,1:T(8,128)(2,1)}, u32[]{:S(2)}, u32[]{:S(2)}) collective-permute-start(bf16[256,1024]{0,1:T(8,128)(2,1)} %broadcast_select_fusion.17), channel_id=1, source_target_pairs={{0,2},{1,3},{2,0},{3,1},{4,6},{5,7},{6,4},{7,5},{8,10},{9,11},{10,... | collective-permute-start | bytes 1572872 | tf_op jit(solution)/shard_map/ppermute | solution.py:154
  732.6 67.2 %collective-permute-start.83 = (bf16[256,1024]{0,1:T(8,128)(2,1)}, bf16[256,1024]{0,1:T(8,128)(2,1)}, u32[]{:S(2)}, u32[]{:S(2)}) collective-permute-start(bf16[256,1024]{0,1:T(8,128)(2,1)} %broadcast_select_fusion.16), channel_id=1, source_target_pairs={{0,2},{1,3},{2,0},{3,1},{4,6},{5,7},{6,4},{7,5},{8,10},{9,11},{10,... | collective-permute-start | bytes 1572872 | tf_op jit(solution)/shard_map/ppermute | solution.py:154
  742.5 51.8 %collective-permute-start.81 = (f32[136,128]{1,0:T(8,128)S(1)}, f32[136,128]{1,0:T(8,128)S(1)}, u32[]{:S(2)}, u32[]{:S(2)}) collective-permute-start(f32[136,128]{1,0:T(8,128)S(1)} %pad_maximum_fusion.23), channel_id=1, source_target_pairs={{0,2},{1,3},{2,0},{3,1},{4,6},{5,7},{6,4},{7,5},{8,10},{9,11},{10,... | collective-permute-start | bytes 208904 | tf_op jit(solution)/shard_map/ppermute | solution.py:154
  (159 other events, 2235.3 us)

commit v4 on v3

--- a/solution.py
+++ b/solution.py
@@ -152,11 +152,6 @@
 
     def swap(values, mask):
         return lax.ppermute(values, ("fsdp", "tp"), [(i, i ^ mask) for i in range(world)])
-
-    def everyone(values):
-        for mask in bits_below(world, tp) + bits_below(tp, 1):
-            values = values + swap(values, mask)
-        return values
 
     def body(
         tokens,
@@ -315,8 +310,8 @@
                 part = jnp.concatenate([part, swap(part, mask)], axis=1)
             return part
 
-        def spread_rows(own):
-            across = swap(own, low)
+        def spread_rows(own, *needed):
+            across = after(swap(own, low), needed)
             near = jnp.concatenate([own, swap(own, mate)], axis=0)
             far = jnp.concatenate([across, swap(across, mate)], axis=0)
             return near, far
@@ -344,7 +339,10 @@
         )
         gain1, shift1, bias_out, gain2, shift2, bias_down = [vectors[i] for i in range(6)]
         weight_mask = valid_mask.astype(jnp.float32)[:, None]
-        counted = everyone(jnp.full((8, 128), jnp.sum(weight_mask), jnp.float32))
+        counted = jnp.full((8, 128), jnp.sum(weight_mask), jnp.float32)
+        for mask in bits_below(world, tp):
+            counted = counted + swap(counted, mask)
+        counted = counted + sum(swap(counted, mask) for mask in range(1, tp))
         valid_count = counted[0, 0]
 
         shards = [
@@ -368,7 +366,7 @@
             return gather_weight(bring_weight(shards[which], across), gathered[which])
 
         cross(0)
-        kv_stages = fetch(0)
+        kv_stages = fetch(0, counted)
         run(kv_stages)
         cross(1, crossed[0])
         run(kv_stages)
@@ -376,9 +374,11 @@
         qo_stages = fetch(1, sent[-1])
         run(qo_stages)
         finish(kv_stages)
+        run(qo_stages, crossed[2])
+        up_stages = fetch(2, sent[-1])
+        run(up_stages)
+        cross(3, crossed[2])
         finish(qo_stages)
-        up_stages = fetch(2, lane[-1])
-        run(up_stages)
         w_kv, w_qo = gathered[0][0], gathered[1][0]
 
         def split_two(joined):
@@ -426,15 +426,15 @@
                 part = jnp.concatenate([part, after(swap(part, mask), needed)], axis=1)
             return jnp.pad(part, ((0, 0), (0, KEY_PAD - part.shape[1]), (0, 0)))
 
-        def collect_sums(whole):
+        def collect_sums(whole, *needed):
             whole = whole[:, : segments * marks]
             for mask in [top] + middle[::-1]:
                 size = whole.shape[1] // 2
-                whole = whole[:, :size] + swap(narrow(whole[:, size:]), mask)
+                whole = whole[:, :size] + after(swap(narrow(whole[:, size:]), mask), needed)
             return whole
 
         normed = narrow(layer_norm(inputs, gain1, shift1))
-        normed_near, normed_far = spread_rows(after(normed, crossed[0], valid_count, bias, tables))
+        normed_near, normed_far = spread_rows(after(normed, crossed[0], bias, tables))
         normed_all = jnp.concatenate([normed_near, normed_far], axis=0)
         key_states = narrow(contract(normed_all, full_key, 1, 0))
         value_states = narrow(contract(normed_all, full_value, 1, 0) + bias_value)
@@ -445,8 +445,7 @@
             axis=1,
         )
         picked = picked.reshape(2, local * marks, 2 * width)
-        cross(3, crossed[2], picked)
-        queries = after(queries, leaving_shards[-1], sent[-1])
+        queries = after(queries, lane[-1], crossed[3])
         picked = spread_sums(picked, queries)
         key_sums = (picked[:, :, :width], picked[:, :, width:])
         (attended,) = attend(
@@ -461,14 +460,14 @@
         down_stages = fetch(3, normed_mid)
         run(down_stages)
         finish(up_stages, normed_mid)
-        mid_near, mid_far = spread_rows(normed_mid)
+        mid_near, mid_far = spread_rows(normed_mid, lane[-1])
+        run(down_stages)
         mid_far = after(mid_far, sent[-1])
         full_up = gathered[2][0]
         active = []
         for part in (mid_near, mid_far):
             part = after(part, active)
             active.append(narrow(jnp.maximum(contract(part, full_up, 1, 0) + bias_up, 0.0)))
-        run(down_stages, active)
         finish(down_stages)
         full_down = gathered[3][0]
         active_all = jnp.concatenate(active, axis=0)
@@ -505,7 +504,8 @@
         grad_branch = narrow(grad_hidden)
         branch_near, branch_far = spread_rows(grad_branch)
         run(up_stages, grad_branch)
-        branch_far = after(branch_far, sent[-1])
+        finish(down_stages, sent[-1])
+        branch_far = after(branch_far, given[0])
         branch_all = jnp.concatenate([branch_near, branch_far], axis=0)
         grad_attended = narrow(contract(branch_all, full_out, 1, 0))
         grad_pre_query, grad_keys, grad_values, key_part, value_part = attend(
@@ -518,7 +518,13 @@
             3,
             2,
         )
-        parts = collect_sums(jnp.concatenate([key_part, value_part], axis=2))
+        first_stages = scatter_weight(
+            [(branch_all, attended), (normed_all, grad_pre_query)], totals[2], grad_pre_query
+        )
+        run(first_stages)
+        finish(up_stages, sent[-1])
+        key_part, value_part = after((key_part, value_part), sent[-1])
+        parts = collect_sums(jnp.concatenate([key_part, value_part], axis=2), given[1], totals[0])
         parts = narrow(parts.reshape(-1, 2 * width))
         grad_keys = narrow(grad_keys + contract(chosen, parts[:, :width], 0, 0))
         grad_values = narrow(grad_values + contract(chosen, parts[:, width:], 0, 0))
@@ -532,17 +538,16 @@
             )
 
         normed_leaving, complete = start_collect(joined_grads, normed_part)
-        first_stages = scatter_weight(
-            [(branch_all, attended), (normed_all, grad_pre_query)], totals[2], normed_leaving
-        )
-        run(first_stages, normed_leaving)
         last_stages = scatter_weight(
-            [(normed_all, grad_keys), (normed_all, grad_values)], totals[3], sent[-1]
-        )
-        finish(down_stages, normed_leaving)
-        run(last_stages, given[0])
-        finish(up_stages, given[0])
-        grad_normed = complete(sent[-1])
+            [(normed_all, grad_keys), (normed_all, grad_values)], totals[3], normed_leaving
+        )
+        run(last_stages)
+        late = sent[-1]
+        grad_normed = complete(late)
+        run(first_stages, given[1])
+        run(last_stages, totals[1])
+        finish(first_stages, late)
+        finish(last_stages)
         first_norm, first_pull = jax.vjp(layer_norm, inputs, gain1, shift1)
         grad_input_norm, grad_gain1, grad_shift1 = first_pull(grad_normed)
         grad_tokens = grad_hidden + grad_input_norm
@@ -565,14 +570,9 @@
         cut = lines * depth // 128
         joined = to_absolute(jnp.stack(feature_rows)).reshape(-1, 128)
         joined = jnp.concatenate([joined] + [v.reshape(-1, 128) for v in head_rows])
-        turns = [first_stages, last_stages]
-        for turn, mask in enumerate(plane):
-            came = swap(joined, mask)
-            run(turns[turn % 2], given[1])
-            joined = joined + after(came, sent[-1])
+        for mask in plane:
+            joined = joined + after(swap(joined, mask), lane[-1] if mask == plane[-1] else sent[-1])
         came = swap(joined, mate)
-        finish(first_stages)
-        came = after(came, given[2])
         features = joined[:cut] + came[:cut]
         tails = [jnp.where(alike, joined[cut:], came[cut:]), jnp.where(alike, came[cut:], joined[cut:])]
         sizes = [v.shape[0] // 128 for v in head_rows]
@@ -585,11 +585,10 @@
                     offset += size
                 tails[which] = jnp.concatenate(keep) + swap(jnp.concatenate(give), mask)
             sizes = [size // 2 for size in sizes]
-        for mask in middle + [low]:
-            came = swap(features, mask)
-            finish(last_stages)
-            features = features + after(came, given[3])
+        for mask in middle:
+            features = features + swap(features, mask)
         came = swap(jnp.concatenate([features, tails[1]]), top)
+        features = features + swap(features, low) + swap(features, low | top)
         features = (features + came[:cut]).reshape(lines, depth)
         tail = tails[0] + came[cut:]
         ends = [sum(sizes[: i + 1]) for i in range(len(sizes))]

time: 816 us -> 750 us (0.919)
  waiting for transfers between devices: 419 us -> 354 us
  matrix products: 162 us -> 150 us
    ppermute x86 -> x88, waiting for transfers between devices: 419 us -> 354 us  [swap(): lax.ppermute(values, ('fsdp', 'tp'), [(i, i ^ mask) for i in range(world)])]
    dot_general x60, matrix products: 161 us -> 149 us  [contract(): lax.dot_general(left_side, right_side, (((left_dim,), (right_dim,)), ((),...]
    ppermute x86 -> x88, starting transfers between devices: 69.1 us -> 74.3 us  [swap(): lax.ppermute(values, ('fsdp', 'tp'), [(i, i ^ mask) for i in range(world)])]
    unnamed x279 -> x318, local copies, waits for them, and re-layouts: 40.3 us -> 43.3 us
  transfers between devices with their start and end apart: 86 -> 88, of which waited for: 38 -> 41; matrix products, arithmetic and copies ran while one was open for 25% -> 27% of each run, Pallas kernels for 3% -> 3%
where the time goes in v4:
time: 750 us; the launch traced here: 740 us
  waiting for transfers between devices  354 us (47%)
  matrix products  150 us (20%)
  starting transfers between devices  74.3 us (10%)
  other arithmetic  63.5 us (8%)
  local copies, waits for them, and re-layouts  62.5 us (8%)
  Pallas kernels  28.9 us (4%)
    ppermute x88, waiting for transfers between devices, swap(): lax.ppermute(values, ('fsdp', 'tp'), [(i, i ^ mask) for i in range(world)])  354 us
    dot_general x60, matrix products, contract(): lax.dot_general(left_side, right_side, (((left_dim,), (right_dim,)), ((),...  149 us
    ppermute x88, starting transfers between devices, swap(): lax.ppermute(values, ('fsdp', 'tp'), [(i, i ^ mask) for i in range(world)])  74.3 us
    unnamed x318, local copies, waits for them, and re-layouts  43.3 us
    pallas_call x2, Pallas kernels, attend(): pl.pallas_call(lambda *refs: kernel(rows, seg, *refs), grid=(width // PAI...  28.9 us
  transfers between devices with their start and end apart: 88, of which 41 were waited for; matrix products, arithmetic and copies ran while one was open for 27% of the time, Pallas kernels for 3%

profile of v4, /device:TPU:0, one launch (start us, length us, event | category | flops | bytes accessed | tf_op | source)
XLA Modules:
  0.0 740.2 jit_solution(15219758915884373044)
XLA Ops:
  44.8 10.0 %collective-permute-done.14 = bf16[256,1024]{0,1:T(8,128)(2,1)S(1)} collective-permute-done((bf16[256,1024]{0,1:T(8,128)(2,1)S(1)}, bf16[256,1024]{0,1:T(8,128)(2,1)S(1)}, u32[]{:S(2)}, u32[]{:S(2)}) %collective-permute-start.14) | collective-permute-done | bytes 524320 | tf_op jit(solution)/shard_map/ppermute | solution.py:154
  57.5 5.3 collective-permute-done.6
  70.0 15.7 %collective-permute-done.4 = bf16[256,2048]{1,0:T(8,128)(2,1)} collective-permute-done((bf16[256,2048]{1,0:T(8,128)(2,1)}, bf16[256,2048]{1,0:T(8,128)(2,1)}, u32[]{:S(2)}, u32[]{:S(2)}) %collective-permute-start.4) | collective-permute-done | bytes 1048608 | tf_op jit(solution)/shard_map/ppermute | solution.py:154
  88.9 13.8 %collective-permute-done.17 = bf16[256,1024]{0,1:T(8,128)(2,1)} collective-permute-done((bf16[256,1024]{0,1:T(8,128)(2,1)S(1)}, bf16[256,1024]{0,1:T(8,128)(2,1)}, u32[]{:S(2)}, u32[]{:S(2)}) %collective-permute-start.17) | collective-permute-done | bytes 524320 | tf_op jit(solution)/shard_map/ppermute | solution.py:154
  103.2 10.2 %collective-permute-done.19 = bf16[256,2048]{1,0:T(8,128)(2,1)} collective-permute-done((bf16[256,2048]{1,0:T(8,128)(2,1)}, bf16[256,2048]{1,0:T(8,128)(2,1)}, u32[]{:S(2)}, u32[]{:S(2)}) %collective-permute-start.19) | collective-permute-done | bytes 1048608 | tf_op jit(solution)/shard_map/ppermute | solution.py:154
  146.5 5.4 multiply_convert_fusion.refs_0_
  151.9 24.0 %collective-permute-done.27 = bf16[256,2048]{1,0:T(8,128)(2,1)S(1)} collective-permute-done((bf16[256,2048]{1,0:T(8,128)(2,1)S(1)}, bf16[256,2048]{1,0:T(8,128)(2,1)S(1)}, u32[]{:S(2)}, u32[]{:S(2)}) %collective-permute-start.27) | collective-permute-done | bytes 1048608 | tf_op jit(solution)/shard_map/ppermute | solution.py:154
  180.5 8.3 %attend_forward.1 = bf16[1024,512]{1,0:T(8,128)(2,1)} custom-call(bf16[1024,512]{1,0:T(8,128)(2,1)} %multiply_convert_fusion.refs_0_, bf16[1024,512]{1,0:T(8,128)(2,1)} %copy-done.15, bf16[1024,512]{1,0:T(8,128)(2,1)} %copy-done.14, bf16[2,128,512]{2,1,0:T(8,128)(2,1)} %get-tuple-element.336.refs_3_.refs_4_, ...), custom_call_target="tpu_custom_call" | custom-call | flops 1 | bytes 1 | tf_op jit(solution)/shard_map/attend_forward/pallas_call | solution.py:131
  200.3 21.5 %collective-permute-done.31 = bf16[256,2048]{1,0:T(8,128)(2,1)S(1)} collective-permute-done((bf16[256,2048]{1,0:T(8,128)(2,1)S(1)}, bf16[256,2048]{1,0:T(8,128)(2,1)S(1)}, u32[]{:S(2)}, u32[]{:S(2)}) %collective-permute-start.31) | collective-permute-done | bytes 1048608 | tf_op jit(solution)/shard_map/ppermute | solution.py:154
  230.6 16.4 %collective-permute-done.33 = bf16[512,2048]{1,0:T(8,128)(2,1)S(1)} collective-permute-done((bf16[512,2048]{1,0:T(8,128)(2,1)S(1)}, bf16[512,2048]{1,0:T(8,128)(2,1)S(1)}, u32[]{:S(2)}, u32[]{:S(2)}) %collective-permute-start.33) | collective-permute-done | bytes 2097184 | tf_op jit(solution)/shard_map/ppermute | solution.py:154
  249.3 19.5 %collective-permute-done.37 = bf16[256,2048]{1,0:T(8,128)(2,1)S(1)} collective-permute-done((bf16[256,2048]{1,0:T(8,128)(2,1)S(1)}, bf16[256,2048]{1,0:T(8,128)(2,1)S(1)}, u32[]{:S(2)}, u32[]{:S(2)}) %collective-permute-start.37) | collective-permute-done | bytes 1048608 | tf_op jit(solution)/shard_map/ppermute | solution.py:154
  271.5 4.7 maximum_convert_fusion.1
  277.6 4.9 maximum_convert_fusion
  282.5 33.5 %collective-permute-done.40 = bf16[512,2048]{1,0:T(8,128)(2,1)S(1)} collective-permute-done((bf16[512,2048]{1,0:T(8,128)(2,1)S(1)}, bf16[512,2048]{1,0:T(8,128)(2,1)S(1)}, u32[]{:S(2)}, u32[]{:S(2)}) %collective-permute-start.40) | collective-permute-done | bytes 2097184 | tf_op jit(solution)/shard_map/ppermute | solution.py:154
  322.2 5.7 convolution_convert_fusion.9
  335.9 5.7 convolution_convert_fusion.8
  343.3 15.5 %collective-permute-done.44 = bf16[256,2048]{1,0:T(8,128)(2,1)S(1)} collective-permute-done((bf16[256,2048]{1,0:T(8,128)(2,1)S(1)}, bf16[256,2048]{1,0:T(8,128)(2,1)S(1)}, u32[]{:S(2)}, u32[]{:S(2)}) %collective-permute-start.44) | collective-permute-done | bytes 1048608 | tf_op jit(solution)/shard_map/ppermute | solution.py:154
  358.7 7.7 %multiply_convert_fusion.1 = (bf16[256,2048]{1,0:T(8,128)(2,1)S(1)}, f32[256,2048]{1,0:T(8,128)}) fusion(f32[256]{0:T(256)S(1)} %broadcast_multiply_fusion, bf16[256,2048]{1,0:T(8,128)(2,1)S(1)} %constant_dynamic-update-slice_fusion.48, f32[2048]{0:T(1024)S(1)} %bitcast.243, f32[256,2048]{1,0:T(8,128)S(1)} %get-tuple-element.319, ...), kind=kOutput, calls=%fused_computation.117 | convolution fusion | flops 2152726528 | bytes 17835008 | tf_op jit(solution)/shard_map/dot_general | solution.py:23
  368.2 22.2 %collective-permute-done.46 = bf16[256,2048]{1,0:T(8,128)(2,1)S(1)} collective-permute-done((bf16[256,2048]{1,0:T(8,128)(2,1)S(1)}, bf16[256,2048]{1,0:T(8,128)(2,1)S(1)}, u32[]{:S(2)}, u32[]{:S(2)}) %collective-permute-start.46) | collective-permute-done | bytes 1048608 | tf_op jit(solution)/shard_map/ppermute | solution.py:154
  401.7 5.7 select_convert_fusion.1
  407.4 4.8 select_convert_fusion
  423.2 6.0 fusion.9
  438.3 6.9 convolution_convert_fusion.6
  446.7 23.6 %collective-permute-done.51 = bf16[512,2048]{1,0:T(8,128)(2,1)} collective-permute-done((bf16[512,2048]{1,0:T(8,128)(2,1)}, bf16[512,2048]{1,0:T(8,128)(2,1)}, u32[]{:S(2)}, u32[]{:S(2)}) %collective-permute-start.51) | collective-permute-done | bytes 2097184 | tf_op jit(solution)/shard_map/ppermute | solution.py:154
  485.3 6.9 multiply_reduce_fusion.1
  497.4 17.8 %collective-permute-done.58 = bf16[512,2048]{1,0:T(8,128)(2,1)} collective-permute-done((bf16[512,2048]{1,0:T(8,128)(2,1)}, bf16[512,2048]{1,0:T(8,128)(2,1)}, u32[]{:S(2)}, u32[]{:S(2)}) %collective-permute-start.58) | collective-permute-done | bytes 2097184 | tf_op jit(solution)/shard_map/ppermute | solution.py:154
  530.3 9.2 %collective-permute-done.56 = bf16[256,2048]{1,0:T(8,128)(2,1)} collective-permute-done((bf16[256,2048]{1,0:T(8,128)(2,1)}, bf16[256,2048]{1,0:T(8,128)(2,1)}, u32[]{:S(2)}, u32[]{:S(2)}) %collective-permute-start.56) | collective-permute-done | bytes 1048608 | tf_op jit(solution)/shard_map/ppermute | solution.py:154
  554.2 20.5 %attend_backward.1 = (bf16[1024,512]{1,0:T(8,128)(2,1)}, bf16[1024,512]{1,0:T(8,128)(2,1)}, bf16[1024,512]{1,0:T(8,128)(2,1)}, f32[2,128,512]{2,1,0:T(8,128)}, f32[2,128,512]{2,1,0:T(8,128)}) custom-call(bf16[1024,512]{1,0:T(8,128)(2,1)} %multiply_convert_fusion.refs_0_, bf16[1024,512]{1,0:T(8,128)(2,1)} %copy-done.15, bf16[1024,512]{1,0:T(8,128)(2,1)} %copy-done.14, ...), custom_call_target="tpu_custom_call" | custom-call | flops 1 | bytes 1 | tf_op jit(solution)/shard_map/attend_backward/pallas_call | solution.py:131
  594.7 12.2 %collective-permute-done.65 = bf16[256,2048]{1,0:T(8,128)(2,1)} collective-permute-done((bf16[256,2048]{1,0:T(8,128)(2,1)}, bf16[256,2048]{1,0:T(8,128)(2,1)}, u32[]{:S(2)}, u32[]{:S(2)}) %collective-permute-start.65) | collective-permute-done | bytes 1048608 | tf_op jit(solution)/shard_map/ppermute | solution.py:154
  645.8 11.7 %collective-permute-done.72 = bf16[256,2048]{1,0:T(8,128)(2,1)S(1)} collective-permute-done((bf16[256,2048]{1,0:T(8,128)(2,1)S(1)}, bf16[256,2048]{1,0:T(8,128)(2,1)S(1)}, u32[]{:S(2)}, u32[]{:S(2)}) %collective-permute-start.72) | collective-permute-done | bytes 1048608 | tf_op jit(solution)/shard_map/ppermute | solution.py:154
  660.6 12.9 %collective-permute-done.68 = bf16[256,2048]{1,0:T(8,128)(2,1)S(1)} collective-permute-done((bf16[256,2048]{1,0:T(8,128)(2,1)S(1)}, bf16[256,2048]{1,0:T(8,128)(2,1)S(1)}, u32[]{:S(2)}, u32[]{:S(2)}) %collective-permute-start.68) | collective-permute-done | bytes 1048608 | tf_op jit(solution)/shard_map/ppermute | solution.py:154
  716.3 20.2 %collective-permute-done.87 = bf16[256,1024]{0,1:T(8,128)(2,1)S(1)} collective-permute-done((bf16[256,1024]{0,1:T(8,128)(2,1)S(1)}, bf16[256,1024]{0,1:T(8,128)(2,1)S(1)}, u32[]{:S(2)}, u32[]{:S(2)}) %collective-permute-start.87) | collective-permute-done | bytes 524320 | tf_op jit(solution)/shard_map/ppermute | solution.py:154
  (678 shorter events, 324.8 us)
Async XLA Ops:
  10.0 34.1 %collective-permute-start.1 = (f32[1,3072]{1,0:T(1,128)S(1)}, f32[1,3072]{1,0:T(1,128)S(1)}, u32[]{:S(2)}, u32[]{:S(2)}) collective-permute-start(f32[1,3072]{1,0:T(1,128)S(1)} %bitcast.220), channel_id=1, source_target_pairs={{0,2},{1,3},{2,0},{3,1},{4,6},{5,7},{6,4},{7,5},{8,10},{9,11},{10,... | collective-permute-start | bytes 36872 | tf_op jit(solution)/shard_map/ppermute | solution.py:154
  44.1 41.6 %collective-permute-start.4 = (bf16[256,2048]{1,0:T(8,128)(2,1)}, bf16[256,2048]{1,0:T(8,128)(2,1)}, u32[]{:S(2)}, u32[]{:S(2)}) collective-permute-start(bf16[256,2048]{1,0:T(8,128)(2,1)} %fusion.15), channel_id=1, source_target_pairs={{0,1},{1,0},{2,3},{3,2},{4,5},{5,4},{6,7},{7,6},{8,9},{9,8},{10,11... | collective-permute-start | bytes 3145736 | tf_op jit(solution)/shard_map/ppermute | solution.py:154
  64.1 49.3 %collective-permute-start.19 = (bf16[256,2048]{1,0:T(8,128)(2,1)}, bf16[256,2048]{1,0:T(8,128)(2,1)}, u32[]{:S(2)}, u32[]{:S(2)}) collective-permute-start(bf16[256,2048]{1,0:T(8,128)(2,1)} %param.32), channel_id=1, source_target_pairs={{0,2},{1,3},{2,0},{3,1},{4,6},{5,7},{6,4},{7,5},{8,10},{9,11},{10,... | collective-permute-start | bytes 3145736 | tf_op jit(solution)/shard_map/ppermute | solution.py:154
  64.3 50.3 %collective-permute-start.20 = (bf16[512,1024]{0,1:T(8,128)(2,1)}, bf16[512,1024]{0,1:T(8,128)(2,1)}, u32[]{:S(2)}, u32[]{:S(2)}) collective-permute-start(bf16[512,1024]{0,1:T(8,128)(2,1)} %get-tuple-element.132), channel_id=1, source_target_pairs={{0,16},{1,17},{2,18},{3,19},{4,20},{5,21},{6,22},{7,23},{8,24},{9,... | collective-permute-start | bytes 3145736 | tf_op jit(solution)/shard_map/ppermute | solution.py:154
  65.8 48.8 %collective-permute-start.21 = (bf16[512,1024]{0,1:T(8,128)(2,1)}, bf16[512,1024]{0,1:T(8,128)(2,1)}, u32[]{:S(2)}, u32[]{:S(2)}) collective-permute-start(bf16[512,1024]{0,1:T(8,128)(2,1)} %get-tuple-element.133), channel_id=1, source_target_pairs={{0,8},{1,9},{2,10},{3,11},{4,12},{5,13},{6,14},{7,15},{8,0},{9,1},... | collective-permute-start | bytes 3145736 | tf_op jit(solution)/shard_map/ppermute | solution.py:154
  122.3 53.6 %collective-permute-start.27 = (bf16[256,2048]{1,0:T(8,128)(2,1)S(1)}, bf16[256,2048]{1,0:T(8,128)(2,1)S(1)}, u32[]{:S(2)}, u32[]{:S(2)}) collective-permute-start(bf16[256,2048]{1,0:T(8,128)(2,1)S(1)} %copy-done.39), channel_id=1, source_target_pairs={{0,2},{1,3},{2,0},{3,1},{4,6},{5,7},{6,4},{7,5},{8,10},{9,11},{10,... | collective-permute-start | bytes 3145736 | tf_op jit(solution)/shard_map/ppermute | solution.py:154
  131.6 48.0 %collective-permute-start.28 = (bf16[2,48,1024]{2,1,0:T(8,128)(2,1)S(1)}, bf16[2,48,1024]{2,1,0:T(8,128)(2,1)S(1)}, u32[]{:S(2)}, u32[]{:S(2)}) collective-permute-start(bf16[2,48,1024]{2,1,0:T(8,128)(2,1)S(1)} %bitcast.203), channel_id=1, source_target_pairs={{0,2},{1,3},{2,0},{3,1},{4,6},{5,7},{6,4},{7,5},{8,10},{9,11},{10,... | collective-permute-start | bytes 589832 | tf_op jit(solution)/shard_map/ppermute | solution.py:154
  198.4 48.6 %collective-permute-start.33 = (bf16[512,2048]{1,0:T(8,128)(2,1)S(1)}, bf16[512,2048]{1,0:T(8,128)(2,1)S(1)}, u32[]{:S(2)}, u32[]{:S(2)}) collective-permute-start(bf16[512,2048]{1,0:T(8,128)(2,1)S(1)} %pad_maximum_fusion.7), channel_id=1, source_target_pairs={{0,16},{1,17},{2,18},{3,19},{4,20},{5,21},{6,22},{7,23},{8,24},{9,... | collective-permute-start | bytes 6291464 | tf_op jit(solution)/shard_map/ppermute | solution.py:154
  199.0 48.5 %collective-permute-start.34 = (bf16[512,2048]{1,0:T(8,128)(2,1)S(1)}, bf16[512,2048]{1,0:T(8,128)(2,1)S(1)}, u32[]{:S(2)}, u32[]{:S(2)}) collective-permute-start(bf16[512,2048]{1,0:T(8,128)(2,1)S(1)} %pad_maximum_fusion.8), channel_id=1, source_target_pairs={{0,8},{1,9},{2,10},{3,11},{4,12},{5,13},{6,14},{7,15},{8,0},{9,1},... | collective-permute-start | bytes 6291464 | tf_op jit(solution)/shard_map/ppermute | solution.py:154
  225.3 46.1 %collective-permute-start.35 = (bf16[256,2048]{1,0:T(8,128)(2,1)S(1)}, bf16[256,2048]{1,0:T(8,128)(2,1)S(1)}, u32[]{:S(2)}, u32[]{:S(2)}) collective-permute-start(bf16[256,2048]{1,0:T(8,128)(2,1)S(1)} %add_convert_fusion.3), channel_id=1, source_target_pairs={{0,1},{1,0},{2,3},{3,2},{4,5},{5,4},{6,7},{7,6},{8,9},{9,8},{10,11... | collective-permute-start | bytes 3145736 | tf_op jit(solution)/shard_map/ppermute | solution.py:154
  229.0 39.8 %collective-permute-start.37 = (bf16[256,2048]{1,0:T(8,128)(2,1)S(1)}, bf16[256,2048]{1,0:T(8,128)(2,1)S(1)}, u32[]{:S(2)}, u32[]{:S(2)}) collective-permute-start(bf16[256,2048]{1,0:T(8,128)(2,1)S(1)} %get-tuple-element.161), channel_id=1, source_target_pairs={{0,8},{1,9},{2,10},{3,11},{4,12},{5,13},{6,14},{7,15},{8,0},{9,1},... | collective-permute-start | bytes 3145736 | tf_op jit(solution)/shard_map/ppermute | solution.py:154
  229.6 39.3 %collective-permute-start.38 = (bf16[256,2048]{1,0:T(8,128)(2,1)S(1)}, bf16[256,2048]{1,0:T(8,128)(2,1)S(1)}, u32[]{:S(2)}, u32[]{:S(2)}) collective-permute-start(bf16[256,2048]{1,0:T(8,128)(2,1)S(1)} %get-tuple-element.162), channel_id=1, source_target_pairs={{0,16},{1,17},{2,18},{3,19},{4,20},{5,21},{6,22},{7,23},{8,24},{9,... | collective-permute-start | bytes 3145736 | tf_op jit(solution)/shard_map/ppermute | solution.py:154
  269.3 46.6 %collective-permute-start.40 = (bf16[512,2048]{1,0:T(8,128)(2,1)S(1)}, bf16[512,2048]{1,0:T(8,128)(2,1)S(1)}, u32[]{:S(2)}, u32[]{:S(2)}) collective-permute-start(bf16[512,2048]{1,0:T(8,128)(2,1)S(1)} %pad_maximum_fusion.11), channel_id=1, source_target_pairs={{0,16},{1,17},{2,18},{3,19},{4,20},{5,21},{6,22},{7,23},{8,24},{9,... | collective-permute-start | bytes 6291464 | tf_op jit(solution)/shard_map/ppermute | solution.py:154
  270.9 46.3 %collective-permute-start.41 = (bf16[512,2048]{1,0:T(8,128)(2,1)S(1)}, bf16[512,2048]{1,0:T(8,128)(2,1)S(1)}, u32[]{:S(2)}, u32[]{:S(2)}) collective-permute-start(bf16[512,2048]{1,0:T(8,128)(2,1)S(1)} %pad_maximum_fusion.12), channel_id=1, source_target_pairs={{0,8},{1,9},{2,10},{3,11},{4,12},{5,13},{6,14},{7,15},{8,0},{9,1},... | collective-permute-start | bytes 6291464 | tf_op jit(solution)/shard_map/ppermute | solution.py:154
  421.4 48.9 %collective-permute-start.51 = (bf16[512,2048]{1,0:T(8,128)(2,1)}, bf16[512,2048]{1,0:T(8,128)(2,1)}, u32[]{:S(2)}, u32[]{:S(2)}) collective-permute-start(bf16[512,2048]{1,0:T(8,128)(2,1)} %convolution_convert_fusion.3), channel_id=1, source_target_pairs={{0,16},{1,17},{2,18},{3,19},{4,20},{5,21},{6,22},{7,23},{8,24},{9,... | collective-permute-start | bytes 6291464 | tf_op jit(solution)/shard_map/ppermute | solution.py:154
  422.1 48.8 %collective-permute-start.52 = (bf16[512,2048]{1,0:T(8,128)(2,1)}, bf16[512,2048]{1,0:T(8,128)(2,1)}, u32[]{:S(2)}, u32[]{:S(2)}) collective-permute-start(bf16[512,2048]{1,0:T(8,128)(2,1)} %convolution_convert_fusion.2), channel_id=1, source_target_pairs={{0,8},{1,9},{2,10},{3,11},{4,12},{5,13},{6,14},{7,15},{8,0},{9,1},... | collective-permute-start | bytes 6291464 | tf_op jit(solution)/shard_map/ppermute | solution.py:154
  429.2 55.5 %collective-permute-start.50 = (bf16[256,2048]{1,0:T(8,128)(2,1)S(1)}, bf16[256,2048]{1,0:T(8,128)(2,1)S(1)}, u32[]{:S(2)}, u32[]{:S(2)}) collective-permute-start(bf16[256,2048]{1,0:T(8,128)(2,1)S(1)} %fusion.9), channel_id=1, source_target_pairs={{0,1},{1,0},{2,3},{3,2},{4,5},{5,4},{6,7},{7,6},{8,9},{9,8},{10,11... | collective-permute-start | bytes 3145736 | tf_op jit(solution)/shard_map/ppermute | solution.py:154
  445.2 40.1 %collective-permute-start.49 = (bf16[256,2048]{1,0:T(8,128)(2,1)}, bf16[256,2048]{1,0:T(8,128)(2,1)}, u32[]{:S(2)}, u32[]{:S(2)}) collective-permute-start(bf16[256,2048]{1,0:T(8,128)(2,1)} %convolution_convert_fusion.6), channel_id=1, source_target_pairs={{0,4},{1,5},{2,6},{3,7},{4,0},{5,1},{6,2},{7,3},{8,12},{9,13},{10,... | collective-permute-start | bytes 3145736 | tf_op jit(solution)/shard_map/ppermute | solution.py:154
  445.3 70.0 %collective-permute-start.58 = (bf16[512,2048]{1,0:T(8,128)(2,1)}, bf16[512,2048]{1,0:T(8,128)(2,1)}, u32[]{:S(2)}, u32[]{:S(2)}) collective-permute-start(bf16[512,2048]{1,0:T(8,128)(2,1)} %convolution_convert_fusion.1), channel_id=1, source_target_pairs={{0,16},{1,17},{2,18},{3,19},{4,20},{5,21},{6,22},{7,23},{8,24},{9,... | collective-permute-start | bytes 6291464 | tf_op jit(solution)/shard_map/ppermute | solution.py:154
  470.3 48.8 %collective-permute-start.59 = (bf16[512,2048]{1,0:T(8,128)(2,1)}, bf16[512,2048]{1,0:T(8,128)(2,1)}, u32[]{:S(2)}, u32[]{:S(2)}) collective-permute-start(bf16[512,2048]{1,0:T(8,128)(2,1)} %convolution_convert_fusion), channel_id=1, source_target_pairs={{0,8},{1,9},{2,10},{3,11},{4,12},{5,13},{6,14},{7,15},{8,0},{9,1},... | collective-permute-start | bytes 6291464 | tf_op jit(solution)/shard_map/ppermute | solution.py:154
  483.2 56.3 %collective-permute-start.56 = (bf16[256,2048]{1,0:T(8,128)(2,1)}, bf16[256,2048]{1,0:T(8,128)(2,1)}, u32[]{:S(2)}, u32[]{:S(2)}) collective-permute-start(bf16[256,2048]{1,0:T(8,128)(2,1)} %slice.709), channel_id=1, source_target_pairs={{0,8},{1,9},{2,10},{3,11},{4,12},{5,13},{6,14},{7,15},{8,0},{9,1},... | collective-permute-start | bytes 3145736 | tf_op jit(solution)/shard_map/ppermute | solution.py:154
  484.7 54.8 %collective-permute-start.57 = (bf16[256,2048]{1,0:T(8,128)(2,1)}, bf16[256,2048]{1,0:T(8,128)(2,1)}, u32[]{:S(2)}, u32[]{:S(2)}) collective-permute-start(bf16[256,2048]{1,0:T(8,128)(2,1)} %slice.708), channel_id=1, source_target_pairs={{0,16},{1,17},{2,18},{3,19},{4,20},{5,21},{6,22},{7,23},{8,24},{9,... | collective-permute-start | bytes 3145736 | tf_op jit(solution)/shard_map/ppermute | solution.py:154
  495.9 47.7 %collective-permute-start.54 = (bf16[256,2048]{1,0:T(8,128)(2,1)S(1)}, bf16[256,2048]{1,0:T(8,128)(2,1)S(1)}, u32[]{:S(2)}, u32[]{:S(2)}) collective-permute-start(bf16[256,2048]{1,0:T(8,128)(2,1)S(1)} %convert_element_type.348), channel_id=1, source_target_pairs={{0,1},{1,0},{2,3},{3,2},{4,5},{5,4},{6,7},{7,6},{8,9},{9,8},{10,11... | collective-permute-start | bytes 3145736 | tf_op jit(solution)/shard_map/ppermute | solution.py:154
  543.8 43.3 %collective-permute-start.62 = (bf16[256,2048]{1,0:T(8,128)(2,1)}, bf16[256,2048]{1,0:T(8,128)(2,1)}, u32[]{:S(2)}, u32[]{:S(2)}) collective-permute-start(bf16[256,2048]{1,0:T(8,128)(2,1)} %slice.707), channel_id=1, source_target_pairs={{0,8},{1,9},{2,10},{3,11},{4,12},{5,13},{6,14},{7,15},{8,0},{9,1},... | collective-permute-start | bytes 3145736 | tf_op jit(solution)/shard_map/ppermute | solution.py:154
  544.4 44.5 %collective-permute-start.63 = (bf16[256,2048]{1,0:T(8,128)(2,1)}, bf16[256,2048]{1,0:T(8,128)(2,1)}, u32[]{:S(2)}, u32[]{:S(2)}) collective-permute-start(bf16[256,2048]{1,0:T(8,128)(2,1)} %slice.706), channel_id=1, source_target_pairs={{0,16},{1,17},{2,18},{3,19},{4,20},{5,21},{6,22},{7,23},{8,24},{9,... | collective-permute-start | bytes 3145736 | tf_op jit(solution)/shard_map/ppermute | solution.py:154
  553.0 53.9 %collective-permute-start.65 = (bf16[256,2048]{1,0:T(8,128)(2,1)}, bf16[256,2048]{1,0:T(8,128)(2,1)}, u32[]{:S(2)}, u32[]{:S(2)}) collective-permute-start(bf16[256,2048]{1,0:T(8,128)(2,1)} %broadcast_select_fusion.3), channel_id=1, source_target_pairs={{0,2},{1,3},{2,0},{3,1},{4,6},{5,7},{6,4},{7,5},{8,10},{9,11},{10,... | collective-permute-start | bytes 3145736 | tf_op jit(solution)/shard_map/ppermute | solution.py:154
  583.5 35.4 %collective-permute-start.80 = (bf16[512,1024]{0,1:T(8,128)(2,1)S(1)}, bf16[512,1024]{0,1:T(8,128)(2,1)S(1)}, u32[]{:S(2)}, u32[]{:S(2)}) collective-permute-start(bf16[512,1024]{0,1:T(8,128)(2,1)S(1)} %maximum_bitcast_fusion.4), channel_id=1, source_target_pairs={{0,16},{1,17},{2,18},{3,19},{4,20},{5,21},{6,22},{7,23},{8,24},{9,... | collective-permute-start | bytes 3145736 | tf_op jit(solution)/shard_map/ppermute | solution.py:154
  585.5 33.5 %collective-permute-start.81 = (bf16[512,1024]{0,1:T(8,128)(2,1)S(1)}, bf16[512,1024]{0,1:T(8,128)(2,1)S(1)}, u32[]{:S(2)}, u32[]{:S(2)}) collective-permute-start(bf16[512,1024]{0,1:T(8,128)(2,1)S(1)} %maximum_bitcast_fusion.5), channel_id=1, source_target_pairs={{0,8},{1,9},{2,10},{3,11},{4,12},{5,13},{6,14},{7,15},{8,0},{9,1},... | collective-permute-start | bytes 3145736 | tf_op jit(solution)/shard_map/ppermute | solution.py:154
  611.9 45.6 %collective-permute-start.72 = (bf16[256,2048]{1,0:T(8,128)(2,1)S(1)}, bf16[256,2048]{1,0:T(8,128)(2,1)S(1)}, u32[]{:S(2)}, u32[]{:S(2)}) collective-permute-start(bf16[256,2048]{1,0:T(8,128)(2,1)S(1)} %broadcast_select_fusion.2), channel_id=1, source_target_pairs={{0,2},{1,3},{2,0},{3,1},{4,6},{5,7},{6,4},{7,5},{8,10},{9,11},{10,... | collective-permute-start | bytes 3145736 | tf_op jit(solution)/shard_map/ppermute | solution.py:154
  626.0 47.5 %collective-permute-start.68 = (bf16[256,2048]{1,0:T(8,128)(2,1)S(1)}, bf16[256,2048]{1,0:T(8,128)(2,1)S(1)}, u32[]{:S(2)}, u32[]{:S(2)}) collective-permute-start(bf16[256,2048]{1,0:T(8,128)(2,1)S(1)} %add_convert_fusion), channel_id=1, source_target_pairs={{0,1},{1,0},{2,3},{3,2},{4,5},{5,4},{6,7},{7,6},{8,9},{9,8},{10,11... | collective-permute-start | bytes 3145736 | tf_op jit(solution)/shard_map/ppermute | solution.py:154
  637.0 41.2 %collective-permute-start.70 = (bf16[512,1024]{0,1:T(8,128)(2,1)}, bf16[512,1024]{0,1:T(8,128)(2,1)}, u32[]{:S(2)}, u32[]{:S(2)}) collective-permute-start(bf16[512,1024]{0,1:T(8,128)(2,1)} %maximum_bitcast_fusion.6), channel_id=1, source_target_pairs={{0,16},{1,17},{2,18},{3,19},{4,20},{5,21},{6,22},{7,23},{8,24},{9,... | collective-permute-start | bytes 3145736 | tf_op jit(solution)/shard_map/ppermute | solution.py:154
  640.0 38.1 %collective-permute-start.71 = (bf16[512,1024]{0,1:T(8,128)(2,1)}, bf16[512,1024]{0,1:T(8,128)(2,1)}, u32[]{:S(2)}, u32[]{:S(2)}) collective-permute-start(bf16[512,1024]{0,1:T(8,128)(2,1)} %maximum_bitcast_fusion.7), channel_id=1, source_target_pairs={{0,8},{1,9},{2,10},{3,11},{4,12},{5,13},{6,14},{7,15},{8,0},{9,1},... | collective-permute-start | bytes 3145736 | tf_op jit(solution)/shard_map/ppermute | solution.py:154
  (183 other events, 2397.2 us)

commit v5 on v4

--- a/solution.py
+++ b/solution.py
@@ -445,24 +445,24 @@
             axis=1,
         )
         picked = picked.reshape(2, local * marks, 2 * width)
-        queries = after(queries, lane[-1], crossed[3])
+        run(up_stages)
+        down_stages = fetch(3, sent[-1])
+        run(down_stages)
+        queries, normed_all = after((queries, normed_all), sent[-1])
+        up_came = lane[-2]
         picked = spread_sums(picked, queries)
         key_sums = (picked[:, :, :width], picked[:, :, width:])
         (attended,) = attend(
             forward_kernel, rows, seg, (queries, key_states, value_states), key_sums, seen, 1, 0
         )
-        leaving, complete = start_collect(attended, lambda block: contract(block, full_out, 1, 1))
-        run(up_stages, leaving)
+        leaving, complete = start_collect(after(attended, up_came), lambda block: contract(block, full_out, 1, 1))
+        run(down_stages, leaving)
         branch = complete(sent[-1])
         hidden = inputs + branch + bias_out
 
         normed_mid = narrow(layer_norm(hidden, gain2, shift2))
-        down_stages = fetch(3, normed_mid)
-        run(down_stages)
         finish(up_stages, normed_mid)
-        mid_near, mid_far = spread_rows(normed_mid, lane[-1])
-        run(down_stages)
-        mid_far = after(mid_far, sent[-1])
+        mid_near, mid_far = spread_rows(normed_mid)
         full_up = gathered[2][0]
         active = []
         for part in (mid_near, mid_far):
@@ -587,6 +587,7 @@
             sizes = [size // 2 for size in sizes]
         for mask in middle:
             features = features + swap(features, mask)
+        features, tails = after((features, tails), given[3])
         came = swap(jnp.concatenate([features, tails[1]]), top)
         features = features + swap(features, low) + swap(features, low | top)
         features = (features + came[:cut]).reshape(lines, depth)

time: 750 us -> 745 us (level)
  waiting for transfers between devices: 354 us -> 317 us
  other arithmetic: 63.5 us -> 74 us
  starting transfers between devices: 74.3 us -> 83.8 us
  matrix products: 150 us -> 159 us
    ppermute x88, waiting for transfers between devices: 354 us -> 317 us  [swap(): lax.ppermute(values, ('fsdp', 'tp'), [(i, i ^ mask) for i in range(world)])]
    ppermute x88, starting transfers between devices: 74.3 us -> 83.8 us  [swap(): lax.ppermute(values, ('fsdp', 'tp'), [(i, i ^ mask) for i in range(world)])]
    dot_general x60, matrix products: 149 us -> 159 us  [contract(): lax.dot_general(left_side, right_side, (((left_dim,), (right_dim,)), ((),...]
    unnamed x318 -> x298, local copies, waits for them, and re-layouts: 43.3 us -> 43.8 us
  transfers between devices with their start and end apart: 88 -> 88, of which waited for: 41 -> 39; matrix products, arithmetic and copies ran while one was open for 27% -> 30% of each run, Pallas kernels for 3% -> 4%
where the time goes in v5:
time: 745 us; the launch traced here: 735 us
  waiting for transfers between devices  317 us (43%)
  matrix products  159 us (21%)
  starting transfers between devices  83.8 us (11%)
  other arithmetic  74 us (10%)
  local copies, waits for them, and re-layouts  64.3 us (9%)
  Pallas kernels  29 us (4%)
    ppermute x88, waiting for transfers between devices, swap(): lax.ppermute(values, ('fsdp', 'tp'), [(i, i ^ mask) for i in range(world)])  317 us
    dot_general x60, matrix products, contract(): lax.dot_general(left_side, right_side, (((left_dim,), (right_dim,)), ((),...  159 us
    ppermute x88, starting transfers between devices, swap(): lax.ppermute(values, ('fsdp', 'tp'), [(i, i ^ mask) for i in range(world)])  83.8 us
    unnamed x298, local copies, waits for them, and re-layouts  43.8 us
    pallas_call x2, Pallas kernels, attend(): pl.pallas_call(lambda *refs: kernel(rows, seg, *refs), grid=(width // PAI...  29 us
  transfers between devices with their start and end apart: 88, of which 39 were waited for; matrix products, arithmetic and copies ran while one was open for 30% of the time, Pallas kernels for 4%

profile of v5, /device:TPU:0, one launch (start us, length us, event | category | flops | bytes accessed | tf_op | source)
XLA Modules:
  0.0 734.5 jit_solution(2506785666969253765)
XLA Ops:
  44.8 10.0 %collective-permute-done.14 = bf16[256,1024]{0,1:T(8,128)(2,1)S(1)} collective-permute-done((bf16[256,1024]{0,1:T(8,128)(2,1)S(1)}, bf16[256,1024]{0,1:T(8,128)(2,1)S(1)}, u32[]{:S(2)}, u32[]{:S(2)}) %collective-permute-start.14) | collective-permute-done | bytes 524320 | tf_op jit(solution)/shard_map/ppermute | solution.py:154
  57.5 5.3 collective-permute-done.6
  70.0 15.6 %collective-permute-done.4 = bf16[256,2048]{1,0:T(8,128)(2,1)} collective-permute-done((bf16[256,2048]{1,0:T(8,128)(2,1)}, bf16[256,2048]{1,0:T(8,128)(2,1)}, u32[]{:S(2)}, u32[]{:S(2)}) %collective-permute-start.4) | collective-permute-done | bytes 1048608 | tf_op jit(solution)/shard_map/ppermute | solution.py:154
  88.9 13.8 %collective-permute-done.17 = bf16[256,1024]{0,1:T(8,128)(2,1)} collective-permute-done((bf16[256,1024]{0,1:T(8,128)(2,1)S(1)}, bf16[256,1024]{0,1:T(8,128)(2,1)}, u32[]{:S(2)}, u32[]{:S(2)}) %collective-permute-start.17) | collective-permute-done | bytes 524320 | tf_op jit(solution)/shard_map/ppermute | solution.py:154
  103.2 10.2 %collective-permute-done.19 = bf16[256,2048]{1,0:T(8,128)(2,1)} collective-permute-done((bf16[256,2048]{1,0:T(8,128)(2,1)}, bf16[256,2048]{1,0:T(8,128)(2,1)}, u32[]{:S(2)}, u32[]{:S(2)}) %collective-permute-start.19) | collective-permute-done | bytes 1048608 | tf_op jit(solution)/shard_map/ppermute | solution.py:154
  138.8 8.1 %pad_maximum_fusion = bf16[1024,2048]{1,0:T(8,128)(2,1)} fusion(bf16[256,2048]{1,0:T(8,128)(2,1)S(1)} %collective-permute-done.5, bf16[256,2048]{1,0:T(8,128)(2,1)} %collective-permute-done.4, bf16[256,2048]{1,0:T(8,128)(2,1)S(1)} %collective-permute-done.3, bf16[256,2048]{1,0:T(8,128)(2,1)S(1)} %copy-done.44), kind=kLoop, calls=%fused_computation.1 | loop fusion | flops 16777216 | bytes 8388608 | tf_op jit(solution)/shard_map/concatenate | solution.py:438
  151.3 11.8 %collective-permute-done.26 = bf16[256,2048]{1,0:T(8,128)(2,1)S(1)} collective-permute-done((bf16[256,2048]{1,0:T(8,128)(2,1)S(1)}, bf16[256,2048]{1,0:T(8,128)(2,1)S(1)}, u32[]{:S(2)}, u32[]{:S(2)}) %collective-permute-start.26) | collective-permute-done | bytes 1048608 | tf_op jit(solution)/shard_map/ppermute | solution.py:154
  170.3 5.3 multiply_convert_fusion.refs_0_
  178.8 8.5 %attend_forward.1 = bf16[1024,512]{1,0:T(8,128)(2,1)} custom-call(bf16[1024,512]{1,0:T(8,128)(2,1)} %multiply_convert_fusion.refs_0_, bf16[1024,512]{1,0:T(8,128)(2,1)} %copy-done.14, bf16[1024,512]{1,0:T(8,128)(2,1)} %copy-done.13, bf16[2,128,512]{2,1,0:T(8,128)(2,1)} %get-tuple-element.342.refs_3_.refs_4_, ...), custom_call_target="tpu_custom_call" | custom-call | flops 1 | bytes 1 | tf_op jit(solution)/shard_map/attend_forward/pallas_call | solution.py:131
  187.3 26.5 %collective-permute-done.30 = bf16[512,2048]{1,0:T(8,128)(2,1)} collective-permute-done((bf16[512,2048]{1,0:T(8,128)(2,1)}, bf16[512,2048]{1,0:T(8,128)(2,1)}, u32[]{:S(2)}, u32[]{:S(2)}) %collective-permute-start.30) | collective-permute-done | bytes 2097184 | tf_op jit(solution)/shard_map/ppermute | solution.py:154
  224.7 17.7 %collective-permute-done.35 = bf16[256,2048]{1,0:T(8,128)(2,1)S(1)} collective-permute-done((bf16[256,2048]{1,0:T(8,128)(2,1)}, bf16[256,2048]{1,0:T(8,128)(2,1)S(1)}, u32[]{:S(2)}, u32[]{:S(2)}) %collective-permute-start.35) | collective-permute-done | bytes 1048608 | tf_op jit(solution)/shard_map/ppermute | solution.py:154
  258.5 18.2 %collective-permute-done.38 = bf16[256,2048]{1,0:T(8,128)(2,1)S(1)} collective-permute-done((bf16[256,2048]{1,0:T(8,128)(2,1)S(1)}, bf16[256,2048]{1,0:T(8,128)(2,1)S(1)}, u32[]{:S(2)}, u32[]{:S(2)}) %collective-permute-start.38) | collective-permute-done | bytes 1048608 | tf_op jit(solution)/shard_map/ppermute | solution.py:154
  282.5 9.8 %collective-permute-done.40 = bf16[512,2048]{1,0:T(8,128)(2,1)S(1)} collective-permute-done((bf16[512,2048]{1,0:T(8,128)(2,1)S(1)}, bf16[512,2048]{1,0:T(8,128)(2,1)S(1)}, u32[]{:S(2)}, u32[]{:S(2)}) %collective-permute-start.40) | collective-permute-done | bytes 2097184 | tf_op jit(solution)/shard_map/ppermute | solution.py:154
  304.8 6.5 convolution_convert_fusion.9
  314.0 5.8 fusion.8
  323.5 5.7 convolution_convert_fusion.8
  330.8 16.1 %collective-permute-done.44 = bf16[256,2048]{1,0:T(8,128)(2,1)S(1)} collective-permute-done((bf16[256,2048]{1,0:T(8,128)(2,1)S(1)}, bf16[256,2048]{1,0:T(8,128)(2,1)S(1)}, u32[]{:S(2)}, u32[]{:S(2)}) %collective-permute-start.44) | collective-permute-done | bytes 1048608 | tf_op jit(solution)/shard_map/ppermute | solution.py:154
  346.9 7.7 %multiply_convert_fusion.1 = (bf16[256,2048]{1,0:T(8,128)(2,1)S(1)}, f32[256,2048]{1,0:T(8,128)}) fusion(f32[256]{0:T(256)S(1)} %broadcast_multiply_fusion, bf16[256,2048]{1,0:T(8,128)(2,1)S(1)} %constant_dynamic-update-slice_fusion.48, f32[2048]{0:T(1024)S(1)} %bitcast.239, f32[256,2048]{1,0:T(8,128)S(1)} %get-tuple-element.323, ...), kind=kOutput, calls=%fused_computation.118 | convolution fusion | flops 2152726528 | bytes 17835008 | tf_op jit(solution)/shard_map/dot_general | solution.py:23
  356.4 22.9 %collective-permute-done.46 = bf16[256,2048]{1,0:T(8,128)(2,1)S(1)} collective-permute-done((bf16[256,2048]{1,0:T(8,128)(2,1)S(1)}, bf16[256,2048]{1,0:T(8,128)(2,1)S(1)}, u32[]{:S(2)}, u32[]{:S(2)}) %collective-permute-start.46) | collective-permute-done | bytes 1048608 | tf_op jit(solution)/shard_map/ppermute | solution.py:154
  390.7 9.4 %select_convert_fusion.1 = bf16[512,2048]{1,0:T(8,128)(2,1)} fusion(bf16[512,2048]{1,0:T(8,128)(2,1)S(1)} %maximum_convert_fusion.1, bf16[512,2048]{1,0:T(8,128)(2,1)S(1)} %pad_maximum_fusion.13, bf16[2048,2048]{1,0:T(8,128)(2,1)} %constant_dynamic-update-slice_fusion.34), kind=kOutput, calls=%fused_computation.12 | convolution fusion | flops 4298113024 | bytes 14680064 | tf_op jit(solution)/shard_map/dot_general | solution.py:23
  400.0 8.4 %select_convert_fusion = bf16[512,2048]{1,0:T(8,128)(2,1)S(1)} fusion(bf16[512,2048]{1,0:T(8,128)(2,1)S(1)} %maximum_convert_fusion, bf16[512,2048]{1,0:T(8,128)(2,1)S(1)} %pad_maximum_fusion.14, bf16[2048,2048]{1,0:T(8,128)(2,1)} %constant_dynamic-update-slice_fusion.34), kind=kOutput, calls=%fused_computation.11 | convolution fusion | flops 4298113024 | bytes 14680064 | tf_op jit(solution)/shard_map/dot_general | solution.py:23
  416.7 6.0 fusion.9
  431.8 6.9 convolution_convert_fusion.6
  440.2 23.7 %collective-permute-done.51 = bf16[512,2048]{1,0:T(8,128)(2,1)} collective-permute-done((bf16[512,2048]{1,0:T(8,128)(2,1)}, bf16[512,2048]{1,0:T(8,128)(2,1)}, u32[]{:S(2)}, u32[]{:S(2)}) %collective-permute-start.51) | collective-permute-done | bytes 2097184 | tf_op jit(solution)/shard_map/ppermute | solution.py:154
  478.9 6.9 multiply_reduce_fusion.1
  491.1 17.8 %collective-permute-done.58 = bf16[512,2048]{1,0:T(8,128)(2,1)} collective-permute-done((bf16[512,2048]{1,0:T(8,128)(2,1)}, bf16[512,2048]{1,0:T(8,128)(2,1)}, u32[]{:S(2)}, u32[]{:S(2)}) %collective-permute-start.58) | collective-permute-done | bytes 2097184 | tf_op jit(solution)/shard_map/ppermute | solution.py:154
  523.9 9.2 %collective-permute-done.56 = bf16[256,2048]{1,0:T(8,128)(2,1)} collective-permute-done((bf16[256,2048]{1,0:T(8,128)(2,1)}, bf16[256,2048]{1,0:T(8,128)(2,1)}, u32[]{:S(2)}, u32[]{:S(2)}) %collective-permute-start.56) | collective-permute-done | bytes 1048608 | tf_op jit(solution)/shard_map/ppermute | solution.py:154
  547.5 20.5 %attend_backward.1 = (bf16[1024,512]{1,0:T(8,128)(2,1)}, bf16[1024,512]{1,0:T(8,128)(2,1)}, bf16[1024,512]{1,0:T(8,128)(2,1)}, f32[2,128,512]{2,1,0:T(8,128)}, f32[2,128,512]{2,1,0:T(8,128)}) custom-call(bf16[1024,512]{1,0:T(8,128)(2,1)} %multiply_convert_fusion.refs_0_, bf16[1024,512]{1,0:T(8,128)(2,1)} %copy-done.14, bf16[1024,512]{1,0:T(8,128)(2,1)} %copy-done.13, ...), custom_call_target="tpu_custom_call" | custom-call | flops 1 | bytes 1 | tf_op jit(solution)/shard_map/attend_backward/pallas_call | solution.py:131
  588.3 12.5 %collective-permute-done.65 = bf16[256,2048]{1,0:T(8,128)(2,1)} collective-permute-done((bf16[256,2048]{1,0:T(8,128)(2,1)}, bf16[256,2048]{1,0:T(8,128)(2,1)}, u32[]{:S(2)}, u32[]{:S(2)}) %collective-permute-start.65) | collective-permute-done | bytes 1048608 | tf_op jit(solution)/shard_map/ppermute | solution.py:154
  639.5 13.1 %collective-permute-done.72 = bf16[256,2048]{1,0:T(8,128)(2,1)S(1)} collective-permute-done((bf16[256,2048]{1,0:T(8,128)(2,1)S(1)}, bf16[256,2048]{1,0:T(8,128)(2,1)S(1)}, u32[]{:S(2)}, u32[]{:S(2)}) %collective-permute-start.72) | collective-permute-done | bytes 1048608 | tf_op jit(solution)/shard_map/ppermute | solution.py:154
  655.7 11.6 %collective-permute-done.68 = bf16[256,2048]{1,0:T(8,128)(2,1)S(1)} collective-permute-done((bf16[256,2048]{1,0:T(8,128)(2,1)S(1)}, bf16[256,2048]{1,0:T(8,128)(2,1)S(1)}, u32[]{:S(2)}, u32[]{:S(2)}) %collective-permute-start.68) | collective-permute-done | bytes 1048608 | tf_op jit(solution)/shard_map/ppermute | solution.py:154
  711.2 19.5 %collective-permute-done.87 = bf16[256,1024]{0,1:T(8,128)(2,1)S(1)} collective-permute-done((bf16[256,1024]{0,1:T(8,128)(2,1)}, bf16[256,1024]{0,1:T(8,128)(2,1)S(1)}, u32[]{:S(2)}, u32[]{:S(2)}) %collective-permute-start.87) | collective-permute-done | bytes 524320 | tf_op jit(solution)/shard_map/ppermute | solution.py:154
  (657 shorter events, 336.6 us)
Async XLA Ops:
  10.0 34.1 %collective-permute-start.1 = (f32[1,3072]{1,0:T(1,128)S(1)}, f32[1,3072]{1,0:T(1,128)S(1)}, u32[]{:S(2)}, u32[]{:S(2)}) collective-permute-start(f32[1,3072]{1,0:T(1,128)S(1)} %bitcast.216), channel_id=1, source_target_pairs={{0,2},{1,3},{2,0},{3,1},{4,6},{5,7},{6,4},{7,5},{8,10},{9,11},{10,... | collective-permute-start | bytes 36872 | tf_op jit(solution)/shard_map/ppermute | solution.py:154
  44.1 41.6 %collective-permute-start.4 = (bf16[256,2048]{1,0:T(8,128)(2,1)}, bf16[256,2048]{1,0:T(8,128)(2,1)}, u32[]{:S(2)}, u32[]{:S(2)}) collective-permute-start(bf16[256,2048]{1,0:T(8,128)(2,1)} %fusion.16), channel_id=1, source_target_pairs={{0,1},{1,0},{2,3},{3,2},{4,5},{5,4},{6,7},{7,6},{8,9},{9,8},{10,11... | collective-permute-start | bytes 3145736 | tf_op jit(solution)/shard_map/ppermute | solution.py:154
  64.1 49.3 %collective-permute-start.19 = (bf16[256,2048]{1,0:T(8,128)(2,1)}, bf16[256,2048]{1,0:T(8,128)(2,1)}, u32[]{:S(2)}, u32[]{:S(2)}) collective-permute-start(bf16[256,2048]{1,0:T(8,128)(2,1)} %param.32), channel_id=1, source_target_pairs={{0,2},{1,3},{2,0},{3,1},{4,6},{5,7},{6,4},{7,5},{8,10},{9,11},{10,... | collective-permute-start | bytes 3145736 | tf_op jit(solution)/shard_map/ppermute | solution.py:154
  64.3 50.3 %collective-permute-start.20 = (bf16[512,1024]{0,1:T(8,128)(2,1)}, bf16[512,1024]{0,1:T(8,128)(2,1)}, u32[]{:S(2)}, u32[]{:S(2)}) collective-permute-start(bf16[512,1024]{0,1:T(8,128)(2,1)} %get-tuple-element.135), channel_id=1, source_target_pairs={{0,16},{1,17},{2,18},{3,19},{4,20},{5,21},{6,22},{7,23},{8,24},{9,... | collective-permute-start | bytes 3145736 | tf_op jit(solution)/shard_map/ppermute | solution.py:154
  65.8 48.8 %collective-permute-start.21 = (bf16[512,1024]{0,1:T(8,128)(2,1)}, bf16[512,1024]{0,1:T(8,128)(2,1)}, u32[]{:S(2)}, u32[]{:S(2)}) collective-permute-start(bf16[512,1024]{0,1:T(8,128)(2,1)} %get-tuple-element.136), channel_id=1, source_target_pairs={{0,8},{1,9},{2,10},{3,11},{4,12},{5,13},{6,14},{7,15},{8,0},{9,1},... | collective-permute-start | bytes 3145736 | tf_op jit(solution)/shard_map/ppermute | solution.py:154
  69.5 33.2 %collective-permute-start.17 = (bf16[256,1024]{0,1:T(8,128)(2,1)S(1)}, bf16[256,1024]{0,1:T(8,128)(2,1)}, u32[]{:S(2)}, u32[]{:S(2)}) collective-permute-start(bf16[256,1024]{0,1:T(8,128)(2,1)S(1)} %get-tuple-element.138), channel_id=1, source_target_pairs={{0,8},{1,9},{2,10},{3,11},{4,12},{5,13},{6,14},{7,15},{8,0},{9,1},... | collective-permute-start | bytes 1572872 | tf_op jit(solution)/shard_map/ppermute | solution.py:154
  114.6 33.4 %collective-permute-start.22 = (bf16[512,1024]{0,1:T(8,128)(2,1)S(1)}, bf16[512,1024]{0,1:T(8,128)(2,1)S(1)}, u32[]{:S(2)}, u32[]{:S(2)}) collective-permute-start(bf16[512,1024]{0,1:T(8,128)(2,1)S(1)} %pad_maximum_fusion.18), channel_id=1, source_target_pairs={{0,16},{1,17},{2,18},{3,19},{4,20},{5,21},{6,22},{7,23},{8,24},{9,... | collective-permute-start | bytes 3145736 | tf_op jit(solution)/shard_map/ppermute | solution.py:154
  116.2 34.8 %collective-permute-start.23 = (bf16[512,1024]{0,1:T(8,128)(2,1)S(1)}, bf16[512,1024]{0,1:T(8,128)(2,1)S(1)}, u32[]{:S(2)}, u32[]{:S(2)}) collective-permute-start(bf16[512,1024]{0,1:T(8,128)(2,1)S(1)} %pad_maximum_fusion.19), channel_id=1, source_target_pairs={{0,8},{1,9},{2,10},{3,11},{4,12},{5,13},{6,14},{7,15},{8,0},{9,1},... | collective-permute-start | bytes 3145736 | tf_op jit(solution)/shard_map/ppermute | solution.py:154
  117.7 52.2 %collective-permute-start.24 = (bf16[256,2048]{1,0:T(8,128)(2,1)S(1)}, bf16[256,2048]{1,0:T(8,128)(2,1)S(1)}, u32[]{:S(2)}, u32[]{:S(2)}) collective-permute-start(bf16[256,2048]{1,0:T(8,128)(2,1)S(1)} %copy-done.38), channel_id=1, source_target_pairs={{0,2},{1,3},{2,0},{3,1},{4,6},{5,7},{6,4},{7,5},{8,10},{9,11},{10,... | collective-permute-start | bytes 3145736 | tf_op jit(solution)/shard_map/ppermute | solution.py:154
  166.3 47.6 %collective-permute-start.30 = (bf16[512,2048]{1,0:T(8,128)(2,1)}, bf16[512,2048]{1,0:T(8,128)(2,1)}, u32[]{:S(2)}, u32[]{:S(2)}) collective-permute-start(bf16[512,2048]{1,0:T(8,128)(2,1)} %pad_maximum_fusion.7), channel_id=1, source_target_pairs={{0,16},{1,17},{2,18},{3,19},{4,20},{5,21},{6,22},{7,23},{8,24},{9,... | collective-permute-start | bytes 6291464 | tf_op jit(solution)/shard_map/ppermute | solution.py:154
  166.8 47.3 %collective-permute-start.31 = (bf16[512,2048]{1,0:T(8,128)(2,1)}, bf16[512,2048]{1,0:T(8,128)(2,1)}, u32[]{:S(2)}, u32[]{:S(2)}) collective-permute-start(bf16[512,2048]{1,0:T(8,128)(2,1)} %pad_maximum_fusion.8), channel_id=1, source_target_pairs={{0,8},{1,9},{2,10},{3,11},{4,12},{5,13},{6,14},{7,15},{8,0},{9,1},... | collective-permute-start | bytes 6291464 | tf_op jit(solution)/shard_map/ppermute | solution.py:154
  244.2 48.1 %collective-permute-start.40 = (bf16[512,2048]{1,0:T(8,128)(2,1)S(1)}, bf16[512,2048]{1,0:T(8,128)(2,1)S(1)}, u32[]{:S(2)}, u32[]{:S(2)}) collective-permute-start(bf16[512,2048]{1,0:T(8,128)(2,1)S(1)} %pad_maximum_fusion.9), channel_id=1, source_target_pairs={{0,16},{1,17},{2,18},{3,19},{4,20},{5,21},{6,22},{7,23},{8,24},{9,... | collective-permute-start | bytes 6291464 | tf_op jit(solution)/shard_map/ppermute | solution.py:154
  245.8 47.7 %collective-permute-start.41 = (bf16[512,2048]{1,0:T(8,128)(2,1)S(1)}, bf16[512,2048]{1,0:T(8,128)(2,1)S(1)}, u32[]{:S(2)}, u32[]{:S(2)}) collective-permute-start(bf16[512,2048]{1,0:T(8,128)(2,1)S(1)} %pad_maximum_fusion.10), channel_id=1, source_target_pairs={{0,8},{1,9},{2,10},{3,11},{4,12},{5,13},{6,14},{7,15},{8,0},{9,1},... | collective-permute-start | bytes 6291464 | tf_op jit(solution)/shard_map/ppermute | solution.py:154
  415.0 48.9 %collective-permute-start.51 = (bf16[512,2048]{1,0:T(8,128)(2,1)}, bf16[512,2048]{1,0:T(8,128)(2,1)}, u32[]{:S(2)}, u32[]{:S(2)}) collective-permute-start(bf16[512,2048]{1,0:T(8,128)(2,1)} %convolution_convert_fusion.3), channel_id=1, source_target_pairs={{0,16},{1,17},{2,18},{3,19},{4,20},{5,21},{6,22},{7,23},{8,24},{9,... | collective-permute-start | bytes 6291464 | tf_op jit(solution)/shard_map/ppermute | solution.py:154
  415.6 48.9 %collective-permute-start.52 = (bf16[512,2048]{1,0:T(8,128)(2,1)}, bf16[512,2048]{1,0:T(8,128)(2,1)}, u32[]{:S(2)}, u32[]{:S(2)}) collective-permute-start(bf16[512,2048]{1,0:T(8,128)(2,1)} %convolution_convert_fusion.2), channel_id=1, source_target_pairs={{0,8},{1,9},{2,10},{3,11},{4,12},{5,13},{6,14},{7,15},{8,0},{9,1},... | collective-permute-start | bytes 6291464 | tf_op jit(solution)/shard_map/ppermute | solution.py:154
  422.7 55.6 %collective-permute-start.50 = (bf16[256,2048]{1,0:T(8,128)(2,1)S(1)}, bf16[256,2048]{1,0:T(8,128)(2,1)S(1)}, u32[]{:S(2)}, u32[]{:S(2)}) collective-permute-start(bf16[256,2048]{1,0:T(8,128)(2,1)S(1)} %fusion.9), channel_id=1, source_target_pairs={{0,1},{1,0},{2,3},{3,2},{4,5},{5,4},{6,7},{7,6},{8,9},{9,8},{10,11... | collective-permute-start | bytes 3145736 | tf_op jit(solution)/shard_map/ppermute | solution.py:154
  438.7 40.2 %collective-permute-start.49 = (bf16[256,2048]{1,0:T(8,128)(2,1)}, bf16[256,2048]{1,0:T(8,128)(2,1)}, u32[]{:S(2)}, u32[]{:S(2)}) collective-permute-start(bf16[256,2048]{1,0:T(8,128)(2,1)} %convolution_convert_fusion.6), channel_id=1, source_target_pairs={{0,4},{1,5},{2,6},{3,7},{4,0},{5,1},{6,2},{7,3},{8,12},{9,13},{10,... | collective-permute-start | bytes 3145736 | tf_op jit(solution)/shard_map/ppermute | solution.py:154
  438.7 70.1 %collective-permute-start.58 = (bf16[512,2048]{1,0:T(8,128)(2,1)}, bf16[512,2048]{1,0:T(8,128)(2,1)}, u32[]{:S(2)}, u32[]{:S(2)}) collective-permute-start(bf16[512,2048]{1,0:T(8,128)(2,1)} %convolution_convert_fusion.1), channel_id=1, source_target_pairs={{0,16},{1,17},{2,18},{3,19},{4,20},{5,21},{6,22},{7,23},{8,24},{9,... | collective-permute-start | bytes 6291464 | tf_op jit(solution)/shard_map/ppermute | solution.py:154
  463.9 48.8 %collective-permute-start.59 = (bf16[512,2048]{1,0:T(8,128)(2,1)}, bf16[512,2048]{1,0:T(8,128)(2,1)}, u32[]{:S(2)}, u32[]{:S(2)}) collective-permute-start(bf16[512,2048]{1,0:T(8,128)(2,1)} %convolution_convert_fusion), channel_id=1, source_target_pairs={{0,8},{1,9},{2,10},{3,11},{4,12},{5,13},{6,14},{7,15},{8,0},{9,1},... | collective-permute-start | bytes 6291464 | tf_op jit(solution)/shard_map/ppermute | solution.py:154
  476.9 56.2 %collective-permute-start.56 = (bf16[256,2048]{1,0:T(8,128)(2,1)}, bf16[256,2048]{1,0:T(8,128)(2,1)}, u32[]{:S(2)}, u32[]{:S(2)}) collective-permute-start(bf16[256,2048]{1,0:T(8,128)(2,1)} %slice.705), channel_id=1, source_target_pairs={{0,8},{1,9},{2,10},{3,11},{4,12},{5,13},{6,14},{7,15},{8,0},{9,1},... | collective-permute-start | bytes 3145736 | tf_op jit(solution)/shard_map/ppermute | solution.py:154
  478.4 54.8 %collective-permute-start.57 = (bf16[256,2048]{1,0:T(8,128)(2,1)}, bf16[256,2048]{1,0:T(8,128)(2,1)}, u32[]{:S(2)}, u32[]{:S(2)}) collective-permute-start(bf16[256,2048]{1,0:T(8,128)(2,1)} %slice.704), channel_id=1, source_target_pairs={{0,16},{1,17},{2,18},{3,19},{4,20},{5,21},{6,22},{7,23},{8,24},{9,... | collective-permute-start | bytes 3145736 | tf_op jit(solution)/shard_map/ppermute | solution.py:154
  489.5 47.8 %collective-permute-start.54 = (bf16[256,2048]{1,0:T(8,128)(2,1)S(1)}, bf16[256,2048]{1,0:T(8,128)(2,1)S(1)}, u32[]{:S(2)}, u32[]{:S(2)}) collective-permute-start(bf16[256,2048]{1,0:T(8,128)(2,1)S(1)} %convert_element_type.348), channel_id=1, source_target_pairs={{0,1},{1,0},{2,3},{3,2},{4,5},{5,4},{6,7},{7,6},{8,9},{9,8},{10,11... | collective-permute-start | bytes 3145736 | tf_op jit(solution)/shard_map/ppermute | solution.py:154
  537.6 42.8 %collective-permute-start.62 = (bf16[256,2048]{1,0:T(8,128)(2,1)}, bf16[256,2048]{1,0:T(8,128)(2,1)}, u32[]{:S(2)}, u32[]{:S(2)}) collective-permute-start(bf16[256,2048]{1,0:T(8,128)(2,1)} %slice.703), channel_id=1, source_target_pairs={{0,8},{1,9},{2,10},{3,11},{4,12},{5,13},{6,14},{7,15},{8,0},{9,1},... | collective-permute-start | bytes 3145736 | tf_op jit(solution)/shard_map/ppermute | solution.py:154
  538.2 44.2 %collective-permute-start.63 = (bf16[256,2048]{1,0:T(8,128)(2,1)}, bf16[256,2048]{1,0:T(8,128)(2,1)}, u32[]{:S(2)}, u32[]{:S(2)}) collective-permute-start(bf16[256,2048]{1,0:T(8,128)(2,1)} %slice.702), channel_id=1, source_target_pairs={{0,16},{1,17},{2,18},{3,19},{4,20},{5,21},{6,22},{7,23},{8,24},{9,... | collective-permute-start | bytes 3145736 | tf_op jit(solution)/shard_map/ppermute | solution.py:154
  546.8 54.0 %collective-permute-start.65 = (bf16[256,2048]{1,0:T(8,128)(2,1)}, bf16[256,2048]{1,0:T(8,128)(2,1)}, u32[]{:S(2)}, u32[]{:S(2)}) collective-permute-start(bf16[256,2048]{1,0:T(8,128)(2,1)} %broadcast_select_fusion.3), channel_id=1, source_target_pairs={{0,2},{1,3},{2,0},{3,1},{4,6},{5,7},{6,4},{7,5},{8,10},{9,11},{10,... | collective-permute-start | bytes 3145736 | tf_op jit(solution)/shard_map/ppermute | solution.py:154
  576.6 36.1 %collective-permute-start.81 = (bf16[512,1024]{0,1:T(8,128)(2,1)S(1)}, bf16[512,1024]{0,1:T(8,128)(2,1)S(1)}, u32[]{:S(2)}, u32[]{:S(2)}) collective-permute-start(bf16[512,1024]{0,1:T(8,128)(2,1)S(1)} %maximum_bitcast_fusion.4), channel_id=1, source_target_pairs={{0,16},{1,17},{2,18},{3,19},{4,20},{5,21},{6,22},{7,23},{8,24},{9,... | collective-permute-start | bytes 3145736 | tf_op jit(solution)/shard_map/ppermute | solution.py:154
  578.7 34.0 %collective-permute-start.82 = (bf16[512,1024]{0,1:T(8,128)(2,1)S(1)}, bf16[512,1024]{0,1:T(8,128)(2,1)S(1)}, u32[]{:S(2)}, u32[]{:S(2)}) collective-permute-start(bf16[512,1024]{0,1:T(8,128)(2,1)S(1)} %maximum_bitcast_fusion.5), channel_id=1, source_target_pairs={{0,8},{1,9},{2,10},{3,11},{4,12},{5,13},{6,14},{7,15},{8,0},{9,1},... | collective-permute-start | bytes 3145736 | tf_op jit(solution)/shard_map/ppermute | solution.py:154
  605.7 46.8 %collective-permute-start.72 = (bf16[256,2048]{1,0:T(8,128)(2,1)S(1)}, bf16[256,2048]{1,0:T(8,128)(2,1)S(1)}, u32[]{:S(2)}, u32[]{:S(2)}) collective-permute-start(bf16[256,2048]{1,0:T(8,128)(2,1)S(1)} %broadcast_select_fusion.2), channel_id=1, source_target_pairs={{0,2},{1,3},{2,0},{3,1},{4,6},{5,7},{6,4},{7,5},{8,10},{9,11},{10,... | collective-permute-start | bytes 3145736 | tf_op jit(solution)/shard_map/ppermute | solution.py:154
  619.8 47.5 %collective-permute-start.68 = (bf16[256,2048]{1,0:T(8,128)(2,1)S(1)}, bf16[256,2048]{1,0:T(8,128)(2,1)S(1)}, u32[]{:S(2)}, u32[]{:S(2)}) collective-permute-start(bf16[256,2048]{1,0:T(8,128)(2,1)S(1)} %add_convert_fusion), channel_id=1, source_target_pairs={{0,1},{1,0},{2,3},{3,2},{4,5},{5,4},{6,7},{7,6},{8,9},{9,8},{10,11... | collective-permute-start | bytes 3145736 | tf_op jit(solution)/shard_map/ppermute | solution.py:154
  630.5 41.6 %collective-permute-start.70 = (bf16[512,1024]{0,1:T(8,128)(2,1)}, bf16[512,1024]{0,1:T(8,128)(2,1)}, u32[]{:S(2)}, u32[]{:S(2)}) collective-permute-start(bf16[512,1024]{0,1:T(8,128)(2,1)} %maximum_bitcast_fusion.6), channel_id=1, source_target_pairs={{0,16},{1,17},{2,18},{3,19},{4,20},{5,21},{6,22},{7,23},{8,24},{9,... | collective-permute-start | bytes 3145736 | tf_op jit(solution)/shard_map/ppermute | solution.py:154
  633.5 38.6 %collective-permute-start.71 = (bf16[512,1024]{0,1:T(8,128)(2,1)}, bf16[512,1024]{0,1:T(8,128)(2,1)}, u32[]{:S(2)}, u32[]{:S(2)}) collective-permute-start(bf16[512,1024]{0,1:T(8,128)(2,1)} %maximum_bitcast_fusion.7), channel_id=1, source_target_pairs={{0,8},{1,9},{2,10},{3,11},{4,12},{5,13},{6,14},{7,15},{8,0},{9,1},... | collective-permute-start | bytes 3145736 | tf_op jit(solution)/shard_map/ppermute | solution.py:154
  636.1 31.2 %collective-permute-start.67 = (bf16[256,2048]{1,0:T(8,128)(2,1)S(1)}, bf16[256,2048]{1,0:T(8,128)(2,1)S(1)}, u32[]{:S(2)}, u32[]{:S(2)}) collective-permute-start(bf16[256,2048]{1,0:T(8,128)(2,1)S(1)} %fusion.12), channel_id=1, source_target_pairs={{0,4},{1,5},{2,6},{3,7},{4,0},{5,1},{6,2},{7,3},{8,12},{9,13},{10,... | collective-permute-start | bytes 3145736 | tf_op jit(solution)/shard_map/ppermute | solution.py:154
  (173 other events, 2429.4 us)

commit v6 on v5

--- a/solution.py
+++ b/solution.py
@@ -468,7 +468,7 @@
         for part in (mid_near, mid_far):
             part = after(part, active)
             active.append(narrow(jnp.maximum(contract(part, full_up, 1, 0) + bias_up, 0.0)))
-        finish(down_stages)
+        finish(down_stages, active)
         full_down = gathered[3][0]
         active_all = jnp.concatenate(active, axis=0)
         mid_all = jnp.concatenate([mid_near, mid_far], axis=0)

time: 745 us -> 738 us (level)
  no operation moved by 1% of the time
where the time goes in v6:
time: 738 us; the launch traced here: 728 us
  waiting for transfers between devices  311 us (42%)
  matrix products  158 us (21%)
  starting transfers between devices  84.2 us (11%)
  other arithmetic  73.9 us (10%)
  local copies, waits for them, and re-layouts  64.1 us (9%)
  Pallas kernels  29 us (4%)
    ppermute x88, waiting for transfers between devices, swap(): lax.ppermute(values, ('fsdp', 'tp'), [(i, i ^ mask) for i in range(world)])  311 us
    dot_general x60, matrix products, contract(): lax.dot_general(left_side, right_side, (((left_dim,), (right_dim,)), ((),...  158 us
    ppermute x88, starting transfers between devices, swap(): lax.ppermute(values, ('fsdp', 'tp'), [(i, i ^ mask) for i in range(world)])  84.2 us
    unnamed x298, local copies, waits for them, and re-layouts  43.6 us
    pallas_call x2, Pallas kernels, attend(): pl.pallas_call(lambda *refs: kernel(rows, seg, *refs), grid=(width // PAI...  29 us
  transfers between devices with their start and end apart: 88, of which 39 were waited for; matrix products, arithmetic and copies ran while one was open for 30% of the time, Pallas kernels for 4%

profile of v6, /device:TPU:0, one launch (start us, length us, event | category | flops | bytes accessed | tf_op | source)
XLA Modules:
  0.0 728.0 jit_solution(3349690888996311696)
XLA Ops:
  44.8 10.0 %collective-permute-done.14 = bf16[256,1024]{0,1:T(8,128)(2,1)S(1)} collective-permute-done((bf16[256,1024]{0,1:T(8,128)(2,1)S(1)}, bf16[256,1024]{0,1:T(8,128)(2,1)S(1)}, u32[]{:S(2)}, u32[]{:S(2)}) %collective-permute-start.14) | collective-permute-done | bytes 524320 | tf_op jit(solution)/shard_map/ppermute | solution.py:154
  57.5 5.3 collective-permute-done.6
  70.0 15.6 %collective-permute-done.4 = bf16[256,2048]{1,0:T(8,128)(2,1)} collective-permute-done((bf16[256,2048]{1,0:T(8,128)(2,1)}, bf16[256,2048]{1,0:T(8,128)(2,1)}, u32[]{:S(2)}, u32[]{:S(2)}) %collective-permute-start.4) | collective-permute-done | bytes 1048608 | tf_op jit(solution)/shard_map/ppermute | solution.py:154
  88.9 13.8 %collective-permute-done.17 = bf16[256,1024]{0,1:T(8,128)(2,1)} collective-permute-done((bf16[256,1024]{0,1:T(8,128)(2,1)S(1)}, bf16[256,1024]{0,1:T(8,128)(2,1)}, u32[]{:S(2)}, u32[]{:S(2)}) %collective-permute-start.17) | collective-permute-done | bytes 524320 | tf_op jit(solution)/shard_map/ppermute | solution.py:154
  103.2 10.2 %collective-permute-done.19 = bf16[256,2048]{1,0:T(8,128)(2,1)} collective-permute-done((bf16[256,2048]{1,0:T(8,128)(2,1)}, bf16[256,2048]{1,0:T(8,128)(2,1)}, u32[]{:S(2)}, u32[]{:S(2)}) %collective-permute-start.19) | collective-permute-done | bytes 1048608 | tf_op jit(solution)/shard_map/ppermute | solution.py:154
  138.8 8.1 %pad_maximum_fusion = bf16[1024,2048]{1,0:T(8,128)(2,1)} fusion(bf16[256,2048]{1,0:T(8,128)(2,1)S(1)} %collective-permute-done.5, bf16[256,2048]{1,0:T(8,128)(2,1)} %collective-permute-done.4, bf16[256,2048]{1,0:T(8,128)(2,1)S(1)} %collective-permute-done.3, bf16[256,2048]{1,0:T(8,128)(2,1)S(1)} %copy-done.44), kind=kLoop, calls=%fused_computation.1 | loop fusion | flops 16777216 | bytes 8388608 | tf_op jit(solution)/shard_map/concatenate | solution.py:438
  151.3 11.8 %collective-permute-done.26 = bf16[256,2048]{1,0:T(8,128)(2,1)S(1)} collective-permute-done((bf16[256,2048]{1,0:T(8,128)(2,1)S(1)}, bf16[256,2048]{1,0:T(8,128)(2,1)S(1)}, u32[]{:S(2)}, u32[]{:S(2)}) %collective-permute-start.26) | collective-permute-done | bytes 1048608 | tf_op jit(solution)/shard_map/ppermute | solution.py:154
  170.3 5.3 multiply_convert_fusion.refs_0_
  178.8 8.5 %attend_forward.1 = bf16[1024,512]{1,0:T(8,128)(2,1)} custom-call(bf16[1024,512]{1,0:T(8,128)(2,1)} %multiply_convert_fusion.refs_0_, bf16[1024,512]{1,0:T(8,128)(2,1)} %copy-done.14, bf16[1024,512]{1,0:T(8,128)(2,1)} %copy-done.13, bf16[2,128,512]{2,1,0:T(8,128)(2,1)} %get-tuple-element.342.refs_3_.refs_4_, ...), custom_call_target="tpu_custom_call" | custom-call | flops 1 | bytes 1 | tf_op jit(solution)/shard_map/attend_forward/pallas_call | solution.py:131
  187.3 26.7 %collective-permute-done.30 = bf16[512,2048]{1,0:T(8,128)(2,1)} collective-permute-done((bf16[512,2048]{1,0:T(8,128)(2,1)}, bf16[512,2048]{1,0:T(8,128)(2,1)}, u32[]{:S(2)}, u32[]{:S(2)}) %collective-permute-start.30) | collective-permute-done | bytes 2097184 | tf_op jit(solution)/shard_map/ppermute | solution.py:154
  224.8 17.7 %collective-permute-done.35 = bf16[256,2048]{1,0:T(8,128)(2,1)S(1)} collective-permute-done((bf16[256,2048]{1,0:T(8,128)(2,1)}, bf16[256,2048]{1,0:T(8,128)(2,1)S(1)}, u32[]{:S(2)}, u32[]{:S(2)}) %collective-permute-start.35) | collective-permute-done | bytes 1048608 | tf_op jit(solution)/shard_map/ppermute | solution.py:154
  259.7 17.8 %collective-permute-done.38 = bf16[256,2048]{1,0:T(8,128)(2,1)S(1)} collective-permute-done((bf16[256,2048]{1,0:T(8,128)(2,1)S(1)}, bf16[256,2048]{1,0:T(8,128)(2,1)S(1)}, u32[]{:S(2)}, u32[]{:S(2)}) %collective-permute-start.38) | collective-permute-done | bytes 1048608 | tf_op jit(solution)/shard_map/ppermute | solution.py:154
  283.3 5.0 maximum_convert_fusion
  299.0 5.7 convolution_convert_fusion.9
  307.4 5.8 fusion.8
  316.9 5.7 convolution_convert_fusion.8
  324.2 16.1 %collective-permute-done.44 = bf16[256,2048]{1,0:T(8,128)(2,1)S(1)} collective-permute-done((bf16[256,2048]{1,0:T(8,128)(2,1)S(1)}, bf16[256,2048]{1,0:T(8,128)(2,1)S(1)}, u32[]{:S(2)}, u32[]{:S(2)}) %collective-permute-start.44) | collective-permute-done | bytes 1048608 | tf_op jit(solution)/shard_map/ppermute | solution.py:154
  340.3 7.7 %multiply_convert_fusion.1 = (bf16[256,2048]{1,0:T(8,128)(2,1)S(1)}, f32[256,2048]{1,0:T(8,128)}) fusion(f32[256]{0:T(256)S(1)} %broadcast_multiply_fusion, bf16[256,2048]{1,0:T(8,128)(2,1)S(1)} %constant_dynamic-update-slice_fusion.48, f32[2048]{0:T(1024)S(1)} %bitcast.239, f32[256,2048]{1,0:T(8,128)S(1)} %get-tuple-element.323, ...), kind=kOutput, calls=%fused_computation.118 | convolution fusion | flops 2152726528 | bytes 17835008 | tf_op jit(solution)/shard_map/dot_general | solution.py:23
  349.8 22.9 %collective-permute-done.46 = bf16[256,2048]{1,0:T(8,128)(2,1)S(1)} collective-permute-done((bf16[256,2048]{1,0:T(8,128)(2,1)S(1)}, bf16[256,2048]{1,0:T(8,128)(2,1)S(1)}, u32[]{:S(2)}, u32[]{:S(2)}) %collective-permute-start.46) | collective-permute-done | bytes 1048608 | tf_op jit(solution)/shard_map/ppermute | solution.py:154
  384.1 9.4 %select_convert_fusion.1 = bf16[512,2048]{1,0:T(8,128)(2,1)} fusion(bf16[512,2048]{1,0:T(8,128)(2,1)S(1)} %maximum_convert_fusion.1, bf16[512,2048]{1,0:T(8,128)(2,1)S(1)} %pad_maximum_fusion.13, bf16[2048,2048]{1,0:T(8,128)(2,1)} %constant_dynamic-update-slice_fusion.34), kind=kOutput, calls=%fused_computation.12 | convolution fusion | flops 4298113024 | bytes 14680064 | tf_op jit(solution)/shard_map/dot_general | solution.py:23
  393.5 8.4 %select_convert_fusion = bf16[512,2048]{1,0:T(8,128)(2,1)S(1)} fusion(bf16[512,2048]{1,0:T(8,128)(2,1)S(1)} %maximum_convert_fusion, bf16[512,2048]{1,0:T(8,128)(2,1)S(1)} %pad_maximum_fusion.14, bf16[2048,2048]{1,0:T(8,128)(2,1)} %constant_dynamic-update-slice_fusion.34), kind=kOutput, calls=%fused_computation.11 | convolution fusion | flops 4298113024 | bytes 14680064 | tf_op jit(solution)/shard_map/dot_general | solution.py:23
  410.1 6.0 fusion.9
  425.2 6.9 convolution_convert_fusion.6
  433.7 23.7 %collective-permute-done.51 = bf16[512,2048]{1,0:T(8,128)(2,1)} collective-permute-done((bf16[512,2048]{1,0:T(8,128)(2,1)}, bf16[512,2048]{1,0:T(8,128)(2,1)}, u32[]{:S(2)}, u32[]{:S(2)}) %collective-permute-start.51) | collective-permute-done | bytes 2097184 | tf_op jit(solution)/shard_map/ppermute | solution.py:154
  472.3 6.9 multiply_reduce_fusion.1
  484.5 17.8 %collective-permute-done.58 = bf16[512,2048]{1,0:T(8,128)(2,1)} collective-permute-done((bf16[512,2048]{1,0:T(8,128)(2,1)}, bf16[512,2048]{1,0:T(8,128)(2,1)}, u32[]{:S(2)}, u32[]{:S(2)}) %collective-permute-start.58) | collective-permute-done | bytes 2097184 | tf_op jit(solution)/shard_map/ppermute | solution.py:154
  517.3 9.2 %collective-permute-done.56 = bf16[256,2048]{1,0:T(8,128)(2,1)} collective-permute-done((bf16[256,2048]{1,0:T(8,128)(2,1)}, bf16[256,2048]{1,0:T(8,128)(2,1)}, u32[]{:S(2)}, u32[]{:S(2)}) %collective-permute-start.56) | collective-permute-done | bytes 1048608 | tf_op jit(solution)/shard_map/ppermute | solution.py:154
  541.1 20.5 %attend_backward.1 = (bf16[1024,512]{1,0:T(8,128)(2,1)}, bf16[1024,512]{1,0:T(8,128)(2,1)}, bf16[1024,512]{1,0:T(8,128)(2,1)}, f32[2,128,512]{2,1,0:T(8,128)}, f32[2,128,512]{2,1,0:T(8,128)}) custom-call(bf16[1024,512]{1,0:T(8,128)(2,1)} %multiply_convert_fusion.refs_0_, bf16[1024,512]{1,0:T(8,128)(2,1)} %copy-done.14, bf16[1024,512]{1,0:T(8,128)(2,1)} %copy-done.13, ...), custom_call_target="tpu_custom_call" | custom-call | flops 1 | bytes 1 | tf_op jit(solution)/shard_map/attend_backward/pallas_call | solution.py:131
  581.7 12.3 %collective-permute-done.65 = bf16[256,2048]{1,0:T(8,128)(2,1)} collective-permute-done((bf16[256,2048]{1,0:T(8,128)(2,1)}, bf16[256,2048]{1,0:T(8,128)(2,1)}, u32[]{:S(2)}, u32[]{:S(2)}) %collective-permute-start.65) | collective-permute-done | bytes 1048608 | tf_op jit(solution)/shard_map/ppermute | solution.py:154
  632.9 13.1 %collective-permute-done.72 = bf16[256,2048]{1,0:T(8,128)(2,1)S(1)} collective-permute-done((bf16[256,2048]{1,0:T(8,128)(2,1)S(1)}, bf16[256,2048]{1,0:T(8,128)(2,1)S(1)}, u32[]{:S(2)}, u32[]{:S(2)}) %collective-permute-start.72) | collective-permute-done | bytes 1048608 | tf_op jit(solution)/shard_map/ppermute | solution.py:154
  649.1 11.6 %collective-permute-done.68 = bf16[256,2048]{1,0:T(8,128)(2,1)S(1)} collective-permute-done((bf16[256,2048]{1,0:T(8,128)(2,1)S(1)}, bf16[256,2048]{1,0:T(8,128)(2,1)S(1)}, u32[]{:S(2)}, u32[]{:S(2)}) %collective-permute-start.68) | collective-permute-done | bytes 1048608 | tf_op jit(solution)/shard_map/ppermute | solution.py:154
  704.6 19.5 %collective-permute-done.87 = bf16[256,1024]{0,1:T(8,128)(2,1)S(1)} collective-permute-done((bf16[256,1024]{0,1:T(8,128)(2,1)}, bf16[256,1024]{0,1:T(8,128)(2,1)S(1)}, u32[]{:S(2)}, u32[]{:S(2)}) %collective-permute-start.87) | collective-permute-done | bytes 524320 | tf_op jit(solution)/shard_map/ppermute | solution.py:154
  (657 shorter events, 336.0 us)
Async XLA Ops:
  10.0 34.1 %collective-permute-start.1 = (f32[1,3072]{1,0:T(1,128)S(1)}, f32[1,3072]{1,0:T(1,128)S(1)}, u32[]{:S(2)}, u32[]{:S(2)}) collective-permute-start(f32[1,3072]{1,0:T(1,128)S(1)} %bitcast.216), channel_id=1, source_target_pairs={{0,2},{1,3},{2,0},{3,1},{4,6},{5,7},{6,4},{7,5},{8,10},{9,11},{10,... | collective-permute-start | bytes 36872 | tf_op jit(solution)/shard_map/ppermute | solution.py:154
  44.1 41.6 %collective-permute-start.4 = (bf16[256,2048]{1,0:T(8,128)(2,1)}, bf16[256,2048]{1,0:T(8,128)(2,1)}, u32[]{:S(2)}, u32[]{:S(2)}) collective-permute-start(bf16[256,2048]{1,0:T(8,128)(2,1)} %fusion.16), channel_id=1, source_target_pairs={{0,1},{1,0},{2,3},{3,2},{4,5},{5,4},{6,7},{7,6},{8,9},{9,8},{10,11... | collective-permute-start | bytes 3145736 | tf_op jit(solution)/shard_map/ppermute | solution.py:154
  64.1 49.3 %collective-permute-start.19 = (bf16[256,2048]{1,0:T(8,128)(2,1)}, bf16[256,2048]{1,0:T(8,128)(2,1)}, u32[]{:S(2)}, u32[]{:S(2)}) collective-permute-start(bf16[256,2048]{1,0:T(8,128)(2,1)} %param.32), channel_id=1, source_target_pairs={{0,2},{1,3},{2,0},{3,1},{4,6},{5,7},{6,4},{7,5},{8,10},{9,11},{10,... | collective-permute-start | bytes 3145736 | tf_op jit(solution)/shard_map/ppermute | solution.py:154
  64.3 50.3 %collective-permute-start.20 = (bf16[512,1024]{0,1:T(8,128)(2,1)}, bf16[512,1024]{0,1:T(8,128)(2,1)}, u32[]{:S(2)}, u32[]{:S(2)}) collective-permute-start(bf16[512,1024]{0,1:T(8,128)(2,1)} %get-tuple-element.135), channel_id=1, source_target_pairs={{0,16},{1,17},{2,18},{3,19},{4,20},{5,21},{6,22},{7,23},{8,24},{9,... | collective-permute-start | bytes 3145736 | tf_op jit(solution)/shard_map/ppermute | solution.py:154
  65.8 48.8 %collective-permute-start.21 = (bf16[512,1024]{0,1:T(8,128)(2,1)}, bf16[512,1024]{0,1:T(8,128)(2,1)}, u32[]{:S(2)}, u32[]{:S(2)}) collective-permute-start(bf16[512,1024]{0,1:T(8,128)(2,1)} %get-tuple-element.136), channel_id=1, source_target_pairs={{0,8},{1,9},{2,10},{3,11},{4,12},{5,13},{6,14},{7,15},{8,0},{9,1},... | collective-permute-start | bytes 3145736 | tf_op jit(solution)/shard_map/ppermute | solution.py:154
  69.5 33.2 %collective-permute-start.17 = (bf16[256,1024]{0,1:T(8,128)(2,1)S(1)}, bf16[256,1024]{0,1:T(8,128)(2,1)}, u32[]{:S(2)}, u32[]{:S(2)}) collective-permute-start(bf16[256,1024]{0,1:T(8,128)(2,1)S(1)} %get-tuple-element.138), channel_id=1, source_target_pairs={{0,8},{1,9},{2,10},{3,11},{4,12},{5,13},{6,14},{7,15},{8,0},{9,1},... | collective-permute-start | bytes 1572872 | tf_op jit(solution)/shard_map/ppermute | solution.py:154
  114.6 33.4 %collective-permute-start.22 = (bf16[512,1024]{0,1:T(8,128)(2,1)S(1)}, bf16[512,1024]{0,1:T(8,128)(2,1)S(1)}, u32[]{:S(2)}, u32[]{:S(2)}) collective-permute-start(bf16[512,1024]{0,1:T(8,128)(2,1)S(1)} %pad_maximum_fusion.18), channel_id=1, source_target_pairs={{0,16},{1,17},{2,18},{3,19},{4,20},{5,21},{6,22},{7,23},{8,24},{9,... | collective-permute-start | bytes 3145736 | tf_op jit(solution)/shard_map/ppermute | solution.py:154
  116.2 34.8 %collective-permute-start.23 = (bf16[512,1024]{0,1:T(8,128)(2,1)S(1)}, bf16[512,1024]{0,1:T(8,128)(2,1)S(1)}, u32[]{:S(2)}, u32[]{:S(2)}) collective-permute-start(bf16[512,1024]{0,1:T(8,128)(2,1)S(1)} %pad_maximum_fusion.19), channel_id=1, source_target_pairs={{0,8},{1,9},{2,10},{3,11},{4,12},{5,13},{6,14},{7,15},{8,0},{9,1},... | collective-permute-start | bytes 3145736 | tf_op jit(solution)/shard_map/ppermute | solution.py:154
  117.7 52.2 %collective-permute-start.24 = (bf16[256,2048]{1,0:T(8,128)(2,1)S(1)}, bf16[256,2048]{1,0:T(8,128)(2,1)S(1)}, u32[]{:S(2)}, u32[]{:S(2)}) collective-permute-start(bf16[256,2048]{1,0:T(8,128)(2,1)S(1)} %copy-done.38), channel_id=1, source_target_pairs={{0,2},{1,3},{2,0},{3,1},{4,6},{5,7},{6,4},{7,5},{8,10},{9,11},{10,... | collective-permute-start | bytes 3145736 | tf_op jit(solution)/shard_map/ppermute | solution.py:154
  166.4 47.6 %collective-permute-start.30 = (bf16[512,2048]{1,0:T(8,128)(2,1)}, bf16[512,2048]{1,0:T(8,128)(2,1)}, u32[]{:S(2)}, u32[]{:S(2)}) collective-permute-start(bf16[512,2048]{1,0:T(8,128)(2,1)} %pad_maximum_fusion.7), channel_id=1, source_target_pairs={{0,16},{1,17},{2,18},{3,19},{4,20},{5,21},{6,22},{7,23},{8,24},{9,... | collective-permute-start | bytes 6291464 | tf_op jit(solution)/shard_map/ppermute | solution.py:154
  166.9 47.3 %collective-permute-start.31 = (bf16[512,2048]{1,0:T(8,128)(2,1)}, bf16[512,2048]{1,0:T(8,128)(2,1)}, u32[]{:S(2)}, u32[]{:S(2)}) collective-permute-start(bf16[512,2048]{1,0:T(8,128)(2,1)} %pad_maximum_fusion.8), channel_id=1, source_target_pairs={{0,8},{1,9},{2,10},{3,11},{4,12},{5,13},{6,14},{7,15},{8,0},{9,1},... | collective-permute-start | bytes 6291464 | tf_op jit(solution)/shard_map/ppermute | solution.py:154
  244.3 48.1 %collective-permute-start.40 = (bf16[512,2048]{1,0:T(8,128)(2,1)S(1)}, bf16[512,2048]{1,0:T(8,128)(2,1)S(1)}, u32[]{:S(2)}, u32[]{:S(2)}) collective-permute-start(bf16[512,2048]{1,0:T(8,128)(2,1)S(1)} %pad_maximum_fusion.9), channel_id=1, source_target_pairs={{0,16},{1,17},{2,18},{3,19},{4,20},{5,21},{6,22},{7,23},{8,24},{9,... | collective-permute-start | bytes 6291464 | tf_op jit(solution)/shard_map/ppermute | solution.py:154
  245.9 47.7 %collective-permute-start.41 = (bf16[512,2048]{1,0:T(8,128)(2,1)S(1)}, bf16[512,2048]{1,0:T(8,128)(2,1)S(1)}, u32[]{:S(2)}, u32[]{:S(2)}) collective-permute-start(bf16[512,2048]{1,0:T(8,128)(2,1)S(1)} %pad_maximum_fusion.10), channel_id=1, source_target_pairs={{0,8},{1,9},{2,10},{3,11},{4,12},{5,13},{6,14},{7,15},{8,0},{9,1},... | collective-permute-start | bytes 6291464 | tf_op jit(solution)/shard_map/ppermute | solution.py:154
  408.4 48.9 %collective-permute-start.51 = (bf16[512,2048]{1,0:T(8,128)(2,1)}, bf16[512,2048]{1,0:T(8,128)(2,1)}, u32[]{:S(2)}, u32[]{:S(2)}) collective-permute-start(bf16[512,2048]{1,0:T(8,128)(2,1)} %convolution_convert_fusion.3), channel_id=1, source_target_pairs={{0,16},{1,17},{2,18},{3,19},{4,20},{5,21},{6,22},{7,23},{8,24},{9,... | collective-permute-start | bytes 6291464 | tf_op jit(solution)/shard_map/ppermute | solution.py:154
  409.0 48.9 %collective-permute-start.52 = (bf16[512,2048]{1,0:T(8,128)(2,1)}, bf16[512,2048]{1,0:T(8,128)(2,1)}, u32[]{:S(2)}, u32[]{:S(2)}) collective-permute-start(bf16[512,2048]{1,0:T(8,128)(2,1)} %convolution_convert_fusion.2), channel_id=1, source_target_pairs={{0,8},{1,9},{2,10},{3,11},{4,12},{5,13},{6,14},{7,15},{8,0},{9,1},... | collective-permute-start | bytes 6291464 | tf_op jit(solution)/shard_map/ppermute | solution.py:154
  416.1 55.6 %collective-permute-start.50 = (bf16[256,2048]{1,0:T(8,128)(2,1)S(1)}, bf16[256,2048]{1,0:T(8,128)(2,1)S(1)}, u32[]{:S(2)}, u32[]{:S(2)}) collective-permute-start(bf16[256,2048]{1,0:T(8,128)(2,1)S(1)} %fusion.9), channel_id=1, source_target_pairs={{0,1},{1,0},{2,3},{3,2},{4,5},{5,4},{6,7},{7,6},{8,9},{9,8},{10,11... | collective-permute-start | bytes 3145736 | tf_op jit(solution)/shard_map/ppermute | solution.py:154
  432.1 40.2 %collective-permute-start.49 = (bf16[256,2048]{1,0:T(8,128)(2,1)}, bf16[256,2048]{1,0:T(8,128)(2,1)}, u32[]{:S(2)}, u32[]{:S(2)}) collective-permute-start(bf16[256,2048]{1,0:T(8,128)(2,1)} %convolution_convert_fusion.6), channel_id=1, source_target_pairs={{0,4},{1,5},{2,6},{3,7},{4,0},{5,1},{6,2},{7,3},{8,12},{9,13},{10,... | collective-permute-start | bytes 3145736 | tf_op jit(solution)/shard_map/ppermute | solution.py:154
  432.1 70.2 %collective-permute-start.58 = (bf16[512,2048]{1,0:T(8,128)(2,1)}, bf16[512,2048]{1,0:T(8,128)(2,1)}, u32[]{:S(2)}, u32[]{:S(2)}) collective-permute-start(bf16[512,2048]{1,0:T(8,128)(2,1)} %convolution_convert_fusion.1), channel_id=1, source_target_pairs={{0,16},{1,17},{2,18},{3,19},{4,20},{5,21},{6,22},{7,23},{8,24},{9,... | collective-permute-start | bytes 6291464 | tf_op jit(solution)/shard_map/ppermute | solution.py:154
  457.3 48.8 %collective-permute-start.59 = (bf16[512,2048]{1,0:T(8,128)(2,1)}, bf16[512,2048]{1,0:T(8,128)(2,1)}, u32[]{:S(2)}, u32[]{:S(2)}) collective-permute-start(bf16[512,2048]{1,0:T(8,128)(2,1)} %convolution_convert_fusion), channel_id=1, source_target_pairs={{0,8},{1,9},{2,10},{3,11},{4,12},{5,13},{6,14},{7,15},{8,0},{9,1},... | collective-permute-start | bytes 6291464 | tf_op jit(solution)/shard_map/ppermute | solution.py:154
  470.3 56.3 %collective-permute-start.56 = (bf16[256,2048]{1,0:T(8,128)(2,1)}, bf16[256,2048]{1,0:T(8,128)(2,1)}, u32[]{:S(2)}, u32[]{:S(2)}) collective-permute-start(bf16[256,2048]{1,0:T(8,128)(2,1)} %slice.705), channel_id=1, source_target_pairs={{0,8},{1,9},{2,10},{3,11},{4,12},{5,13},{6,14},{7,15},{8,0},{9,1},... | collective-permute-start | bytes 3145736 | tf_op jit(solution)/shard_map/ppermute | solution.py:154
  471.8 54.8 %collective-permute-start.57 = (bf16[256,2048]{1,0:T(8,128)(2,1)}, bf16[256,2048]{1,0:T(8,128)(2,1)}, u32[]{:S(2)}, u32[]{:S(2)}) collective-permute-start(bf16[256,2048]{1,0:T(8,128)(2,1)} %slice.704), channel_id=1, source_target_pairs={{0,16},{1,17},{2,18},{3,19},{4,20},{5,21},{6,22},{7,23},{8,24},{9,... | collective-permute-start | bytes 3145736 | tf_op jit(solution)/shard_map/ppermute | solution.py:154
  483.0 47.8 %collective-permute-start.54 = (bf16[256,2048]{1,0:T(8,128)(2,1)S(1)}, bf16[256,2048]{1,0:T(8,128)(2,1)S(1)}, u32[]{:S(2)}, u32[]{:S(2)}) collective-permute-start(bf16[256,2048]{1,0:T(8,128)(2,1)S(1)} %convert_element_type.348), channel_id=1, source_target_pairs={{0,1},{1,0},{2,3},{3,2},{4,5},{5,4},{6,7},{7,6},{8,9},{9,8},{10,11... | collective-permute-start | bytes 3145736 | tf_op jit(solution)/shard_map/ppermute | solution.py:154
  531.1 42.7 %collective-permute-start.62 = (bf16[256,2048]{1,0:T(8,128)(2,1)}, bf16[256,2048]{1,0:T(8,128)(2,1)}, u32[]{:S(2)}, u32[]{:S(2)}) collective-permute-start(bf16[256,2048]{1,0:T(8,128)(2,1)} %slice.703), channel_id=1, source_target_pairs={{0,8},{1,9},{2,10},{3,11},{4,12},{5,13},{6,14},{7,15},{8,0},{9,1},... | collective-permute-start | bytes 3145736 | tf_op jit(solution)/shard_map/ppermute | solution.py:154
  531.7 44.2 %collective-permute-start.63 = (bf16[256,2048]{1,0:T(8,128)(2,1)}, bf16[256,2048]{1,0:T(8,128)(2,1)}, u32[]{:S(2)}, u32[]{:S(2)}) collective-permute-start(bf16[256,2048]{1,0:T(8,128)(2,1)} %slice.702), channel_id=1, source_target_pairs={{0,16},{1,17},{2,18},{3,19},{4,20},{5,21},{6,22},{7,23},{8,24},{9,... | collective-permute-start | bytes 3145736 | tf_op jit(solution)/shard_map/ppermute | solution.py:154
  540.0 54.0 %collective-permute-start.65 = (bf16[256,2048]{1,0:T(8,128)(2,1)}, bf16[256,2048]{1,0:T(8,128)(2,1)}, u32[]{:S(2)}, u32[]{:S(2)}) collective-permute-start(bf16[256,2048]{1,0:T(8,128)(2,1)} %broadcast_select_fusion.3), channel_id=1, source_target_pairs={{0,2},{1,3},{2,0},{3,1},{4,6},{5,7},{6,4},{7,5},{8,10},{9,11},{10,... | collective-permute-start | bytes 3145736 | tf_op jit(solution)/shard_map/ppermute | solution.py:154
  570.2 35.9 %collective-permute-start.81 = (bf16[512,1024]{0,1:T(8,128)(2,1)S(1)}, bf16[512,1024]{0,1:T(8,128)(2,1)S(1)}, u32[]{:S(2)}, u32[]{:S(2)}) collective-permute-start(bf16[512,1024]{0,1:T(8,128)(2,1)S(1)} %maximum_bitcast_fusion.4), channel_id=1, source_target_pairs={{0,16},{1,17},{2,18},{3,19},{4,20},{5,21},{6,22},{7,23},{8,24},{9,... | collective-permute-start | bytes 3145736 | tf_op jit(solution)/shard_map/ppermute | solution.py:154
  572.2 33.9 %collective-permute-start.82 = (bf16[512,1024]{0,1:T(8,128)(2,1)S(1)}, bf16[512,1024]{0,1:T(8,128)(2,1)S(1)}, u32[]{:S(2)}, u32[]{:S(2)}) collective-permute-start(bf16[512,1024]{0,1:T(8,128)(2,1)S(1)} %maximum_bitcast_fusion.5), channel_id=1, source_target_pairs={{0,8},{1,9},{2,10},{3,11},{4,12},{5,13},{6,14},{7,15},{8,0},{9,1},... | collective-permute-start | bytes 3145736 | tf_op jit(solution)/shard_map/ppermute | solution.py:154
  599.0 47.0 %collective-permute-start.72 = (bf16[256,2048]{1,0:T(8,128)(2,1)S(1)}, bf16[256,2048]{1,0:T(8,128)(2,1)S(1)}, u32[]{:S(2)}, u32[]{:S(2)}) collective-permute-start(bf16[256,2048]{1,0:T(8,128)(2,1)S(1)} %broadcast_select_fusion.2), channel_id=1, source_target_pairs={{0,2},{1,3},{2,0},{3,1},{4,6},{5,7},{6,4},{7,5},{8,10},{9,11},{10,... | collective-permute-start | bytes 3145736 | tf_op jit(solution)/shard_map/ppermute | solution.py:154
  613.2 47.5 %collective-permute-start.68 = (bf16[256,2048]{1,0:T(8,128)(2,1)S(1)}, bf16[256,2048]{1,0:T(8,128)(2,1)S(1)}, u32[]{:S(2)}, u32[]{:S(2)}) collective-permute-start(bf16[256,2048]{1,0:T(8,128)(2,1)S(1)} %add_convert_fusion), channel_id=1, source_target_pairs={{0,1},{1,0},{2,3},{3,2},{4,5},{5,4},{6,7},{7,6},{8,9},{9,8},{10,11... | collective-permute-start | bytes 3145736 | tf_op jit(solution)/shard_map/ppermute | solution.py:154
  623.9 41.6 %collective-permute-start.70 = (bf16[512,1024]{0,1:T(8,128)(2,1)}, bf16[512,1024]{0,1:T(8,128)(2,1)}, u32[]{:S(2)}, u32[]{:S(2)}) collective-permute-start(bf16[512,1024]{0,1:T(8,128)(2,1)} %maximum_bitcast_fusion.6), channel_id=1, source_target_pairs={{0,16},{1,17},{2,18},{3,19},{4,20},{5,21},{6,22},{7,23},{8,24},{9,... | collective-permute-start | bytes 3145736 | tf_op jit(solution)/shard_map/ppermute | solution.py:154
  626.9 38.5 %collective-permute-start.71 = (bf16[512,1024]{0,1:T(8,128)(2,1)}, bf16[512,1024]{0,1:T(8,128)(2,1)}, u32[]{:S(2)}, u32[]{:S(2)}) collective-permute-start(bf16[512,1024]{0,1:T(8,128)(2,1)} %maximum_bitcast_fusion.7), channel_id=1, source_target_pairs={{0,8},{1,9},{2,10},{3,11},{4,12},{5,13},{6,14},{7,15},{8,0},{9,1},... | collective-permute-start | bytes 3145736 | tf_op jit(solution)/shard_map/ppermute | solution.py:154
  629.5 31.2 %collective-permute-start.67 = (bf16[256,2048]{1,0:T(8,128)(2,1)S(1)}, bf16[256,2048]{1,0:T(8,128)(2,1)S(1)}, u32[]{:S(2)}, u32[]{:S(2)}) collective-permute-start(bf16[256,2048]{1,0:T(8,128)(2,1)S(1)} %fusion.12), channel_id=1, source_target_pairs={{0,4},{1,5},{2,6},{3,7},{4,0},{5,1},{6,2},{7,3},{8,12},{9,13},{10,... | collective-permute-start | bytes 3145736 | tf_op jit(solution)/shard_map/ppermute | solution.py:154
  (173 other events, 2362.0 us)
